TPU v7x, 256 devices: a whole 4x4x8 slice. The times are simulated.
256 devices in a mesh: gx: 4 (over z_hi, core), gy: 4 (over x), gz: 16 (over y, z_lo).
Axes of the slice: x: 4, y: 4, z: 8 (z_hi: 2, z_lo: 4; z = z_hi * 4 + z_lo), core: 2. Of those that a mesh axis runs over, the one named last changes fastest.
Arguments:
- local_solution: float32 [3, 68, 180, 2048], P(None, 'gx', 'gy', 'gz'), may hold values from -6 to 6
- top_nodes: float32 [3, 68, 180, 16], P(None, 'gx', 'gy', 'gz'), may hold values from -6 to 6
- coarse_solution: float32 [3, 8192], P(None, 'gz'), may hold values from -6 to 6
- corner_dofs: int32 [4, 4, 16, 8], P('gx', 'gy', 'gz'), may hold values from 0 to 8191
- density: float32 [64, 176, 2048], P('gx', 'gy', 'gz'), may hold values from 0.1 to 1
- element_stiffness: float32 [24, 24], replicated, may hold values from -0.15 to 4.5, as said below
Outputs:
- filtered_sens: float32 [64, 176, 2048], P('gx', 'gy', 'gz')
- filtered_density: float32 [64, 176, 2048], P('gx', 'gy', 'gz')
Inputs may be any that keep to these rules, and one draw needn't show every extreme that they name: element_stiffness is symmetric.
All inputs are finite; a program needn't handle non-finite values.
Results may differ from a plain program's by a relative error of at most 0.00005.
Values sent between devices are 32-bit elements; how exact they have to be, the bound alone decides.
A program may use at most 64 MiB of HBM per device.

v0:
```python
import jax
import jax.numpy as jnp
from jax import lax
from jax.sharding import PartitionSpec as P

RADIUS = 3


penal_scale = -3.0 / 96.0


def with_halo(shard, sides, width):
    for axis, dim in sides:
        count, length = (lax.axis_size(axis), shard.shape[dim])
        up = [(i, (i + 1) % count) for i in range(count - 1)]
        down = [(j, i) for i, j in up]
        last = lax.slice_in_dim(shard, length - width, length, axis=dim)
        initial = lax.slice_in_dim(shard, 0, width, axis=dim)
        before = lax.ppermute(last, axis, up)
        after = lax.ppermute(initial, axis, down)
        shard = jnp.concatenate([before, shard, after], axis=dim)
    return shard


def recover(local_nodes, corner_vals, ratio_z):
    ex = local_nodes.shape[1] - 1
    ey = local_nodes.shape[2] - 1
    ratio_x = jnp.arange(ex + 1, dtype=jnp.float32) / ex
    ratio_y = jnp.arange(ey + 1, dtype=jnp.float32) / ey
    summed = local_nodes
    for corner in range(8):
        along_x = ratio_x if corner // 4 == 1 else 1.0 - ratio_x
        along_y = ratio_y if corner // 2 % 2 == 1 else 1.0 - ratio_y
        along_z = ratio_z if corner % 2 == 1 else 1.0 - ratio_z
        basis = along_x[:, None, None] * along_y[None, :, None] * along_z[None, None, :]
        summed = summed + basis[None] * corner_vals[:, corner][:, None, None, None]
    return summed


def average_rows(extended, dim, has_lower, has_upper):
    inner = extended.shape[dim] - 2
    own_rows = lax.slice_in_dim(extended, 1, inner + 1, axis=dim)
    rim_low = lax.slice_in_dim(extended, 0, 1, axis=dim)
    rim_high = lax.slice_in_dim(extended, inner + 1, inner + 2, axis=dim)
    shape_row = [1] * extended.ndim
    shape_row[dim] = inner
    rows = jnp.arange(inner, dtype=jnp.int32).reshape(shape_row)
    is_low = rows == 0
    is_high = rows == inner - 1
    factor = jnp.where(is_low & has_lower, 0.5, jnp.where(is_high & has_upper, 0.5, 1.0))
    rim_part = jnp.where(is_low, rim_low, 0.0) + jnp.where(is_high, rim_high, 0.0)
    return own_rows * factor + rim_part * 0.5


def element_energy(lower_nodes, upper_nodes, stiffness):
    ex = lower_nodes.shape[1] - 1
    ey = lower_nodes.shape[2] - 1

    def rows_energy(first_row):
        slab_low = lax.dynamic_slice_in_dim(lower_nodes, first_row, 5, axis=1)
        slab_up = lax.dynamic_slice_in_dim(upper_nodes, first_row, 5, axis=1)
        columns = []
        for corner in range(8):
            shift_x = corner // 4
            shift_y = corner // 2 % 2
            source = slab_up if corner % 2 == 1 else slab_low
            columns.append(source[:, shift_x : shift_x + 4, shift_y : shift_y + ey, :])
        vectors = jnp.stack(columns, axis=1)
        vectors = vectors.reshape((24,) + vectors.shape[2:])
        product = jnp.einsum(
            "ij,jabc->iabc",
            stiffness,
            vectors,
            precision=lax.Precision.HIGHEST,
            preferred_element_type=jnp.float32,
        )
        return jnp.sum(vectors * product, axis=0)

    starts = jnp.arange(ex // 4, dtype=jnp.int32) * 4
    energies = lax.map(rows_energy, starts)
    return energies.reshape((ex,) + energies.shape[2:])


def smooth(field, axis, count):
    summed = None
    for offset in range(-RADIUS, RADIUS + 1):
        term_piece = lax.slice_in_dim(field, RADIUS + offset, RADIUS + offset + count, axis=axis)
        term_value = float(RADIUS + 1 - abs(offset)) * term_piece
        summed = term_value if summed is None else summed + term_value
    return summed


def edge_counts(count, position, parts):
    places = position * count + jnp.arange(count, dtype=jnp.int32)
    summed = None
    for offset in range(-RADIUS, RADIUS + 1):
        inside = ((places + offset >= 0) & (places + offset < count * parts)).astype(jnp.float32)
        term_value = float(RADIUS + 1 - abs(offset)) * inside
        summed = term_value if summed is None else summed + term_value
    return summed


def local(local_solution, top_nodes, coarse_solution, corner_dofs, density, element_stiffness):
    wanted = corner_dofs.reshape(8)
    columns = lax.all_gather(coarse_solution, "gz", axis=1, tiled=True)
    matches = wanted[:, None] == jnp.arange(columns.shape[1], dtype=jnp.int32)[None, :]
    corner_vals = jnp.sum(jnp.where(matches[None], columns[:, None, :], 0.0), axis=2)
    depth = local_solution.shape[3]
    main_nodes = recover(local_solution, corner_vals, jnp.arange(depth, dtype=jnp.float32) / depth)
    top_plane = recover(top_nodes, corner_vals, jnp.ones((1,), jnp.float32))
    index_x = lax.axis_index("gx")
    index_y = lax.axis_index("gy")
    index_z = lax.axis_index("gz")
    lower_x = index_x > 0
    upper_x = index_x < lax.axis_size("gx") - 1
    lower_y = index_y > 0
    upper_y = index_y < lax.axis_size("gy") - 1
    extended = with_halo(main_nodes, (("gx", 1), ("gy", 2)), 1)
    extended = average_rows(extended, 1, lower_x, upper_x)
    main_avg = average_rows(extended, 2, lower_y, upper_y)
    planes = jnp.concatenate([main_nodes[:, :, :, 0:1], top_plane], axis=3)
    faces = with_halo(planes, (("gx", 1), ("gy", 2), ("gz", 3)), 1)
    faces = average_rows(faces, 1, lower_x, upper_x)
    faces = average_rows(faces, 2, lower_y, upper_y)
    low_factor = jnp.where(index_z > 0, 0.5, 1.0)
    high_factor = jnp.where(index_z < lax.axis_size("gz") - 1, 0.5, 1.0)
    first_plane = faces[:, :, :, 1:2] * low_factor + faces[:, :, :, 0:1] * 0.5
    last_plane = faces[:, :, :, 2:3] * high_factor + faces[:, :, :, 3:4] * 0.5
    plane_rows = jnp.arange(depth, dtype=jnp.int32)[None, None, None, :]
    lower_nodes = jnp.where(plane_rows == 0, first_plane, main_avg)
    upper_nodes = jnp.concatenate([lower_nodes[:, :, :, 1:], last_plane], axis=3)
    energy = element_energy(lower_nodes, upper_nodes, element_stiffness)
    sens = penal_scale * density * density * energy
    count_x, count_y, count_z = density.shape
    normalizer = (
        edge_counts(count_x, index_x, lax.axis_size("gx"))[:, None, None]
        * edge_counts(count_y, index_y, lax.axis_size("gy"))[None, :, None]
        * edge_counts(count_z, index_z, lax.axis_size("gz"))[None, None, :]
    )
    stacked = jnp.stack([density * sens, density])
    padded = with_halo(stacked, (("gx", 1), ("gy", 2), ("gz", 3)), RADIUS)
    smoothed = smooth(padded, 1, count_x)
    smoothed = smooth(smoothed, 2, count_y)
    smoothed = smooth(smoothed, 3, count_z)
    numerator = smoothed[0]
    smooth_density = smoothed[1]
    return (numerator / (density * normalizer), smooth_density / normalizer)


def solution(mesh):
    in_specs = (
        P(None, "gx", "gy", "gz"),
        P(None, "gx", "gy", "gz"),
        P(None, "gz"),
        P("gx", "gy", "gz", None),
        P("gx", "gy", "gz"),
        P(),
    )
    out_specs = (P("gx", "gy", "gz"), P("gx", "gy", "gz"))
    return jax.shard_map(local, mesh=mesh, in_specs=in_specs, out_specs=out_specs, check_vma=False)
```

profile of v0, /device:TPU:1, one launch (start us, length us, event | category | flops | bytes accessed | tf_op | source)
XLA Modules:
  0.0 186.2 jit_solution(12606002679593429779)
XLA Ops:
  0.7 38.6 %all_gather.3 = f32[3,8192]{1,0:T(4,128)S(1)} all-gather(f32[3,512]{1,0:T(4,128)} %param.10), channel_id=1, replica_groups=mesh['gx'=4,'gy'=4,'gz'=16] {'gz'}, dimensions={1}, use_global_device_ids=true | all-gather | bytes 104448 | tf_op jit(solution)/shard_map/all_gather | solution.py:105
  43.4 14.0 %collective-permute-start = (f32[3,1,45,2]{2,3,1,0:T(2,128)S(1)}, f32[3,1,45,2]{2,3,1,0:T(2,128)S(1)}, u32[]{:S(2)}, u32[]{:S(2)}) collective-permute-start(f32[3,1,45,2]{2,3,1,0:T(2,128)S(1)} %get-tuple-element.143), channel_id=1, source_target_pairs={{0,64},{64,128},{128,192},{1,65},{65,129},{129,193},{2,66},{66,130... | collective-permute-start | bytes 3248 | tf_op jit(solution)/shard_map/ppermute | solution.py:19
  57.4 1.9 %collective-permute-start.1 = (f32[3,1,45,2]{2,3,1,0:T(2,128)S(1)}, f32[3,1,45,2]{2,3,1,0:T(2,128)S(1)}, u32[]{:S(2)}, u32[]{:S(2)}) collective-permute-start(f32[3,1,45,2]{2,3,1,0:T(2,128)S(1)} %get-tuple-element.144), channel_id=1, source_target_pairs={{64,0},{128,64},{192,128},{65,1},{129,65},{193,129},{66,2},{130,66... | collective-permute-start | bytes 3248 | tf_op jit(solution)/shard_map/ppermute | solution.py:20
  59.3 7.5 %collective-permute-start.6 = (f32[3,1,45,128]{3,2,1,0:T(8,128)S(1)}, f32[3,1,45,128]{3,2,1,0:T(8,128)S(1)}, u32[]{:S(2)}, u32[]{:S(2)}) collective-permute-start(f32[3,1,45,128]{3,2,1,0:T(8,128)S(1)} %get-tuple-element.123), channel_id=1, source_target_pairs={{0,64},{64,128},{128,192},{1,65},{65,129},{129,193},{2,66},{66,130... | collective-permute-start | bytes 207368 | tf_op jit(solution)/shard_map/ppermute | solution.py:19
  66.9 1.9 %collective-permute-start.7 = (f32[3,1,45,128]{3,2,1,0:T(8,128)S(1)}, f32[3,1,45,128]{3,2,1,0:T(8,128)S(1)}, u32[]{:S(2)}, u32[]{:S(2)}) collective-permute-start(f32[3,1,45,128]{3,2,1,0:T(8,128)S(1)} %get-tuple-element.124), channel_id=1, source_target_pairs={{64,0},{128,64},{192,128},{65,1},{129,65},{193,129},{66,2},{130,66... | collective-permute-start | bytes 207368 | tf_op jit(solution)/shard_map/ppermute | solution.py:20
  70.1 3.1 %collective-permute-start.2 = (f32[3,19,1,2]{2,3,1,0:T(2,128)S(1)}, f32[3,19,1,2]{2,3,1,0:T(2,128)S(1)}, u32[]{:S(2)}, u32[]{:S(2)}) collective-permute-start(f32[3,19,1,2]{2,3,1,0:T(2,128)S(1)} %get-tuple-element.141), channel_id=1, source_target_pairs={{0,16},{16,32},{32,48},{1,17},{17,33},{33,49},{2,18},{18,34},{34,5... | collective-permute-start | bytes 1376 | tf_op jit(solution)/shard_map/ppermute | solution.py:19
  73.2 1.3 collective-permute-start.3
  74.6 3.6 %collective-permute-done.3 = f32[3,19,1,2]{2,3,1,0:T(2,128)S(1)} collective-permute-done((f32[3,19,1,2]{2,3,1,0:T(2,128)S(1)}, f32[3,19,1,2]{2,3,1,0:T(2,128)S(1)}, u32[]{:S(2)}, u32[]{:S(2)}) %collective-permute-start.3) | collective-permute-done | bytes 488 | tf_op jit(solution)/shard_map/ppermute | solution.py:20
  81.1 3.3 %collective-permute-done.5 = f32[3,19,47,1]{2,3,1,0:T(1,128)S(1)} collective-permute-done((f32[3,19,47,1]{2,3,1,0:T(1,128)S(1)}, f32[3,19,47,1]{2,3,1,0:T(1,128)S(1)}, u32[]{:S(2)}, u32[]{:S(2)}) %collective-permute-start.5) | collective-permute-done | bytes 10748 | tf_op jit(solution)/shard_map/ppermute | solution.py:20
  85.5 3.1 %collective-permute-start.8 = (f32[3,19,1,128]{3,2,1,0:T(1,128)S(1)}, f32[3,19,1,128]{3,2,1,0:T(1,128)S(1)}, u32[]{:S(2)}, u32[]{:S(2)}) collective-permute-start(f32[3,19,1,128]{3,2,1,0:T(1,128)S(1)} %get-tuple-element.121), channel_id=1, source_target_pairs={{0,16},{16,32},{32,48},{1,17},{17,33},{33,49},{2,18},{18,34},{34,5... | collective-permute-start | bytes 87560 | tf_op jit(solution)/shard_map/ppermute | solution.py:19
  88.7 1.5 collective-permute-start.9
  90.3 1.6 copy.284
  91.9 1.4 collective-permute-done.9
  98.1 36.0 %while.10 = (s32[]{:T(128)}, f32[4,4,44,128]{3,1,0,2:T(4,128)S(1)}, s32[4]{0:T(128)}, f32[3,17,45,128]{3,0,2,1:T(4,128)S(1)}, f32[3,17,45,128]{3,2,1,0:T(8,128)S...) while((s32[]{:T(128)}, f32[4,4,44,128]{3,1,0,2:T(4,128)S(1)}, s32[4]{0:T(128)}, ...), condition=%wide.region_3.4_spmd, body=%wide.region_1.3_spmd.sunk | while | flops 156772352 | bytes 10021331 | solution.py:80
  98.1 1.3 dynamic_slice.11
  102.7 4.4 %fusion.89 = f32[4,44,128]{2,1,0:T(8,128)S(1)} fusion(f32[3,8,4,44,128]{4,0,3,2,1:T(4,128)S(1)} %fusion.88, f32[24,24]{1,0:T(8,128)S(1)} %get-tuple-element.253), kind=kOutput, calls=%fused_computation.1.clone.1 | convolution fusion | flops 156772352 | bytes 2255104 | tf_op jit(solution)/shard_map/while/body/eval_jaxpr/ij,jabc->iabc/dot_general | solution.py:70
  111.7 4.4 %fusion.89 = f32[4,44,128]{2,1,0:T(8,128)S(1)} fusion(f32[3,8,4,44,128]{4,0,3,2,1:T(4,128)S(1)} %fusion.88, f32[24,24]{1,0:T(8,128)S(1)} %get-tuple-element.253), kind=kOutput, calls=%fused_computation.1.clone.1 | convolution fusion | flops 156772352 | bytes 2255104 | tf_op jit(solution)/shard_map/while/body/eval_jaxpr/ij,jabc->iabc/dot_general | solution.py:70
  120.7 4.4 %fusion.89 = f32[4,44,128]{2,1,0:T(8,128)S(1)} fusion(f32[3,8,4,44,128]{4,0,3,2,1:T(4,128)S(1)} %fusion.88, f32[24,24]{1,0:T(8,128)S(1)} %get-tuple-element.253), kind=kOutput, calls=%fused_computation.1.clone.1 | convolution fusion | flops 156772352 | bytes 2255104 | tf_op jit(solution)/shard_map/while/body/eval_jaxpr/ij,jabc->iabc/dot_general | solution.py:70
  129.7 4.4 %fusion.89 = f32[4,44,128]{2,1,0:T(8,128)S(1)} fusion(f32[3,8,4,44,128]{4,0,3,2,1:T(4,128)S(1)} %fusion.88, f32[24,24]{1,0:T(8,128)S(1)} %get-tuple-element.253), kind=kOutput, calls=%fused_computation.1.clone.1 | convolution fusion | flops 156772352 | bytes 2255104 | tf_op jit(solution)/shard_map/while/body/eval_jaxpr/ij,jabc->iabc/dot_general | solution.py:70
  134.3 11.6 %collective-permute-start.10 = (f32[2,3,44,128]{3,1,2,0:T(4,128)S(1)}, f32[2,3,44,128]{3,1,2,0:T(4,128)S(1)}, u32[]{:S(2)}, u32[]{:S(2)}) collective-permute-start(f32[2,3,44,128]{3,1,2,0:T(4,128)S(1)} %get-tuple-element.132), channel_id=1, source_target_pairs={{0,64},{64,128},{128,192},{1,65},{65,129},{129,193},{2,66},{66,130... | collective-permute-start | bytes 405512 | tf_op jit(solution)/shard_map/ppermute | solution.py:19
  145.9 1.9 %collective-permute-start.11 = (f32[2,3,44,128]{3,1,2,0:T(4,128)S(1)}, f32[2,3,44,128]{3,1,2,0:T(4,128)S(1)}, u32[]{:S(2)}, u32[]{:S(2)}) collective-permute-start(f32[2,3,44,128]{3,1,2,0:T(4,128)S(1)} %get-tuple-element.131), channel_id=1, source_target_pairs={{64,0},{128,64},{192,128},{65,1},{129,65},{193,129},{66,2},{130,66... | collective-permute-start | bytes 405512 | tf_op jit(solution)/shard_map/ppermute | solution.py:20
  148.9 7.6 %collective-permute-done.11 = f32[2,3,44,128]{3,1,2,0:T(4,128)S(1)} collective-permute-done((f32[2,3,44,128]{3,1,2,0:T(4,128)S(1)}, f32[2,3,44,128]{3,1,2,0:T(4,128)S(1)}, u32[]{:S(2)}, u32[]{:S(2)}) %collective-permute-start.11) | collective-permute-done | bytes 135200 | tf_op jit(solution)/shard_map/ppermute | solution.py:20
  156.7 2.8 %collective-permute-start.12 = (f32[2,22,3,128]{3,0,2,1:T(2,128)S(1)}, f32[2,22,3,128]{3,0,2,1:T(2,128)S(1)}, u32[]{:S(2)}, u32[]{:S(2)}) collective-permute-start(f32[2,22,3,128]{3,0,2,1:T(2,128)S(1)} %get-tuple-element.127), channel_id=1, source_target_pairs={{0,16},{16,32},{32,48},{1,17},{17,33},{33,49},{2,18},{18,34},{34,5... | collective-permute-start | bytes 202760 | tf_op jit(solution)/shard_map/ppermute | solution.py:19
  159.6 1.5 collective-permute-start.13
  161.2 3.4 %collective-permute-done.13 = f32[2,22,3,128]{3,0,2,1:T(2,128)S(1)} collective-permute-done((f32[2,22,3,128]{3,0,2,1:T(2,128)S(1)}, f32[2,22,3,128]{3,0,2,1:T(2,128)S(1)}, u32[]{:S(2)}, u32[]{:S(2)}) %collective-permute-start.13) | collective-permute-done | bytes 67616 | tf_op jit(solution)/shard_map/ppermute | solution.py:20
  165.1 2.2 %fusion.63 = (f32[2,22,50,3]{3,0,2,1:T(2,128)}, f32[2,22,50,3]{3,0,2,1:T(2,128)S(1)}) fusion(f32[2,22,50,128]{3,0,2,1:T(2,128)S(1)} %pad_maximum_fusion.3), kind=kLoop, calls=%fused_computation.198 | loop fusion | bytes 105600 | tf_op jit(solution)/shard_map/slice | solution.py:17
  167.3 1.7 copy.306
  169.0 3.3 %collective-permute-start.14 = (f32[2,22,50,3]{2,0,3,1:T(2,128)S(1)}, f32[2,22,50,3]{2,0,3,1:T(2,128)S(1)}, u32[]{:S(2)}, u32[]{:S(2)}) collective-permute-start(f32[2,22,50,3]{2,0,3,1:T(2,128)S(1)} %copy.306), channel_id=1, source_target_pairs={{0,1},{1,2},{2,3},{3,4},{4,5},{5,6},{6,7},{7,8},{8,9},{9,10},{10,1... | collective-permute-start | bytes 79208 | tf_op jit(solution)/shard_map/ppermute | solution.py:19
  174.4 1.6 copy.293
  176.0 2.0 %collective-permute-done.15 = f32[2,22,50,3]{2,0,3,1:T(2,128)S(1)} collective-permute-done((f32[2,22,50,3]{2,0,3,1:T(2,128)S(1)}, f32[2,22,50,3]{2,0,3,1:T(2,128)S(1)}, u32[]{:S(2)}, u32[]{:S(2)}) %collective-permute-start.15) | collective-permute-done | bytes 26432 | tf_op jit(solution)/shard_map/ppermute | solution.py:20
  178.0 1.6 copy.295
  179.6 2.7 %pad_maximum_fusion = f32[2,22,50,134]{3,1,2,0:T(8,128)S(1)} fusion(f32[2,22,50,3]{3,1,2,0:T(8,128)} %copy.295, f32[2,22,50,128]{3,1,2,0:T(8,128)S(1)} %copy.294, f32[2,22,50,3]{3,1,2,0:T(8,128)} %copy.293), kind=kLoop, calls=%fused_computation.27 | loop fusion | flops 589600 | bytes 2358400 | tf_op jit(solution)/shard_map/concatenate | solution.py:21
  (135 shorter events, 31.4 us)
Async XLA Ops:
  40.6 1.3 copy-start.2
  41.9 1.2 copy-start.4
  43.4 26.5 %collective-permute-start = (f32[3,1,45,2]{2,3,1,0:T(2,128)S(1)}, f32[3,1,45,2]{2,3,1,0:T(2,128)S(1)}, u32[]{:S(2)}, u32[]{:S(2)}) collective-permute-start(f32[3,1,45,2]{2,3,1,0:T(2,128)S(1)} %get-tuple-element.143), channel_id=1, source_target_pairs={{0,64},{64,128},{128,192},{1,65},{65,129},{129,193},{2,66},{66,130... | collective-permute-start | bytes 3248 | tf_op jit(solution)/shard_map/ppermute | solution.py:19
  57.4 12.5 %collective-permute-start.1 = (f32[3,1,45,2]{2,3,1,0:T(2,128)S(1)}, f32[3,1,45,2]{2,3,1,0:T(2,128)S(1)}, u32[]{:S(2)}, u32[]{:S(2)}) collective-permute-start(f32[3,1,45,2]{2,3,1,0:T(2,128)S(1)} %get-tuple-element.144), channel_id=1, source_target_pairs={{64,0},{128,64},{192,128},{65,1},{129,65},{193,129},{66,2},{130,66... | collective-permute-start | bytes 3248 | tf_op jit(solution)/shard_map/ppermute | solution.py:20
  59.3 26.1 %collective-permute-start.6 = (f32[3,1,45,128]{3,2,1,0:T(8,128)S(1)}, f32[3,1,45,128]{3,2,1,0:T(8,128)S(1)}, u32[]{:S(2)}, u32[]{:S(2)}) collective-permute-start(f32[3,1,45,128]{3,2,1,0:T(8,128)S(1)} %get-tuple-element.123), channel_id=1, source_target_pairs={{0,64},{64,128},{128,192},{1,65},{65,129},{129,193},{2,66},{66,130... | collective-permute-start | bytes 207368 | tf_op jit(solution)/shard_map/ppermute | solution.py:19
  66.9 18.6 %collective-permute-start.7 = (f32[3,1,45,128]{3,2,1,0:T(8,128)S(1)}, f32[3,1,45,128]{3,2,1,0:T(8,128)S(1)}, u32[]{:S(2)}, u32[]{:S(2)}) collective-permute-start(f32[3,1,45,128]{3,2,1,0:T(8,128)S(1)} %get-tuple-element.124), channel_id=1, source_target_pairs={{64,0},{128,64},{192,128},{65,1},{129,65},{193,129},{66,2},{130,66... | collective-permute-start | bytes 207368 | tf_op jit(solution)/shard_map/ppermute | solution.py:20
  70.1 4.5 %collective-permute-start.2 = (f32[3,19,1,2]{2,3,1,0:T(2,128)S(1)}, f32[3,19,1,2]{2,3,1,0:T(2,128)S(1)}, u32[]{:S(2)}, u32[]{:S(2)}) collective-permute-start(f32[3,19,1,2]{2,3,1,0:T(2,128)S(1)} %get-tuple-element.141), channel_id=1, source_target_pairs={{0,16},{16,32},{32,48},{1,17},{17,33},{33,49},{2,18},{18,34},{34,5... | collective-permute-start | bytes 1376 | tf_op jit(solution)/shard_map/ppermute | solution.py:19
  73.2 4.9 %collective-permute-start.3 = (f32[3,19,1,2]{2,3,1,0:T(2,128)S(1)}, f32[3,19,1,2]{2,3,1,0:T(2,128)S(1)}, u32[]{:S(2)}, u32[]{:S(2)}) collective-permute-start(f32[3,19,1,2]{2,3,1,0:T(2,128)S(1)} %get-tuple-element.142), channel_id=1, source_target_pairs={{16,0},{32,16},{48,32},{17,1},{33,17},{49,33},{18,2},{34,18},{50,3... | collective-permute-start | bytes 1376 | tf_op jit(solution)/shard_map/ppermute | solution.py:20
  78.5 2.6 %collective-permute-start.4 = (f32[3,19,47,1]{2,3,1,0:T(1,128)S(1)}, f32[3,19,47,1]{2,3,1,0:T(1,128)S(1)}, u32[]{:S(2)}, u32[]{:S(2)}) collective-permute-start(f32[3,19,47,1]{2,3,1,0:T(1,128)S(1)} %get-tuple-element.139), channel_id=1, source_target_pairs={{0,1},{1,2},{2,3},{3,4},{4,5},{5,6},{6,7},{7,8},{8,9},{9,10},{10,1... | collective-permute-start | bytes 32156 | tf_op jit(solution)/shard_map/ppermute | solution.py:19
  79.8 4.6 %collective-permute-start.5 = (f32[3,19,47,1]{2,3,1,0:T(1,128)S(1)}, f32[3,19,47,1]{2,3,1,0:T(1,128)S(1)}, u32[]{:S(2)}, u32[]{:S(2)}) collective-permute-start(f32[3,19,47,1]{2,3,1,0:T(1,128)S(1)} %get-tuple-element.140), channel_id=1, source_target_pairs={{1,0},{2,1},{3,2},{4,3},{5,4},{6,5},{7,6},{8,7},{9,8},{10,9},{11,1... | collective-permute-start | bytes 32156 | tf_op jit(solution)/shard_map/ppermute | solution.py:20
  85.5 6.4 %collective-permute-start.8 = (f32[3,19,1,128]{3,2,1,0:T(1,128)S(1)}, f32[3,19,1,128]{3,2,1,0:T(1,128)S(1)}, u32[]{:S(2)}, u32[]{:S(2)}) collective-permute-start(f32[3,19,1,128]{3,2,1,0:T(1,128)S(1)} %get-tuple-element.121), channel_id=1, source_target_pairs={{0,16},{16,32},{32,48},{1,17},{17,33},{33,49},{2,18},{18,34},{34,5... | collective-permute-start | bytes 87560 | tf_op jit(solution)/shard_map/ppermute | solution.py:19
  88.7 4.6 %collective-permute-start.9 = (f32[3,19,1,128]{3,2,1,0:T(1,128)S(1)}, f32[3,19,1,128]{3,2,1,0:T(1,128)S(1)}, u32[]{:S(2)}, u32[]{:S(2)}) collective-permute-start(f32[3,19,1,128]{3,2,1,0:T(1,128)S(1)} %get-tuple-element.122), channel_id=1, source_target_pairs={{16,0},{32,16},{48,32},{17,1},{33,17},{49,33},{18,2},{34,18},{50,3... | collective-permute-start | bytes 87560 | tf_op jit(solution)/shard_map/ppermute | solution.py:20
  96.1 1.3 copy-start.1
  97.4 0.7 copy-start.3
  98.1 36.0 %copy-start = (f32[16,44,128]{2,0,1:T(8,128)S(1)}, f32[16,44,128]{2,0,1:T(8,128)}, u32[]{:S(2)}) copy-start(f32[16,44,128]{2,0,1:T(8,128)} %param.12) | copy-start | bytes 1081348
  134.3 14.0 %collective-permute-start.10 = (f32[2,3,44,128]{3,1,2,0:T(4,128)S(1)}, f32[2,3,44,128]{3,1,2,0:T(4,128)S(1)}, u32[]{:S(2)}, u32[]{:S(2)}) collective-permute-start(f32[2,3,44,128]{3,1,2,0:T(4,128)S(1)} %get-tuple-element.132), channel_id=1, source_target_pairs={{0,64},{64,128},{128,192},{1,65},{65,129},{129,193},{2,66},{66,130... | collective-permute-start | bytes 405512 | tf_op jit(solution)/shard_map/ppermute | solution.py:19
  145.9 10.7 %collective-permute-start.11 = (f32[2,3,44,128]{3,1,2,0:T(4,128)S(1)}, f32[2,3,44,128]{3,1,2,0:T(4,128)S(1)}, u32[]{:S(2)}, u32[]{:S(2)}) collective-permute-start(f32[2,3,44,128]{3,1,2,0:T(4,128)S(1)} %get-tuple-element.131), channel_id=1, source_target_pairs={{64,0},{128,64},{192,128},{65,1},{129,65},{193,129},{66,2},{130,66... | collective-permute-start | bytes 405512 | tf_op jit(solution)/shard_map/ppermute | solution.py:20
  147.9 13.2 %copy-start.5 = (f32[16]{0:T(128)S(1)}, f32[16]{0:T(128)}, u32[]{:S(2)}) copy-start(f32[16]{0:T(128)} %fusion.49) | copy-start | bytes 196
  156.7 4.4 %collective-permute-start.12 = (f32[2,22,3,128]{3,0,2,1:T(2,128)S(1)}, f32[2,22,3,128]{3,0,2,1:T(2,128)S(1)}, u32[]{:S(2)}, u32[]{:S(2)}) collective-permute-start(f32[2,22,3,128]{3,0,2,1:T(2,128)S(1)} %get-tuple-element.127), channel_id=1, source_target_pairs={{0,16},{16,32},{32,48},{1,17},{17,33},{33,49},{2,18},{18,34},{34,5... | collective-permute-start | bytes 202760 | tf_op jit(solution)/shard_map/ppermute | solution.py:19
  159.6 5.0 %collective-permute-start.13 = (f32[2,22,3,128]{3,0,2,1:T(2,128)S(1)}, f32[2,22,3,128]{3,0,2,1:T(2,128)S(1)}, u32[]{:S(2)}, u32[]{:S(2)}) collective-permute-start(f32[2,22,3,128]{3,0,2,1:T(2,128)S(1)} %get-tuple-element.128), channel_id=1, source_target_pairs={{16,0},{32,16},{48,32},{17,1},{33,17},{49,33},{18,2},{34,18},{50,3... | collective-permute-start | bytes 202760 | tf_op jit(solution)/shard_map/ppermute | solution.py:20
  169.0 5.4 %collective-permute-start.14 = (f32[2,22,50,3]{2,0,3,1:T(2,128)S(1)}, f32[2,22,50,3]{2,0,3,1:T(2,128)S(1)}, u32[]{:S(2)}, u32[]{:S(2)}) collective-permute-start(f32[2,22,50,3]{2,0,3,1:T(2,128)S(1)} %copy.306), channel_id=1, source_target_pairs={{0,1},{1,2},{2,3},{3,4},{4,5},{5,6},{6,7},{7,8},{8,9},{9,10},{10,1... | collective-permute-start | bytes 79208 | tf_op jit(solution)/shard_map/ppermute | solution.py:19
  173.0 5.0 %collective-permute-start.15 = (f32[2,22,50,3]{2,0,3,1:T(2,128)S(1)}, f32[2,22,50,3]{2,0,3,1:T(2,128)S(1)}, u32[]{:S(2)}, u32[]{:S(2)}) collective-permute-start(f32[2,22,50,3]{2,0,3,1:T(2,128)S(1)} %copy.307), channel_id=1, source_target_pairs={{1,0},{2,1},{3,2},{4,3},{5,4},{6,5},{7,6},{8,7},{9,8},{10,9},{11,1... | collective-permute-start | bytes 79208 | tf_op jit(solution)/shard_map/ppermute | solution.py:20
where the time goes:
time: 187 us; the launch traced here: 186 us
  starting transfers between devices  59.3 us (32%)
  blocking collectives  38.6 us (21%)
  local copies, waits for them, and re-layouts  25.9 us (14%)
  waiting for transfers between devices  21.7 us (12%)
  matrix products  17.4 us (9%)
  other arithmetic  13.9 us (7%)
  loops' own time  8.02 us (4%)
    ppermute x8, starting transfers between devices, with_halo(): before = lax.ppermute(last, axis, up)  46.7 us
    all_gather x1, blocking collectives, local(): columns = lax.all_gather(coarse_solution, 'gz', axis=1, tiled=True)  38.6 us
    ppermute x8, waiting for transfers between devices, with_halo(): after = lax.ppermute(initial, axis, down)  21.3 us
    dot_general x4, matrix products, rows_energy(): jnp.einsum('ij,jabc->iabc', stiffness, vectors, precision=lax.Precision.H...  17.4 us
    ppermute x8, starting transfers between devices, with_halo(): after = lax.ppermute(initial, axis, down)  12.6 us
    another operation x1, loops' own time, element_energy(): energies = lax.map(rows_energy, starts)  8.02 us
    unnamed x16, local copies, waits for them, and re-layouts  5.19 us
    dynamic_slice x4, local copies, waits for them, and re-layouts, element_energy(): energies = lax.map(rows_energy, starts)  5.1 us
  transfers between devices with their start and end apart: 16, of which 7 were waited for; matrix products, arithmetic and copies ran while one was open for 4% of the time, Pallas kernels for 0%

commit v1 on v0

--- a/solution.py
+++ b/solution.py
@@ -100,50 +100,46 @@
     return summed
 
 
+def filter_field(field, sides):
+    for axis, dim in sides:
+        padded = with_halo(field, ((axis, dim),), RADIUS)
+        field = smooth(padded, dim, field.shape[dim])
+    return field
+
+
 def local(local_solution, top_nodes, coarse_solution, corner_dofs, density, element_stiffness):
+    count_x, count_y, count_z = density.shape
+    index_x = lax.axis_index("gx")
+    index_y = lax.axis_index("gy")
+    index_z = lax.axis_index("gz")
+    normalizer = (
+        edge_counts(count_x, index_x, lax.axis_size("gx"))[:, None, None]
+        * edge_counts(count_y, index_y, lax.axis_size("gy"))[None, :, None]
+        * edge_counts(count_z, index_z, lax.axis_size("gz"))[None, None, :]
+    )
+    sides = (("gx", 0), ("gy", 1), ("gz", 2))
+    smooth_density = filter_field(density, sides)
     wanted = corner_dofs.reshape(8)
     columns = lax.all_gather(coarse_solution, "gz", axis=1, tiled=True)
     matches = wanted[:, None] == jnp.arange(columns.shape[1], dtype=jnp.int32)[None, :]
     corner_vals = jnp.sum(jnp.where(matches[None], columns[:, None, :], 0.0), axis=2)
     depth = local_solution.shape[3]
-    main_nodes = recover(local_solution, corner_vals, jnp.arange(depth, dtype=jnp.float32) / depth)
-    top_plane = recover(top_nodes, corner_vals, jnp.ones((1,), jnp.float32))
-    index_x = lax.axis_index("gx")
-    index_y = lax.axis_index("gy")
-    index_z = lax.axis_index("gz")
+    full = jnp.concatenate([local_solution, top_nodes], axis=3)
+    nodes = recover(full, corner_vals, jnp.arange(depth + 1, dtype=jnp.float32) / depth)
     lower_x = index_x > 0
     upper_x = index_x < lax.axis_size("gx") - 1
     lower_y = index_y > 0
     upper_y = index_y < lax.axis_size("gy") - 1
-    extended = with_halo(main_nodes, (("gx", 1), ("gy", 2)), 1)
+    lower_z = index_z > 0
+    upper_z = index_z < lax.axis_size("gz") - 1
+    extended = with_halo(nodes, (("gx", 1), ("gy", 2)), 1)
     extended = average_rows(extended, 1, lower_x, upper_x)
-    main_avg = average_rows(extended, 2, lower_y, upper_y)
-    planes = jnp.concatenate([main_nodes[:, :, :, 0:1], top_plane], axis=3)
-    faces = with_halo(planes, (("gx", 1), ("gy", 2), ("gz", 3)), 1)
-    faces = average_rows(faces, 1, lower_x, upper_x)
-    faces = average_rows(faces, 2, lower_y, upper_y)
-    low_factor = jnp.where(index_z > 0, 0.5, 1.0)
-    high_factor = jnp.where(index_z < lax.axis_size("gz") - 1, 0.5, 1.0)
-    first_plane = faces[:, :, :, 1:2] * low_factor + faces[:, :, :, 0:1] * 0.5
-    last_plane = faces[:, :, :, 2:3] * high_factor + faces[:, :, :, 3:4] * 0.5
-    plane_rows = jnp.arange(depth, dtype=jnp.int32)[None, None, None, :]
-    lower_nodes = jnp.where(plane_rows == 0, first_plane, main_avg)
-    upper_nodes = jnp.concatenate([lower_nodes[:, :, :, 1:], last_plane], axis=3)
-    energy = element_energy(lower_nodes, upper_nodes, element_stiffness)
+    averaged = average_rows(extended, 2, lower_y, upper_y)
+    extended = with_halo(averaged, (("gz", 3),), 1)
+    averaged = average_rows(extended, 3, lower_z, upper_z)
+    energy = element_energy(averaged[:, :, :, :depth], averaged[:, :, :, 1:], element_stiffness)
     sens = penal_scale * density * density * energy
-    count_x, count_y, count_z = density.shape
-    normalizer = (
-        edge_counts(count_x, index_x, lax.axis_size("gx"))[:, None, None]
-        * edge_counts(count_y, index_y, lax.axis_size("gy"))[None, :, None]
-        * edge_counts(count_z, index_z, lax.axis_size("gz"))[None, None, :]
-    )
-    stacked = jnp.stack([density * sens, density])
-    padded = with_halo(stacked, (("gx", 1), ("gy", 2), ("gz", 3)), RADIUS)
-    smoothed = smooth(padded, 1, count_x)
-    smoothed = smooth(smoothed, 2, count_y)
-    smoothed = smooth(smoothed, 3, count_z)
-    numerator = smoothed[0]
-    smooth_density = smoothed[1]
+    numerator = filter_field(density * sens, sides)
     return (numerator / (density * normalizer), smooth_density / normalizer)
 
 

time: 187 us -> 208 us (1.11)
  waiting for transfers between devices: 21.7 us -> 45.1 us
  local copies, waits for them, and re-layouts: 25.9 us -> 21.2 us
  other arithmetic: 13.9 us -> 16.6 us
    ppermute x8 -> x9, waiting for transfers between devices: 21.3 us -> 36.4 us  [with_halo(): after = lax.ppermute(initial, axis, down)]
    ppermute x8 -> x9, waiting for transfers between devices: 0.42 us -> 8.71 us  [with_halo(): before = lax.ppermute(last, axis, up)]
    concatenate x6 -> x1, other arithmetic: 3.9 us -> 0.46 us  [with_halo(): shard = jnp.concatenate([before, shard, after], axis=dim)]
    ppermute x2 -> x0, local copies, waits for them, and re-layouts: 3.23 us -> none  [the longest x1 1.63 us: with_halo(): after = lax.ppermute(initial, axis, down)]
    dynamic_slice x4, local copies, waits for them, and re-layouts: 5.1 us -> 2.23 us  [element_energy(): energies = lax.map(rows_energy, starts)]
    add x3, other arithmetic: 0.99 us -> 3.45 us  [average_rows(): return own_rows * factor + rim_part * 0.5]
    slice x5 -> x8, local copies, waits for them, and re-layouts: 2.45 us -> 4.47 us  [with_halo(): last = lax.slice_in_dim(shard, length - width, length, axis=dim)]
    unnamed x16 -> x25, local copies, waits for them, and re-layouts: 5.19 us -> 4.03 us
  transfers between devices with their start and end apart: 16 -> 18, of which waited for: 7 -> 9; matrix products, arithmetic and copies ran while one was open for 4% -> 21% of each run, Pallas kernels for 0% -> 0%
where the time goes in v1:
time: 208 us; the launch traced here: 207 us
  starting transfers between devices  59.9 us (29%)
  waiting for transfers between devices  45.1 us (22%)
  blocking collectives  38.6 us (19%)
  local copies, waits for them, and re-layouts  21.2 us (10%)
  matrix products  17.4 us (8%)
  other arithmetic  16.6 us (8%)
  loops' own time  6.89 us (3%)
    ppermute x9, starting transfers between devices, with_halo(): before = lax.ppermute(last, axis, up)  46.4 us
    all_gather x1, blocking collectives, local(): columns = lax.all_gather(coarse_solution, 'gz', axis=1, tiled=True)  38.6 us
    ppermute x9, waiting for transfers between devices, with_halo(): after = lax.ppermute(initial, axis, down)  36.4 us
    dot_general x4, matrix products, rows_energy(): jnp.einsum('ij,jabc->iabc', stiffness, vectors, precision=lax.Precision.H...  17.4 us
    ppermute x9, starting transfers between devices, with_halo(): after = lax.ppermute(initial, axis, down)  13.5 us
    ppermute x9, waiting for transfers between devices, with_halo(): before = lax.ppermute(last, axis, up)  8.71 us
    another operation x1, loops' own time, element_energy(): energies = lax.map(rows_energy, starts)  6.89 us
    while x28, local copies, waits for them, and re-layouts  4.56 us
  transfers between devices with their start and end apart: 18, of which 9 were waited for; matrix products, arithmetic and copies ran while one was open for 21% of the time, Pallas kernels for 0%

profile of v1, /device:TPU:1, one launch (start us, length us, event | category | flops | bytes accessed | tf_op | source)
XLA Modules:
  0.0 206.8 jit_solution(7607796451159554580)
XLA Ops:
  0.7 38.6 %all_gather.3 = f32[3,8192]{1,0:T(4,128)S(1)} all-gather(f32[3,512]{1,0:T(4,128)} %param.10), channel_id=1, replica_groups=mesh['gx'=4,'gy'=4,'gz'=16] {'gz'}, dimensions={1}, use_global_device_ids=true | all-gather | bytes 104448 | tf_op jit(solution)/shard_map/all_gather | solution.py:123
  40.6 2.3 %copy.62 = f32[3,17,45,1]{3,2,0,1:T(8,128)} copy(f32[3,17,45,1]{2,3,1,0:T(1,128)} %param.9) | data formatting | bytes 18360 | tf_op args[1]
  44.6 2.3 %fusion.23 = f32[3,17,45,129]{3,2,0,1:T(8,128)S(1)} fusion(f32[3,17,45,1]{3,2,0,1:T(8,128)S(1)} %copy-done, f32[3]{0:T(128)S(1)} %get-tuple-element.66, f32[17,45,129]{2,1,0:T(8,128)S(1)} %get-tuple-element.132, f32[3]{0:T(128)S(1)} %get-tuple-element.67, f32[17,45,129]{2,1,0:T(8,128)S(1)} %get-tuple-element.131, f32[3]{0:T(128)S(1)} %get-tuple-element.68, ...), kind=kLoop, calls=%fused_computation.43 | loop fusion | flops 5032935 | bytes 5526456 | tf_op jit(solution)/shard_map/add | solution.py:36
  47.0 14.0 %collective-permute-start = (f32[3,1,45,129]{3,2,0,1:T(8,128)S(1)}, f32[3,1,45,129]{3,2,0,1:T(8,128)S(1)}, u32[]{:S(2)}, u32[]{:S(2)}) collective-permute-start(f32[3,1,45,129]{3,2,0,1:T(8,128)S(1)} %get-tuple-element.107), channel_id=1, source_target_pairs={{0,64},{64,128},{128,192},{1,65},{65,129},{129,193},{2,66},{66,130... | collective-permute-start | bytes 208988 | tf_op jit(solution)/shard_map/ppermute | solution.py:19
  60.9 1.9 collective-permute-start.1
  63.6 1.9 collective-permute-start.13
  65.5 7.5 %collective-permute-start.12 = (f32[3,44,128]{2,0,1:T(4,128)}, f32[3,44,128]{2,0,1:T(4,128)S(1)}, u32[]{:S(2)}, u32[]{:S(2)}) collective-permute-start(f32[3,44,128]{2,0,1:T(4,128)} %get-tuple-element.116), channel_id=1, source_target_pairs={{0,64},{64,128},{128,192},{1,65},{65,129},{129,193},{2,66},{66,130... | collective-permute-start | bytes 202760 | tf_op jit(solution)/shard_map/ppermute | solution.py:19
  76.7 3.1 %collective-permute-start.2 = (f32[3,19,1,129]{3,2,0,1:T(1,128)S(1)}, f32[3,19,1,129]{3,2,0,1:T(1,128)S(1)}, u32[]{:S(2)}, u32[]{:S(2)}) collective-permute-start(f32[3,19,1,129]{3,2,0,1:T(1,128)S(1)} %get-tuple-element.99), channel_id=1, source_target_pairs={{0,16},{16,32},{32,48},{1,17},{17,33},{33,49},{2,18},{18,34},{34,5... | collective-permute-start | bytes 88244 | tf_op jit(solution)/shard_map/ppermute | solution.py:19
  81.1 3.6 %collective-permute-done.3 = f32[3,19,1,129]{3,2,0,1:T(1,128)S(1)} collective-permute-done((f32[3,19,1,129]{3,2,0,1:T(1,128)S(1)}, f32[3,19,1,129]{3,2,0,1:T(1,128)S(1)}, u32[]{:S(2)}, u32[]{:S(2)}) %collective-permute-start.3) | collective-permute-done | bytes 29444 | tf_op jit(solution)/shard_map/ppermute | solution.py:20
  91.9 2.4 %copy.67 = f32[3,17,45,1]{2,3,1,0:T(1,128)} copy(f32[3,17,45,1]{3,2,0,1:T(8,128)} %get-tuple-element.103) | data formatting | bytes 18360 | tf_op jit(solution)/shard_map/slice | solution.py:17
  94.3 4.2 %collective-permute-start.4 = (f32[3,17,45,1]{2,3,1,0:T(1,128)}, f32[3,17,45,1]{2,3,1,0:T(1,128)S(1)}, u32[]{:S(2)}, u32[]{:S(2)}) collective-permute-start(f32[3,17,45,1]{2,3,1,0:T(1,128)} %copy.67), channel_id=1, source_target_pairs={{0,1},{1,2},{2,3},{3,4},{4,5},{5,6},{6,7},{7,8},{8,9},{9,10},{10,1... | collective-permute-start | bytes 27548 | tf_op jit(solution)/shard_map/ppermute | solution.py:19
  99.5 2.0 multiply_add_fusion
  102.2 32.7 %while.10 = (s32[]{:T(128)}, f32[4,4,44,128]{3,1,0,2:T(4,128)S(1)}, s32[4]{0:T(128)S(1)}, f32[3,17,45,128]{3,2,0,1:T(8,128)S(1)}, f32[3,17,45,128]{3,2,0,1:T(8,1...) while((s32[]{:T(128)}, f32[4,4,44,128]{3,1,0,2:T(4,128)S(1)}, ...), condition=%wide.region_3.4_spmd, body=%wide.region_1.3_spmd.sunk | while | flops 156772352 | bytes 11987387 | solution.py:80
  105.9 4.4 %fusion.157 = f32[4,44,128]{2,1,0:T(8,128)S(1)} fusion(f32[3,8,4,44,128]{4,0,3,2,1:T(4,128)S(1)} %fusion.156, f32[24,24]{1,0:T(8,128)S(1)} %get-tuple-element.233), kind=kOutput, calls=%fused_computation.1.clone.1 | convolution fusion | flops 156772352 | bytes 2255104 | tf_op jit(solution)/shard_map/while/body/eval_jaxpr/ij,jabc->iabc/dot_general | solution.py:70
  114.1 4.4 %fusion.157 = f32[4,44,128]{2,1,0:T(8,128)S(1)} fusion(f32[3,8,4,44,128]{4,0,3,2,1:T(4,128)S(1)} %fusion.156, f32[24,24]{1,0:T(8,128)S(1)} %get-tuple-element.233), kind=kOutput, calls=%fused_computation.1.clone.1 | convolution fusion | flops 156772352 | bytes 2255104 | tf_op jit(solution)/shard_map/while/body/eval_jaxpr/ij,jabc->iabc/dot_general | solution.py:70
  122.3 4.4 %fusion.157 = f32[4,44,128]{2,1,0:T(8,128)S(1)} fusion(f32[3,8,4,44,128]{4,0,3,2,1:T(4,128)S(1)} %fusion.156, f32[24,24]{1,0:T(8,128)S(1)} %get-tuple-element.233), kind=kOutput, calls=%fused_computation.1.clone.1 | convolution fusion | flops 156772352 | bytes 2255104 | tf_op jit(solution)/shard_map/while/body/eval_jaxpr/ij,jabc->iabc/dot_general | solution.py:70
  130.5 4.4 %fusion.157 = f32[4,44,128]{2,1,0:T(8,128)S(1)} fusion(f32[3,8,4,44,128]{4,0,3,2,1:T(4,128)S(1)} %fusion.156, f32[24,24]{1,0:T(8,128)S(1)} %get-tuple-element.233), kind=kOutput, calls=%fused_computation.1.clone.1 | convolution fusion | flops 156772352 | bytes 2255104 | tf_op jit(solution)/shard_map/while/body/eval_jaxpr/ij,jabc->iabc/dot_general | solution.py:70
  135.0 5.6 %collective-permute-start.6 = (f32[3,44,128]{2,0,1:T(4,128)S(1)}, f32[3,44,128]{2,0,1:T(4,128)S(1)}, u32[]{:S(2)}, u32[]{:S(2)}) collective-permute-start(f32[3,44,128]{2,0,1:T(4,128)S(1)} %get-tuple-element.123), channel_id=1, source_target_pairs={{0,64},{64,128},{128,192},{1,65},{65,129},{129,193},{2,66},{66,130... | collective-permute-start | bytes 202760 | tf_op jit(solution)/shard_map/ppermute | solution.py:19
  140.6 1.9 collective-permute-start.7
  142.6 7.8 %collective-permute-done.7 = f32[3,44,128]{2,0,1:T(4,128)S(1)} collective-permute-done((f32[3,44,128]{2,0,1:T(4,128)S(1)}, f32[3,44,128]{2,0,1:T(4,128)S(1)}, u32[]{:S(2)}, u32[]{:S(2)}) %collective-permute-start.7) | collective-permute-done | bytes 67616 | tf_op jit(solution)/shard_map/ppermute | solution.py:20
  150.9 3.1 %collective-permute-start.8 = (f32[16,3,128]{2,0,1:T(8,128)S(1)}, f32[16,3,128]{2,0,1:T(8,128)S(1)}, u32[]{:S(2)}, u32[]{:S(2)}) collective-permute-start(f32[16,3,128]{2,0,1:T(8,128)S(1)} %get-tuple-element.121), channel_id=1, source_target_pairs={{0,16},{16,32},{32,48},{1,17},{17,33},{33,49},{2,18},{18,34},{34,5... | collective-permute-start | bytes 73736 | tf_op jit(solution)/shard_map/ppermute | solution.py:19
  155.3 3.2 %collective-permute-done.9 = f32[16,3,128]{2,0,1:T(8,128)S(1)} collective-permute-done((f32[16,3,128]{2,0,1:T(8,128)S(1)}, f32[16,3,128]{2,0,1:T(8,128)S(1)}, u32[]{:S(2)}, u32[]{:S(2)}) %collective-permute-start.9) | collective-permute-done | bytes 24608 | tf_op jit(solution)/shard_map/ppermute | solution.py:20
  158.9 4.1 %collective-permute-start.10 = (f32[16,44,3]{2,0,1:T(8,128)S(1)}, f32[16,44,3]{2,0,1:T(8,128)S(1)}, u32[]{:S(2)}, u32[]{:S(2)}) collective-permute-start(f32[16,44,3]{2,0,1:T(8,128)S(1)} %get-tuple-element.119), channel_id=1, source_target_pairs={{0,1},{1,2},{2,3},{3,4},{4,5},{5,6},{6,7},{7,8},{8,9},{9,10},{10,1... | collective-permute-start | bytes 25352 | tf_op jit(solution)/shard_map/ppermute | solution.py:19
  165.3 2.1 %collective-permute-done.10 = f32[16,44,3]{2,0,1:T(8,128)S(1)} collective-permute-done((f32[16,44,3]{2,0,1:T(8,128)S(1)}, f32[16,44,3]{2,0,1:T(8,128)S(1)}, u32[]{:S(2)}, u32[]{:S(2)}) %collective-permute-start.10) | collective-permute-done | bytes 8480 | tf_op jit(solution)/shard_map/ppermute | solution.py:19
  167.3 6.9 %collective-permute-done.11 = f32[16,44,3]{2,0,1:T(8,128)S(1)} collective-permute-done((f32[16,44,3]{2,0,1:T(8,128)S(1)}, f32[16,44,3]{2,0,1:T(8,128)S(1)}, u32[]{:S(2)}, u32[]{:S(2)}) %collective-permute-start.11) | collective-permute-done | bytes 8480 | tf_op jit(solution)/shard_map/ppermute | solution.py:20
  174.2 1.9 fusion.60
  176.1 2.8 %collective-permute-start.14 = (f32[16,3,128]{2,0,1:T(8,128)S(1)}, f32[16,3,128]{2,0,1:T(8,128)S(1)}, u32[]{:S(2)}, u32[]{:S(2)}) collective-permute-start(f32[16,3,128]{2,0,1:T(8,128)S(1)} %get-tuple-element.111), channel_id=1, source_target_pairs={{0,16},{16,32},{32,48},{1,17},{17,33},{33,49},{2,18},{18,34},{34,5... | collective-permute-start | bytes 73736 | tf_op jit(solution)/shard_map/ppermute | solution.py:19
  180.3 3.3 %collective-permute-done.15 = f32[16,3,128]{2,0,1:T(8,128)S(1)} collective-permute-done((f32[16,3,128]{2,0,1:T(8,128)S(1)}, f32[16,3,128]{2,0,1:T(8,128)S(1)}, u32[]{:S(2)}, u32[]{:S(2)}) %collective-permute-start.15) | collective-permute-done | bytes 24608 | tf_op jit(solution)/shard_map/ppermute | solution.py:20
  183.8 1.9 collective-permute-start.16
  187.0 6.2 %collective-permute-done.16 = f32[16,44,3]{2,0,1:T(8,128)S(1)} collective-permute-done((f32[16,44,3]{2,0,1:T(8,128)S(1)}, f32[16,44,3]{2,0,1:T(8,128)S(1)}, u32[]{:S(2)}, u32[]{:S(2)}) %collective-permute-start.16) | collective-permute-done | bytes 8480 | tf_op jit(solution)/shard_map/ppermute | solution.py:19
  193.3 11.6 %collective-permute-done.17 = f32[16,44,3]{2,0,1:T(8,128)S(1)} collective-permute-done((f32[16,44,3]{2,0,1:T(8,128)S(1)}, f32[16,44,3]{2,0,1:T(8,128)S(1)}, u32[]{:S(2)}, u32[]{:S(2)}) %collective-permute-start.17) | collective-permute-done | bytes 8480 | tf_op jit(solution)/shard_map/ppermute | solution.py:20
  204.9 1.9 multiply_divide_fusion
  (131 shorter events, 33.1 us)
Async XLA Ops:
  43.0 1.3 copy-start
  43.0 1.7 copy-start.2
  44.6 18.2 %copy-start.1 = (f32[16,44,128]{2,0,1:T(8,128)S(1)}, f32[16,44,128]{2,0,1:T(8,128)}, u32[]{:S(2)}) copy-start(f32[16,44,128]{2,0,1:T(8,128)} %param.12) | copy-start | bytes 1081348
  47.0 29.6 %collective-permute-start = (f32[3,1,45,129]{3,2,0,1:T(8,128)S(1)}, f32[3,1,45,129]{3,2,0,1:T(8,128)S(1)}, u32[]{:S(2)}, u32[]{:S(2)}) collective-permute-start(f32[3,1,45,129]{3,2,0,1:T(8,128)S(1)} %get-tuple-element.107), channel_id=1, source_target_pairs={{0,64},{64,128},{128,192},{1,65},{65,129},{129,193},{2,66},{66,130... | collective-permute-start | bytes 208988 | tf_op jit(solution)/shard_map/ppermute | solution.py:19
  60.9 15.6 %collective-permute-start.1 = (f32[3,1,45,129]{3,2,0,1:T(8,128)S(1)}, f32[3,1,45,129]{3,2,0,1:T(8,128)S(1)}, u32[]{:S(2)}, u32[]{:S(2)}) collective-permute-start(f32[3,1,45,129]{3,2,0,1:T(8,128)S(1)} %get-tuple-element.108), channel_id=1, source_target_pairs={{64,0},{128,64},{192,128},{65,1},{129,65},{193,129},{66,2},{130,66... | collective-permute-start | bytes 208988 | tf_op jit(solution)/shard_map/ppermute | solution.py:20
  63.6 100.7 %collective-permute-start.13 = (f32[3,44,128]{2,0,1:T(4,128)}, f32[3,44,128]{2,0,1:T(4,128)}, u32[]{:S(2)}, u32[]{:S(2)}) collective-permute-start(f32[3,44,128]{2,0,1:T(4,128)} %get-tuple-element.115), channel_id=1, source_target_pairs={{64,0},{128,64},{192,128},{65,1},{129,65},{193,129},{66,2},{130,66... | collective-permute-start | bytes 202760 | tf_op jit(solution)/shard_map/ppermute | solution.py:20
  65.5 99.7 %collective-permute-start.12 = (f32[3,44,128]{2,0,1:T(4,128)}, f32[3,44,128]{2,0,1:T(4,128)S(1)}, u32[]{:S(2)}, u32[]{:S(2)}) collective-permute-start(f32[3,44,128]{2,0,1:T(4,128)} %get-tuple-element.116), channel_id=1, source_target_pairs={{0,64},{64,128},{128,192},{1,65},{65,129},{129,193},{2,66},{66,130... | collective-permute-start | bytes 202760 | tf_op jit(solution)/shard_map/ppermute | solution.py:19
  76.7 4.5 %collective-permute-start.2 = (f32[3,19,1,129]{3,2,0,1:T(1,128)S(1)}, f32[3,19,1,129]{3,2,0,1:T(1,128)S(1)}, u32[]{:S(2)}, u32[]{:S(2)}) collective-permute-start(f32[3,19,1,129]{3,2,0,1:T(1,128)S(1)} %get-tuple-element.99), channel_id=1, source_target_pairs={{0,16},{16,32},{32,48},{1,17},{17,33},{33,49},{2,18},{18,34},{34,5... | collective-permute-start | bytes 88244 | tf_op jit(solution)/shard_map/ppermute | solution.py:19
  79.8 4.9 %collective-permute-start.3 = (f32[3,19,1,129]{3,2,0,1:T(1,128)S(1)}, f32[3,19,1,129]{3,2,0,1:T(1,128)S(1)}, u32[]{:S(2)}, u32[]{:S(2)}) collective-permute-start(f32[3,19,1,129]{3,2,0,1:T(1,128)S(1)} %get-tuple-element.100), channel_id=1, source_target_pairs={{16,0},{32,16},{48,32},{17,1},{33,17},{49,33},{18,2},{34,18},{50,3... | collective-permute-start | bytes 88244 | tf_op jit(solution)/shard_map/ppermute | solution.py:20
  81.1 6.1 %copy-start.5 = (f32[45]{0:T(128)}, f32[45]{0:T(128)S(1)}, u32[]{:S(2)}) copy-start(f32[45]{0:T(128)S(1)} %and_select_fusion.18) | copy-start | bytes 544
  84.8 0.6 copy-start.6
  84.8 0.7 copy-start.7
  84.8 0.7 copy-start.8
  85.5 0.9 copy-start.4
  90.6 8.5 %collective-permute-start.5 = (f32[3,17,45,1]{2,3,1,0:T(1,128)S(1)}, f32[3,17,45,1]{2,3,1,0:T(1,128)S(1)}, u32[]{:S(2)}, u32[]{:S(2)}) collective-permute-start(f32[3,17,45,1]{2,3,1,0:T(1,128)S(1)} %copy.69), channel_id=1, source_target_pairs={{1,0},{2,1},{3,2},{4,3},{5,4},{6,5},{7,6},{8,7},{9,8},{10,9},{11,1... | collective-permute-start | bytes 27548 | tf_op jit(solution)/shard_map/ppermute | solution.py:20
  94.3 5.1 %collective-permute-start.4 = (f32[3,17,45,1]{2,3,1,0:T(1,128)}, f32[3,17,45,1]{2,3,1,0:T(1,128)S(1)}, u32[]{:S(2)}, u32[]{:S(2)}) collective-permute-start(f32[3,17,45,1]{2,3,1,0:T(1,128)} %copy.67), channel_id=1, source_target_pairs={{0,1},{1,2},{2,3},{3,4},{4,5},{5,6},{6,7},{7,8},{8,9},{9,10},{10,1... | collective-permute-start | bytes 27548 | tf_op jit(solution)/shard_map/ppermute | solution.py:19
  101.4 0.7 copy-start.3
  101.5 0.7 copy-start.11
  102.2 40.4 %copy-start.9 = (f32[16]{0:T(128)S(1)}, f32[16]{0:T(128)}, u32[]{:S(2)}) copy-start(f32[16]{0:T(128)} %fusion.112) | copy-start | bytes 196
  102.2 40.4 %copy-start.10 = (f32[44]{0:T(128)S(1)}, f32[44]{0:T(128)}, u32[]{:S(2)}) copy-start(f32[44]{0:T(128)} %fusion.118) | copy-start | bytes 532
  135.0 7.6 %collective-permute-start.6 = (f32[3,44,128]{2,0,1:T(4,128)S(1)}, f32[3,44,128]{2,0,1:T(4,128)S(1)}, u32[]{:S(2)}, u32[]{:S(2)}) collective-permute-start(f32[3,44,128]{2,0,1:T(4,128)S(1)} %get-tuple-element.123), channel_id=1, source_target_pairs={{0,64},{64,128},{128,192},{1,65},{65,129},{129,193},{2,66},{66,130... | collective-permute-start | bytes 202760 | tf_op jit(solution)/shard_map/ppermute | solution.py:19
  140.6 9.9 %collective-permute-start.7 = (f32[3,44,128]{2,0,1:T(4,128)S(1)}, f32[3,44,128]{2,0,1:T(4,128)S(1)}, u32[]{:S(2)}, u32[]{:S(2)}) collective-permute-start(f32[3,44,128]{2,0,1:T(4,128)S(1)} %get-tuple-element.124), channel_id=1, source_target_pairs={{64,0},{128,64},{192,128},{65,1},{129,65},{193,129},{66,2},{130,66... | collective-permute-start | bytes 202760 | tf_op jit(solution)/shard_map/ppermute | solution.py:20
  150.9 4.5 %collective-permute-start.8 = (f32[16,3,128]{2,0,1:T(8,128)S(1)}, f32[16,3,128]{2,0,1:T(8,128)S(1)}, u32[]{:S(2)}, u32[]{:S(2)}) collective-permute-start(f32[16,3,128]{2,0,1:T(8,128)S(1)} %get-tuple-element.121), channel_id=1, source_target_pairs={{0,16},{16,32},{32,48},{1,17},{17,33},{33,49},{2,18},{18,34},{34,5... | collective-permute-start | bytes 73736 | tf_op jit(solution)/shard_map/ppermute | solution.py:19
  154.0 4.6 %collective-permute-start.9 = (f32[16,3,128]{2,0,1:T(8,128)S(1)}, f32[16,3,128]{2,0,1:T(8,128)S(1)}, u32[]{:S(2)}, u32[]{:S(2)}) collective-permute-start(f32[16,3,128]{2,0,1:T(8,128)S(1)} %get-tuple-element.122), channel_id=1, source_target_pairs={{16,0},{32,16},{48,32},{17,1},{33,17},{49,33},{18,2},{34,18},{50,3... | collective-permute-start | bytes 73736 | tf_op jit(solution)/shard_map/ppermute | solution.py:20
  158.9 8.5 %collective-permute-start.10 = (f32[16,44,3]{2,0,1:T(8,128)S(1)}, f32[16,44,3]{2,0,1:T(8,128)S(1)}, u32[]{:S(2)}, u32[]{:S(2)}) collective-permute-start(f32[16,44,3]{2,0,1:T(8,128)S(1)} %get-tuple-element.119), channel_id=1, source_target_pairs={{0,1},{1,2},{2,3},{3,4},{4,5},{5,6},{6,7},{7,8},{8,9},{9,10},{10,1... | collective-permute-start | bytes 25352 | tf_op jit(solution)/shard_map/ppermute | solution.py:19
  163.0 11.2 %collective-permute-start.11 = (f32[16,44,3]{2,0,1:T(8,128)S(1)}, f32[16,44,3]{2,0,1:T(8,128)S(1)}, u32[]{:S(2)}, u32[]{:S(2)}) collective-permute-start(f32[16,44,3]{2,0,1:T(8,128)S(1)} %get-tuple-element.120), channel_id=1, source_target_pairs={{1,0},{2,1},{3,2},{4,3},{5,4},{6,5},{7,6},{8,7},{9,8},{10,9},{11,1... | collective-permute-start | bytes 25352 | tf_op jit(solution)/shard_map/ppermute | solution.py:20
  176.1 4.1 %collective-permute-start.14 = (f32[16,3,128]{2,0,1:T(8,128)S(1)}, f32[16,3,128]{2,0,1:T(8,128)S(1)}, u32[]{:S(2)}, u32[]{:S(2)}) collective-permute-start(f32[16,3,128]{2,0,1:T(8,128)S(1)} %get-tuple-element.111), channel_id=1, source_target_pairs={{0,16},{16,32},{32,48},{1,17},{17,33},{33,49},{2,18},{18,34},{34,5... | collective-permute-start | bytes 73736 | tf_op jit(solution)/shard_map/ppermute | solution.py:19
  179.0 4.6 %collective-permute-start.15 = (f32[16,3,128]{2,0,1:T(8,128)S(1)}, f32[16,3,128]{2,0,1:T(8,128)S(1)}, u32[]{:S(2)}, u32[]{:S(2)}) collective-permute-start(f32[16,3,128]{2,0,1:T(8,128)S(1)} %get-tuple-element.112), channel_id=1, source_target_pairs={{16,0},{32,16},{48,32},{17,1},{33,17},{49,33},{18,2},{34,18},{50,3... | collective-permute-start | bytes 73736 | tf_op jit(solution)/shard_map/ppermute | solution.py:20
  183.8 9.5 %collective-permute-start.16 = (f32[16,44,3]{2,0,1:T(8,128)S(1)}, f32[16,44,3]{2,0,1:T(8,128)S(1)}, u32[]{:S(2)}, u32[]{:S(2)}) collective-permute-start(f32[16,44,3]{2,0,1:T(8,128)S(1)} %get-tuple-element.109), channel_id=1, source_target_pairs={{0,1},{1,2},{2,3},{3,4},{4,5},{5,6},{6,7},{7,8},{8,9},{9,10},{10,1... | collective-permute-start | bytes 25352 | tf_op jit(solution)/shard_map/ppermute | solution.py:19
  185.7 19.2 %collective-permute-start.17 = (f32[16,44,3]{2,0,1:T(8,128)S(1)}, f32[16,44,3]{2,0,1:T(8,128)S(1)}, u32[]{:S(2)}, u32[]{:S(2)}) collective-permute-start(f32[16,44,3]{2,0,1:T(8,128)S(1)} %get-tuple-element.110), channel_id=1, source_target_pairs={{1,0},{2,1},{3,2},{4,3},{5,4},{6,5},{7,6},{8,7},{9,8},{10,9},{11,1... | collective-permute-start | bytes 25352 | tf_op jit(solution)/shard_map/ppermute | solution.py:20

commit v2 on v1

--- a/solution.py
+++ b/solution.py
@@ -117,10 +117,12 @@
         * edge_counts(count_y, index_y, lax.axis_size("gy"))[None, :, None]
         * edge_counts(count_z, index_z, lax.axis_size("gz"))[None, None, :]
     )
-    sides = (("gx", 0), ("gy", 1), ("gz", 2))
-    smooth_density = filter_field(density, sides)
+    sides = (("gx", 1), ("gy", 2), ("gz", 3))
     wanted = corner_dofs.reshape(8)
-    columns = lax.all_gather(coarse_solution, "gz", axis=1, tiled=True)
+    parts = lax.axis_size("gz")
+    spread = jnp.broadcast_to(coarse_solution[None], (parts,) + coarse_solution.shape)
+    gathered = lax.all_to_all(spread, "gz", 0, 0, tiled=True)
+    columns = gathered.transpose(1, 0, 2).reshape(coarse_solution.shape[0], -1)
     matches = wanted[:, None] == jnp.arange(columns.shape[1], dtype=jnp.int32)[None, :]
     corner_vals = jnp.sum(jnp.where(matches[None], columns[:, None, :], 0.0), axis=2)
     depth = local_solution.shape[3]
@@ -139,7 +141,9 @@
     averaged = average_rows(extended, 3, lower_z, upper_z)
     energy = element_energy(averaged[:, :, :, :depth], averaged[:, :, :, 1:], element_stiffness)
     sens = penal_scale * density * density * energy
-    numerator = filter_field(density * sens, sides)
+    smoothed = filter_field(jnp.stack([density * sens, density]), sides)
+    numerator = smoothed[0]
+    smooth_density = smoothed[1]
     return (numerator / (density * normalizer), smooth_density / normalizer)
 
 

time: 208 us -> 141 us (0.68)
  the two profiles are of different devices: /device:TPU:1 before, /device:TPU:97 now
where the time goes in v2:
time: 141 us; the launch traced here: 140 us
  starting transfers between devices  48.3 us (34%)
  waiting for transfers between devices  30.7 us (22%)
  local copies, waits for them, and re-layouts  19.6 us (14%)
  matrix products  17.4 us (12%)
  other arithmetic  15.3 us (11%)
  loops' own time  8.05 us (6%)
    ppermute x6, starting transfers between devices, with_halo(): before = lax.ppermute(last, axis, up)  30.1 us
    ppermute x6, waiting for transfers between devices, with_halo(): after = lax.ppermute(initial, axis, down)  29.4 us
    dot_general x4, matrix products, rows_energy(): jnp.einsum('ij,jabc->iabc', stiffness, vectors, precision=lax.Precision.H...  17.4 us
    ppermute x6, starting transfers between devices, with_halo(): after = lax.ppermute(initial, axis, down)  11 us
    another operation x1, loops' own time, element_energy(): energies = lax.map(rows_energy, starts)  8.05 us
    all_to_all x1, starting transfers between devices, local(): gathered = lax.all_to_all(spread, 'gz', 0, 0, tiled=True)  7.18 us
    while x28, local copies, waits for them, and re-layouts  4.56 us
    slice x6, local copies, waits for them, and re-layouts, with_halo(): last = lax.slice_in_dim(shard, length - width, length, axis=dim)  4.13 us
  transfers between devices with their start and end apart: 13, of which 8 were waited for; matrix products, arithmetic and copies ran while one was open for 6% of the time, Pallas kernels for 0%

profile of v2, /device:TPU:97, one launch (start us, length us, event | category | flops | bytes accessed | tf_op | source)
XLA Modules:
  0.0 140.4 jit_solution(6365353110366206430)
XLA Ops:
  0.6 1.4 broadcast_in_dim.201
  2.0 7.2 %all-to-all-start = ((f32[16,3,512]{2,1,0:T(4,128)}), f32[16,3,512]{2,1,0:T(4,128)S(1)}, u32[]{:S(2)}, u32[]{:S(2)}) async-start(f32[16,3,512]{2,1,0:T(4,128)} %broadcast_in_dim.201), calls=%async_computation | async-start | bytes 262144 | tf_op jit(solution)/shard_map/all_to_all | solution.py:124
  10.0 1.3 copy.101
  11.4 2.8 %broadcast_multiply_fusion.1 = (f32[17,45,129]{2,1,0:T(8,128)S(1)}, f32[17,45,129]{2,1,0:T(8,128)S(1)}, f32[17,45,129]{2,1,0:T(8,128)}, f32[17,45,129]{2,1,0:T(8...) fusion(f32[17,45]{1,0:T(8,128)S(1)} %get-tuple-element.143, ...), kind=kLoop, calls=%fused_computation.116 | loop fusion | flops 789480 | bytes 3171192 | tf_op jit(solution)/shard_map/mul | solution.py:35
  14.7 3.7 %fusion.23 = f32[3,17,45,129]{3,2,0,1:T(8,128)S(1)} fusion(f32[3,17,45,1]{3,2,0,1:T(8,128)S(1)} %copy.101, f32[3]{0:T(128)S(1)} %get-tuple-element.74, f32[17,45,129]{2,1,0:T(8,128)S(1)} %get-tuple-element.134, f32[3]{0:T(128)S(1)} %get-tuple-element.75, f32[17,45,129]{2,1,0:T(8,128)S(1)} %get-tuple-element.133, f32[3]{0:T(128)S(1)} %get-tuple-element.76, ...), kind=kLoop, calls=%fused_computation.43 | loop fusion | flops 5032935 | bytes 5526456 | tf_op jit(solution)/shard_map/add | solution.py:36
  18.5 7.7 %collective-permute-start = (f32[3,1,45,129]{3,2,0,1:T(8,128)S(1)}, f32[3,1,45,129]{3,2,0,1:T(8,128)S(1)}, u32[]{:S(2)}, u32[]{:S(2)}) collective-permute-start(f32[3,1,45,129]{3,2,0,1:T(8,128)S(1)} %get-tuple-element.115), channel_id=1, source_target_pairs={{0,64},{64,128},{128,192},{1,65},{65,129},{129,193},{2,66},{66,130... | collective-permute-start | bytes 208988 | tf_op jit(solution)/shard_map/ppermute | solution.py:19
  26.2 1.9 %collective-permute-start.1 = (f32[3,1,45,129]{3,2,0,1:T(8,128)S(1)}, f32[3,1,45,129]{3,2,0,1:T(8,128)S(1)}, u32[]{:S(2)}, u32[]{:S(2)}) collective-permute-start(f32[3,1,45,129]{3,2,0,1:T(8,128)S(1)} %get-tuple-element.116), channel_id=1, source_target_pairs={{64,0},{128,64},{192,128},{65,1},{129,65},{193,129},{66,2},{130,66... | collective-permute-start | bytes 208988 | tf_op jit(solution)/shard_map/ppermute | solution.py:20
  28.3 8.7 %collective-permute-done.1 = f32[3,1,45,129]{3,2,0,1:T(8,128)S(1)} collective-permute-done((f32[3,1,45,129]{3,2,0,1:T(8,128)S(1)}, f32[3,1,45,129]{3,2,0,1:T(8,128)S(1)}, u32[]{:S(2)}, u32[]{:S(2)}) %collective-permute-start.1) | collective-permute-done | bytes 69692 | tf_op jit(solution)/shard_map/ppermute | solution.py:20
  37.1 3.1 %collective-permute-start.2 = (f32[3,19,1,129]{3,2,0,1:T(1,128)S(1)}, f32[3,19,1,129]{3,2,0,1:T(1,128)S(1)}, u32[]{:S(2)}, u32[]{:S(2)}) collective-permute-start(f32[3,19,1,129]{3,2,0,1:T(1,128)S(1)} %get-tuple-element.107), channel_id=1, source_target_pairs={{0,16},{16,32},{32,48},{1,17},{17,33},{33,49},{2,18},{18,34},{34,5... | collective-permute-start | bytes 88244 | tf_op jit(solution)/shard_map/ppermute | solution.py:19
  40.3 1.3 collective-permute-start.3
  41.6 3.6 %collective-permute-done.3 = f32[3,19,1,129]{3,2,0,1:T(1,128)S(1)} collective-permute-done((f32[3,19,1,129]{3,2,0,1:T(1,128)S(1)}, f32[3,19,1,129]{3,2,0,1:T(1,128)S(1)}, u32[]{:S(2)}, u32[]{:S(2)}) %collective-permute-start.3) | collective-permute-done | bytes 29444 | tf_op jit(solution)/shard_map/ppermute | solution.py:20
  47.4 1.7 %fusion.84 = (f32[3,17,45,1]{3,2,0,1:T(8,128)}, f32[3,17,45,1]{3,2,0,1:T(8,128)}) fusion(f32[3,17,45,129]{3,2,0,1:T(8,128)S(1)} %fusion.15), kind=kLoop, calls=%fused_computation.213 | loop fusion | bytes 36720 | tf_op jit(solution)/shard_map/slice | solution.py:17
  49.1 1.8 %copy.108 = f32[3,17,45,1]{2,3,1,0:T(1,128)S(1)} copy(f32[3,17,45,1]{3,2,0,1:T(8,128)} %get-tuple-element.112) | data formatting | bytes 18360 | tf_op jit(solution)/shard_map/slice | solution.py:18
  50.9 2.5 %collective-permute-start.5 = (f32[3,17,45,1]{2,3,1,0:T(1,128)S(1)}, f32[3,17,45,1]{2,3,1,0:T(1,128)S(1)}, u32[]{:S(2)}, u32[]{:S(2)}) collective-permute-start(f32[3,17,45,1]{2,3,1,0:T(1,128)S(1)} %copy.108), channel_id=1, source_target_pairs={{1,0},{2,1},{3,2},{4,3},{5,4},{6,5},{7,6},{8,7},{9,8},{10,9},{11,1... | collective-permute-start | bytes 27548 | tf_op jit(solution)/shard_map/ppermute | solution.py:20
  53.3 1.8 %copy.106 = f32[3,17,45,1]{2,3,1,0:T(1,128)S(1)} copy(f32[3,17,45,1]{3,2,0,1:T(8,128)} %get-tuple-element.111) | data formatting | bytes 18360 | tf_op jit(solution)/shard_map/slice | solution.py:17
  55.1 5.7 %collective-permute-start.4 = (f32[3,17,45,1]{2,3,1,0:T(1,128)S(1)}, f32[3,17,45,1]{2,3,1,0:T(1,128)S(1)}, u32[]{:S(2)}, u32[]{:S(2)}) collective-permute-start(f32[3,17,45,1]{2,3,1,0:T(1,128)S(1)} %copy.106), channel_id=1, source_target_pairs={{0,1},{1,2},{2,3},{3,4},{4,5},{5,6},{6,7},{7,8},{8,9},{9,10},{10,1... | collective-permute-start | bytes 27548 | tf_op jit(solution)/shard_map/ppermute | solution.py:19
  61.6 1.3 multiply_add_fusion
  63.7 34.0 %while.10 = (s32[]{:T(128)}, f32[4,4,44,128]{3,1,0,2:T(4,128)S(1)}, s32[4]{0:T(128)S(1)}, f32[3,17,45,128]{3,2,0,1:T(8,128)S(1)}, f32[3,17,45,128]{3,2,0,1:T(8,1...) while((s32[]{:T(128)}, f32[4,4,44,128]{3,1,0,2:T(4,128)S(1)}, ...), condition=%wide.region_3.4_spmd, body=%wide.region_1.3_spmd.sunk | while | flops 156772352 | bytes 11987387 | solution.py:80
  67.7 4.4 %fusion.111 = f32[4,44,128]{2,1,0:T(8,128)S(1)} fusion(f32[3,8,4,44,128]{4,0,3,2,1:T(4,128)S(1)} %fusion.110, f32[24,24]{1,0:T(8,128)S(1)} %get-tuple-element.235), kind=kOutput, calls=%fused_computation.1.clone.1 | convolution fusion | flops 156772352 | bytes 2255104 | tf_op jit(solution)/shard_map/while/body/eval_jaxpr/ij,jabc->iabc/dot_general | solution.py:70
  76.2 4.4 %fusion.111 = f32[4,44,128]{2,1,0:T(8,128)S(1)} fusion(f32[3,8,4,44,128]{4,0,3,2,1:T(4,128)S(1)} %fusion.110, f32[24,24]{1,0:T(8,128)S(1)} %get-tuple-element.235), kind=kOutput, calls=%fused_computation.1.clone.1 | convolution fusion | flops 156772352 | bytes 2255104 | tf_op jit(solution)/shard_map/while/body/eval_jaxpr/ij,jabc->iabc/dot_general | solution.py:70
  84.7 4.4 %fusion.111 = f32[4,44,128]{2,1,0:T(8,128)S(1)} fusion(f32[3,8,4,44,128]{4,0,3,2,1:T(4,128)S(1)} %fusion.110, f32[24,24]{1,0:T(8,128)S(1)} %get-tuple-element.235), kind=kOutput, calls=%fused_computation.1.clone.1 | convolution fusion | flops 156772352 | bytes 2255104 | tf_op jit(solution)/shard_map/while/body/eval_jaxpr/ij,jabc->iabc/dot_general | solution.py:70
  93.2 4.4 %fusion.111 = f32[4,44,128]{2,1,0:T(8,128)S(1)} fusion(f32[3,8,4,44,128]{4,0,3,2,1:T(4,128)S(1)} %fusion.110, f32[24,24]{1,0:T(8,128)S(1)} %get-tuple-element.235), kind=kOutput, calls=%fused_computation.1.clone.1 | convolution fusion | flops 156772352 | bytes 2255104 | tf_op jit(solution)/shard_map/while/body/eval_jaxpr/ij,jabc->iabc/dot_general | solution.py:70
  97.8 4.2 %collective-permute-start.6 = (f32[2,3,44,128]{3,1,2,0:T(4,128)S(1)}, f32[2,3,44,128]{3,1,2,0:T(4,128)S(1)}, u32[]{:S(2)}, u32[]{:S(2)}) collective-permute-start(f32[2,3,44,128]{3,1,2,0:T(4,128)S(1)} %get-tuple-element.125), channel_id=1, source_target_pairs={{0,64},{64,128},{128,192},{1,65},{65,129},{129,193},{2,66},{66,130... | collective-permute-start | bytes 405512 | tf_op jit(solution)/shard_map/ppermute | solution.py:19
  102.0 1.9 %collective-permute-start.7 = (f32[2,3,44,128]{3,1,2,0:T(4,128)S(1)}, f32[2,3,44,128]{3,1,2,0:T(4,128)S(1)}, u32[]{:S(2)}, u32[]{:S(2)}) collective-permute-start(f32[2,3,44,128]{3,1,2,0:T(4,128)S(1)} %get-tuple-element.126), channel_id=1, source_target_pairs={{64,0},{128,64},{192,128},{65,1},{129,65},{193,129},{66,2},{130,66... | collective-permute-start | bytes 405512 | tf_op jit(solution)/shard_map/ppermute | solution.py:20
  104.5 8.4 %collective-permute-done.7 = f32[2,3,44,128]{3,1,2,0:T(4,128)S(1)} collective-permute-done((f32[2,3,44,128]{3,1,2,0:T(4,128)S(1)}, f32[2,3,44,128]{3,1,2,0:T(4,128)S(1)}, u32[]{:S(2)}, u32[]{:S(2)}) %collective-permute-start.7) | collective-permute-done | bytes 135200 | tf_op jit(solution)/shard_map/ppermute | solution.py:20
  113.6 3.1 %collective-permute-start.8 = (f32[2,16,3,128]{3,1,2,0:T(8,128)S(1)}, f32[2,16,3,128]{3,1,2,0:T(8,128)S(1)}, u32[]{:S(2)}, u32[]{:S(2)}) collective-permute-start(f32[2,16,3,128]{3,1,2,0:T(8,128)S(1)} %get-tuple-element.121), channel_id=1, source_target_pairs={{0,16},{16,32},{32,48},{1,17},{17,33},{33,49},{2,18},{18,34},{34,5... | collective-permute-start | bytes 147464 | tf_op jit(solution)/shard_map/ppermute | solution.py:19
  116.7 1.3 collective-permute-start.9
  118.1 3.8 %collective-permute-done.9 = f32[2,16,3,128]{3,1,2,0:T(8,128)S(1)} collective-permute-done((f32[2,16,3,128]{3,1,2,0:T(8,128)S(1)}, f32[2,16,3,128]{3,1,2,0:T(8,128)S(1)}, u32[]{:S(2)}, u32[]{:S(2)}) %collective-permute-start.9) | collective-permute-done | bytes 49184 | tf_op jit(solution)/shard_map/ppermute | solution.py:20
  122.7 6.2 %collective-permute-start.10 = (f32[2,16,44,3]{2,1,3,0:T(8,128)S(1)}, f32[2,16,44,3]{2,1,3,0:T(8,128)S(1)}, u32[]{:S(2)}, u32[]{:S(2)}) collective-permute-start(f32[2,16,44,3]{2,1,3,0:T(8,128)S(1)} %copy.113), channel_id=1, source_target_pairs={{0,1},{1,2},{2,3},{3,4},{4,5},{5,6},{6,7},{7,8},{8,9},{9,10},{10,1... | collective-permute-start | bytes 50696 | tf_op jit(solution)/shard_map/ppermute | solution.py:19
  129.3 2.1 %collective-permute-start.11 = (f32[2,16,44,3]{2,1,3,0:T(8,128)S(1)}, f32[2,16,44,3]{2,1,3,0:T(8,128)S(1)}, u32[]{:S(2)}, u32[]{:S(2)}) collective-permute-start(f32[2,16,44,3]{2,1,3,0:T(8,128)S(1)} %copy.115), channel_id=1, source_target_pairs={{1,0},{2,1},{3,2},{4,3},{5,4},{6,5},{7,6},{8,7},{9,8},{10,9},{11,1... | collective-permute-start | bytes 50696 | tf_op jit(solution)/shard_map/ppermute | solution.py:20
  132.0 4.9 %collective-permute-done.11 = f32[2,16,44,3]{2,1,3,0:T(8,128)S(1)} collective-permute-done((f32[2,16,44,3]{2,1,3,0:T(8,128)S(1)}, f32[2,16,44,3]{2,1,3,0:T(8,128)S(1)}, u32[]{:S(2)}, u32[]{:S(2)}) %collective-permute-start.11) | collective-permute-done | bytes 16928 | tf_op jit(solution)/shard_map/ppermute | solution.py:20
  137.3 2.1 %fusion.45 = f32[2,16,44,128]{3,1,2,0:T(8,128)S(1)} fusion(f32[2,16,44,128]{3,1,2,0:T(8,128)S(1)} %fusion.27, f32[2,16,44,3]{3,1,2,0:T(8,128)S(1)} %copy.116, f32[2,16,44,3]{3,1,2,0:T(8,128)S(1)} %copy.114), kind=kLoop, calls=%fused_computation.90 | loop fusion | flops 3063808 | bytes 1475584 | tf_op jit(solution)/shard_map/add | solution.py:89
  (101 shorter events, 18.3 us)
Async XLA Ops:
  2.0 12.2 %all-to-all-start = ((f32[16,3,512]{2,1,0:T(4,128)}), f32[16,3,512]{2,1,0:T(4,128)S(1)}, u32[]{:S(2)}, u32[]{:S(2)}) async-start(f32[16,3,512]{2,1,0:T(4,128)} %broadcast_in_dim.201), calls=%async_computation | async-start | bytes 262144 | tf_op jit(solution)/shard_map/all_to_all | solution.py:124
  18.5 9.8 %collective-permute-start = (f32[3,1,45,129]{3,2,0,1:T(8,128)S(1)}, f32[3,1,45,129]{3,2,0,1:T(8,128)S(1)}, u32[]{:S(2)}, u32[]{:S(2)}) collective-permute-start(f32[3,1,45,129]{3,2,0,1:T(8,128)S(1)} %get-tuple-element.115), channel_id=1, source_target_pairs={{0,64},{64,128},{128,192},{1,65},{65,129},{129,193},{2,66},{66,130... | collective-permute-start | bytes 208988 | tf_op jit(solution)/shard_map/ppermute | solution.py:19
  26.2 10.8 %collective-permute-start.1 = (f32[3,1,45,129]{3,2,0,1:T(8,128)S(1)}, f32[3,1,45,129]{3,2,0,1:T(8,128)S(1)}, u32[]{:S(2)}, u32[]{:S(2)}) collective-permute-start(f32[3,1,45,129]{3,2,0,1:T(8,128)S(1)} %get-tuple-element.116), channel_id=1, source_target_pairs={{64,0},{128,64},{192,128},{65,1},{129,65},{193,129},{66,2},{130,66... | collective-permute-start | bytes 208988 | tf_op jit(solution)/shard_map/ppermute | solution.py:20
  37.1 4.4 %collective-permute-start.2 = (f32[3,19,1,129]{3,2,0,1:T(1,128)S(1)}, f32[3,19,1,129]{3,2,0,1:T(1,128)S(1)}, u32[]{:S(2)}, u32[]{:S(2)}) collective-permute-start(f32[3,19,1,129]{3,2,0,1:T(1,128)S(1)} %get-tuple-element.107), channel_id=1, source_target_pairs={{0,16},{16,32},{32,48},{1,17},{17,33},{33,49},{2,18},{18,34},{34,5... | collective-permute-start | bytes 88244 | tf_op jit(solution)/shard_map/ppermute | solution.py:19
  40.3 4.9 %collective-permute-start.3 = (f32[3,19,1,129]{3,2,0,1:T(1,128)S(1)}, f32[3,19,1,129]{3,2,0,1:T(1,128)S(1)}, u32[]{:S(2)}, u32[]{:S(2)}) collective-permute-start(f32[3,19,1,129]{3,2,0,1:T(1,128)S(1)} %get-tuple-element.108), channel_id=1, source_target_pairs={{16,0},{32,16},{48,32},{17,1},{33,17},{49,33},{18,2},{34,18},{50,3... | collective-permute-start | bytes 88244 | tf_op jit(solution)/shard_map/ppermute | solution.py:20
  50.9 10.0 %collective-permute-start.5 = (f32[3,17,45,1]{2,3,1,0:T(1,128)S(1)}, f32[3,17,45,1]{2,3,1,0:T(1,128)S(1)}, u32[]{:S(2)}, u32[]{:S(2)}) collective-permute-start(f32[3,17,45,1]{2,3,1,0:T(1,128)S(1)} %copy.108), channel_id=1, source_target_pairs={{1,0},{2,1},{3,2},{4,3},{5,4},{6,5},{7,6},{8,7},{9,8},{10,9},{11,1... | collective-permute-start | bytes 27548 | tf_op jit(solution)/shard_map/ppermute | solution.py:20
  55.1 6.5 %collective-permute-start.4 = (f32[3,17,45,1]{2,3,1,0:T(1,128)S(1)}, f32[3,17,45,1]{2,3,1,0:T(1,128)S(1)}, u32[]{:S(2)}, u32[]{:S(2)}) collective-permute-start(f32[3,17,45,1]{2,3,1,0:T(1,128)S(1)} %copy.106), channel_id=1, source_target_pairs={{0,1},{1,2},{2,3},{3,4},{4,5},{5,6},{6,7},{7,8},{8,9},{9,10},{10,1... | collective-permute-start | bytes 27548 | tf_op jit(solution)/shard_map/ppermute | solution.py:19
  63.0 0.7 copy-start.1
  63.7 34.0 %copy-start = (f32[16,44,128]{2,0,1:T(8,128)S(1)}, f32[16,44,128]{2,0,1:T(8,128)}, u32[]{:S(2)}) copy-start(f32[16,44,128]{2,0,1:T(8,128)} %param.12) | copy-start | bytes 1081348
  97.8 6.6 %collective-permute-start.6 = (f32[2,3,44,128]{3,1,2,0:T(4,128)S(1)}, f32[2,3,44,128]{3,1,2,0:T(4,128)S(1)}, u32[]{:S(2)}, u32[]{:S(2)}) collective-permute-start(f32[2,3,44,128]{3,1,2,0:T(4,128)S(1)} %get-tuple-element.125), channel_id=1, source_target_pairs={{0,64},{64,128},{128,192},{1,65},{65,129},{129,193},{2,66},{66,130... | collective-permute-start | bytes 405512 | tf_op jit(solution)/shard_map/ppermute | solution.py:19
  102.0 10.8 %collective-permute-start.7 = (f32[2,3,44,128]{3,1,2,0:T(4,128)S(1)}, f32[2,3,44,128]{3,1,2,0:T(4,128)S(1)}, u32[]{:S(2)}, u32[]{:S(2)}) collective-permute-start(f32[2,3,44,128]{3,1,2,0:T(4,128)S(1)} %get-tuple-element.126), channel_id=1, source_target_pairs={{64,0},{128,64},{192,128},{65,1},{129,65},{193,129},{66,2},{130,66... | collective-permute-start | bytes 405512 | tf_op jit(solution)/shard_map/ppermute | solution.py:20
  113.6 4.5 %collective-permute-start.8 = (f32[2,16,3,128]{3,1,2,0:T(8,128)S(1)}, f32[2,16,3,128]{3,1,2,0:T(8,128)S(1)}, u32[]{:S(2)}, u32[]{:S(2)}) collective-permute-start(f32[2,16,3,128]{3,1,2,0:T(8,128)S(1)} %get-tuple-element.121), channel_id=1, source_target_pairs={{0,16},{16,32},{32,48},{1,17},{17,33},{33,49},{2,18},{18,34},{34,5... | collective-permute-start | bytes 147464 | tf_op jit(solution)/shard_map/ppermute | solution.py:19
  116.7 5.1 %collective-permute-start.9 = (f32[2,16,3,128]{3,1,2,0:T(8,128)S(1)}, f32[2,16,3,128]{3,1,2,0:T(8,128)S(1)}, u32[]{:S(2)}, u32[]{:S(2)}) collective-permute-start(f32[2,16,3,128]{3,1,2,0:T(8,128)S(1)} %get-tuple-element.122), channel_id=1, source_target_pairs={{16,0},{32,16},{48,32},{17,1},{33,17},{49,33},{18,2},{34,18},{50,3... | collective-permute-start | bytes 147464 | tf_op jit(solution)/shard_map/ppermute | solution.py:20
  122.7 8.8 %collective-permute-start.10 = (f32[2,16,44,3]{2,1,3,0:T(8,128)S(1)}, f32[2,16,44,3]{2,1,3,0:T(8,128)S(1)}, u32[]{:S(2)}, u32[]{:S(2)}) collective-permute-start(f32[2,16,44,3]{2,1,3,0:T(8,128)S(1)} %copy.113), channel_id=1, source_target_pairs={{0,1},{1,2},{2,3},{3,4},{4,5},{5,6},{6,7},{7,8},{8,9},{9,10},{10,1... | collective-permute-start | bytes 50696 | tf_op jit(solution)/shard_map/ppermute | solution.py:19
  129.3 7.5 %collective-permute-start.11 = (f32[2,16,44,3]{2,1,3,0:T(8,128)S(1)}, f32[2,16,44,3]{2,1,3,0:T(8,128)S(1)}, u32[]{:S(2)}, u32[]{:S(2)}) collective-permute-start(f32[2,16,44,3]{2,1,3,0:T(8,128)S(1)} %copy.115), channel_id=1, source_target_pairs={{1,0},{2,1},{3,2},{4,3},{5,4},{6,5},{7,6},{8,7},{9,8},{10,9},{11,1... | collective-permute-start | bytes 50696 | tf_op jit(solution)/shard_map/ppermute | solution.py:20

commit v3 on v2

--- a/solution.py
+++ b/solution.py
@@ -1,7 +1,11 @@
+import functools
+
 import jax
 import jax.numpy as jnp
 from jax import lax
 from jax.sharding import PartitionSpec as P
+from jax.experimental import pallas as pl
+from jax.experimental.pallas import tpu as pltpu
 
 RADIUS = 3
 
@@ -52,33 +56,51 @@
     return own_rows * factor + rim_part * 0.5
 
 
-def element_energy(lower_nodes, upper_nodes, stiffness):
-    ex = lower_nodes.shape[1] - 1
-    ey = lower_nodes.shape[2] - 1
+def energy_kernel(weights, base, up_y, up_z, up_yz, out, *, count_x, chunks):
+    sources = (base, up_z, up_y, up_yz)
 
-    def rows_energy(first_row):
-        slab_low = lax.dynamic_slice_in_dim(lower_nodes, first_row, 5, axis=1)
-        slab_up = lax.dynamic_slice_in_dim(upper_nodes, first_row, 5, axis=1)
-        columns = []
-        for corner in range(8):
-            shift_x = corner // 4
-            shift_y = corner // 2 % 2
-            source = slab_up if corner % 2 == 1 else slab_low
-            columns.append(source[:, shift_x : shift_x + 4, shift_y : shift_y + ey, :])
-        vectors = jnp.stack(columns, axis=1)
-        vectors = vectors.reshape((24,) + vectors.shape[2:])
-        product = jnp.einsum(
-            "ij,jabc->iabc",
-            stiffness,
-            vectors,
-            precision=lax.Precision.HIGHEST,
-            preferred_element_type=jnp.float32,
-        )
-        return jnp.sum(vectors * product, axis=0)
+    def row(i, carry):
+        for first in chunks:
+            vectors = []
+            for component in range(3):
+                for corner in range(8):
+                    shift_x = corner // 4
+                    source = sources[corner % 4]
+                    vectors.append(source[component, i + shift_x, pl.ds(first, 8), :])
+            total = None
+            for a in range(24):
+                inner = weights[a * 24 + a] * vectors[a]
+                for b in range(a + 1, 24):
+                    inner = inner + weights[a * 24 + b] * vectors[b]
+                term = vectors[a] * inner
+                total = term if total is None else total + term
+            out[i, pl.ds(first, 8), :] = total
+        return carry
 
-    starts = jnp.arange(ex // 4, dtype=jnp.int32) * 4
-    energies = lax.map(rows_energy, starts)
-    return energies.reshape((ex,) + energies.shape[2:])
+    lax.fori_loop(0, count_x, row, 0)
+
+
+def element_energy(nodes, stiffness):
+    count_x = nodes.shape[1] - 1
+    count_y = nodes.shape[2] - 1
+    count_z = nodes.shape[3] - 1
+    rows = -(-count_y // 8) * 8
+    pad = ((0, 0), (0, 0), (0, rows - count_y), (0, 0))
+    shifted = [
+        jnp.pad(nodes[:, :, dy : dy + count_y, dz : dz + count_z], pad)
+        for dy, dz in ((0, 0), (1, 0), (0, 1), (1, 1))
+    ]
+    upper = jnp.triu(stiffness + stiffness.T, 1) + jnp.diag(jnp.diagonal(stiffness))
+    weights = upper.reshape(-1)
+    kernel = functools.partial(energy_kernel, count_x=count_x, chunks=tuple(range(0, rows, 8)))
+    vmem = pl.BlockSpec(memory_space=pltpu.VMEM)
+    energy = pl.pallas_call(
+        kernel,
+        out_shape=jax.ShapeDtypeStruct((count_x, rows, count_z), jnp.float32),
+        in_specs=[pl.BlockSpec(memory_space=pltpu.SMEM)] + [vmem] * 4,
+        out_specs=vmem,
+    )(weights, *shifted)
+    return energy[:, :count_y, :]
 
 
 def smooth(field, axis, count):
@@ -139,7 +161,7 @@
     averaged = average_rows(extended, 2, lower_y, upper_y)
     extended = with_halo(averaged, (("gz", 3),), 1)
     averaged = average_rows(extended, 3, lower_z, upper_z)
-    energy = element_energy(averaged[:, :, :, :depth], averaged[:, :, :, 1:], element_stiffness)
+    energy = element_energy(averaged, element_stiffness)
     sens = penal_scale * density * density * energy
     smoothed = filter_field(jnp.stack([density * sens, density]), sides)
     numerator = smoothed[0]

time: 141 us -> 132 us (0.936)
  the two profiles are of different devices: /device:TPU:97 before, /device:TPU:29 now
where the time goes in v3:
time: 132 us; the launch traced here: 130 us
  starting transfers between devices  49.3 us (37%)
  waiting for transfers between devices  26.4 us (20%)
  local copies, waits for them, and re-layouts  21.3 us (16%)
  other arithmetic  16.7 us (13%)
  Pallas kernels  15.2 us (12%)
    ppermute x6, waiting for transfers between devices, with_halo(): after = lax.ppermute(initial, axis, down)  21.6 us
    ppermute x6, starting transfers between devices, with_halo(): after = lax.ppermute(initial, axis, down)  20.6 us
    ppermute x6, starting transfers between devices, with_halo(): before = lax.ppermute(last, axis, up)  20.5 us
    pallas_call x1, Pallas kernels, element_energy(): pl.pallas_call(kernel, out_shape=jax.ShapeDtypeStruct((count_x, rows, cou...  15.2 us
    all_to_all x1, starting transfers between devices, local(): gathered = lax.all_to_all(spread, 'gz', 0, 0, tiled=True)  8.21 us
    unnamed x12, local copies, waits for them, and re-layouts  4.84 us
    ppermute x6, waiting for transfers between devices, with_halo(): before = lax.ppermute(last, axis, up)  4.83 us
    pad x4, local copies, waits for them, and re-layouts, element_energy(): jnp.pad(nodes[:, :, dy:dy + count_y, dz:dz + count_z], pad)  4.55 us
  transfers between devices with their start and end apart: 13, of which 8 were waited for; matrix products, arithmetic and copies ran while one was open for 9% of the time, Pallas kernels for 0%

profile of v3, /device:TPU:29, one launch (start us, length us, event | category | flops | bytes accessed | tf_op | source)
XLA Modules:
  0.0 129.9 jit_solution(8704761999043540844)
XLA Ops:
  0.6 1.4 %broadcast_in_dim.219 = f32[16,3,512]{2,1,0:T(4,128)} broadcast(f32[3,512]{1,0:T(4,128)} %param.8), dimensions={1,2} | broadcast | bytes 104448 | tf_op jit(solution)/shard_map/broadcast_in_dim | solution.py:145
  2.0 8.2 %all-to-all-start = ((f32[16,3,512]{2,1,0:T(4,128)}), f32[16,3,512]{2,1,0:T(4,128)S(1)}, u32[]{:S(2)}, u32[]{:S(2)}) async-start(f32[16,3,512]{2,1,0:T(4,128)} %broadcast_in_dim.219), calls=%async_computation | async-start | bytes 262144 | tf_op jit(solution)/shard_map/all_to_all | solution.py:146
  11.1 2.3 %copy.80 = f32[3,17,45,1]{3,2,1,0:T(8,128)} copy(f32[3,17,45,1]{2,3,1,0:T(1,128)} %param.7) | data formatting | bytes 18360 | tf_op args[1]
  14.2 1.5 %gather_fusion = f32[24]{0:T(128)S(1)} fusion(f32[24,24]{1,0:T(8,128)} %param.11, s32[24]{0:T(128)S(1)} %or_bitcast_fusion), kind=kCustom, calls=%fused_computation | custom fusion | bytes 384 | tf_op jit(solution)/shard_map/jit(diagonal)/cond/branch_0_fun/gather | solution.py:93
  15.8 3.0 %broadcast_multiply_fusion.1 = (f32[17,45,129]{2,1,0:T(8,128)S(1)}, f32[17,45,129]{2,1,0:T(8,128)}, f32[17,45,129]{2,1,0:T(8,128)}, f32[17,45,129]{2,1,0:T(8,128...) fusion(f32[17,45]{1,0:T(8,128)S(1)} %get-tuple-element.64, ...), kind=kLoop, calls=%fused_computation.82 | loop fusion | flops 789480 | bytes 3171192 | tf_op jit(solution)/shard_map/mul | solution.py:39
  19.3 4.2 %fusion.8 = f32[3,17,45,129]{3,2,1,0:T(8,128)S(1)} fusion(f32[3,17,45,1]{3,2,1,0:T(8,128)} %copy.80, f32[3,17,45,128]{3,2,1,0:T(8,128)} %param.6, f32[3]{0:T(128)S(1)} %get-tuple-element.15, f32[17,45,129]{2,1,0:T(8,128)} %get-tuple-element.55, f32[3]{0:T(128)S(1)} %get-tuple-element.16, f32[17,45,129]{2,1,0:T(8,128)S(1)} %get-tuple-element.54, ...), kind=kLoop, calls=%fused_computation.13 | loop fusion | flops 5032935 | bytes 5526456 | tf_op jit(solution)/shard_map/add | solution.py:40
  23.6 7.2 %collective-permute-start = (f32[3,1,45,129]{3,2,1,0:T(8,128)S(1)}, f32[3,1,45,129]{3,2,1,0:T(8,128)S(1)}, u32[]{:S(2)}, u32[]{:S(2)}) collective-permute-start(f32[3,1,45,129]{3,2,1,0:T(8,128)S(1)} %get-tuple-element.34), channel_id=1, source_target_pairs={{0,64},{64,128},{128,192},{1,65},{65,129},{129,193},{2,66},{66,130... | collective-permute-start | bytes 208988 | tf_op jit(solution)/shard_map/ppermute | solution.py:23
  30.8 1.9 %collective-permute-start.1 = (f32[3,1,45,129]{3,2,1,0:T(8,128)S(1)}, f32[3,1,45,129]{3,2,1,0:T(8,128)S(1)}, u32[]{:S(2)}, u32[]{:S(2)}) collective-permute-start(f32[3,1,45,129]{3,2,1,0:T(8,128)S(1)} %get-tuple-element.35), channel_id=1, source_target_pairs={{64,0},{128,64},{192,128},{65,1},{129,65},{193,129},{66,2},{130,66... | collective-permute-start | bytes 208988 | tf_op jit(solution)/shard_map/ppermute | solution.py:24
  32.9 8.8 %collective-permute-done.1 = f32[3,1,45,129]{3,2,1,0:T(8,128)S(1)} collective-permute-done((f32[3,1,45,129]{3,2,1,0:T(8,128)S(1)}, f32[3,1,45,129]{3,2,1,0:T(8,128)S(1)}, u32[]{:S(2)}, u32[]{:S(2)}) %collective-permute-start.1) | collective-permute-done | bytes 69692 | tf_op jit(solution)/shard_map/ppermute | solution.py:24
  41.8 2.8 %collective-permute-start.2 = (f32[3,19,1,129]{3,2,1,0:T(1,128)S(1)}, f32[3,19,1,129]{3,2,1,0:T(1,128)S(1)}, u32[]{:S(2)}, u32[]{:S(2)}) collective-permute-start(f32[3,19,1,129]{3,2,1,0:T(1,128)S(1)} %get-tuple-element.24), channel_id=1, source_target_pairs={{0,16},{16,32},{32,48},{1,17},{17,33},{33,49},{2,18},{18,34},{34,5... | collective-permute-start | bytes 88244 | tf_op jit(solution)/shard_map/ppermute | solution.py:23
  44.6 2.5 %collective-permute-start.3 = (f32[3,19,1,129]{3,2,1,0:T(1,128)S(1)}, f32[3,19,1,129]{3,2,1,0:T(1,128)S(1)}, u32[]{:S(2)}, u32[]{:S(2)}) collective-permute-start(f32[3,19,1,129]{3,2,1,0:T(1,128)S(1)} %get-tuple-element.25), channel_id=1, source_target_pairs={{16,0},{32,16},{48,32},{17,1},{33,17},{49,33},{18,2},{34,18},{50,3... | collective-permute-start | bytes 88244 | tf_op jit(solution)/shard_map/ppermute | solution.py:24
  47.1 2.4 %collective-permute-done.3 = f32[3,19,1,129]{3,2,1,0:T(1,128)S(1)} collective-permute-done((f32[3,19,1,129]{3,2,1,0:T(1,128)S(1)}, f32[3,19,1,129]{3,2,1,0:T(1,128)S(1)}, u32[]{:S(2)}, u32[]{:S(2)}) %collective-permute-start.3) | collective-permute-done | bytes 29444 | tf_op jit(solution)/shard_map/ppermute | solution.py:24
  51.7 1.7 %fusion.71 = (f32[3,17,45,1]{3,2,1,0:T(8,128)}, f32[3,17,45,1]{3,2,1,0:T(8,128)}) fusion(f32[3,17,45,129]{3,2,1,0:T(8,128)S(1)} %fusion), kind=kLoop, calls=%fused_computation.185 | loop fusion | bytes 36720 | tf_op jit(solution)/shard_map/slice | solution.py:21
  53.4 1.8 %copy.82 = f32[3,17,45,1]{2,3,1,0:T(1,128)S(1)} copy(f32[3,17,45,1]{3,2,1,0:T(8,128)} %get-tuple-element.31) | data formatting | bytes 18360 | tf_op jit(solution)/shard_map/slice | solution.py:22
  55.2 4.7 %collective-permute-start.5 = (f32[3,17,45,1]{2,3,1,0:T(1,128)S(1)}, f32[3,17,45,1]{2,3,1,0:T(1,128)S(1)}, u32[]{:S(2)}, u32[]{:S(2)}) collective-permute-start(f32[3,17,45,1]{2,3,1,0:T(1,128)S(1)} %copy.82), channel_id=1, source_target_pairs={{1,0},{2,1},{3,2},{4,3},{5,4},{6,5},{7,6},{8,7},{9,8},{10,9},{11,1... | collective-permute-start | bytes 27548 | tf_op jit(solution)/shard_map/ppermute | solution.py:24
  59.9 1.8 %copy.81 = f32[3,17,45,1]{2,3,1,0:T(1,128)S(1)} copy(f32[3,17,45,1]{3,2,1,0:T(8,128)} %get-tuple-element.30) | data formatting | bytes 18360 | tf_op jit(solution)/shard_map/slice | solution.py:21
  61.7 1.9 %collective-permute-start.4 = (f32[3,17,45,1]{2,3,1,0:T(1,128)S(1)}, f32[3,17,45,1]{2,3,1,0:T(1,128)S(1)}, u32[]{:S(2)}, u32[]{:S(2)}) collective-permute-start(f32[3,17,45,1]{2,3,1,0:T(1,128)S(1)} %copy.81), channel_id=1, source_target_pairs={{0,1},{1,2},{2,3},{3,4},{4,5},{5,6},{6,7},{7,8},{8,9},{9,10},{10,1... | collective-permute-start | bytes 27548 | tf_op jit(solution)/shard_map/ppermute | solution.py:23
  64.4 4.6 %collective-permute-done.4 = f32[3,17,45,1]{2,3,1,0:T(1,128)S(1)} collective-permute-done((f32[3,17,45,1]{2,3,1,0:T(1,128)S(1)}, f32[3,17,45,1]{2,3,1,0:T(1,128)S(1)}, u32[]{:S(2)}, u32[]{:S(2)}) %collective-permute-start.4) | collective-permute-done | bytes 9212 | tf_op jit(solution)/shard_map/ppermute | solution.py:23
  68.9 1.3 %multiply_add_fusion = f32[3,17,45,129]{3,2,1,0:T(8,128)S(1)} fusion(f32[3,17,45]{2,1,0:T(8,128)S(1)} %bitcast.45, f32[3,17,45]{2,1,0:T(8,128)S(1)} %bitcast.46, f32[129]{0:T(256)S(1)} %and_select_fusion.16, pred[129]{0:T(512)(128)(4,1)S(1)} %get-tuple-element.76, pred[129]{0:T(512)(128)(4,1)S(1)} %get-tuple-element.77, f32[3,17,129]{2,1,0:T(8,128)S(1)} %bitcast.41, ...), kind=kLoop, calls=%fused_computation.14 | loop fusion | flops 3552660 | bytes 2440476 | tf_op jit(solution)/shard_map/add | solution.py:56
  71.1 1.1 pad.13.base
  73.4 1.1 pad.15.up_z
  74.5 1.2 pad.16.up_yz
  75.7 15.2 %shard_map.77 = f32[16,48,128]{2,1,0:T(8,128)} custom-call(f32[576]{0:T(1024)} %reshape.412.weights, f32[3,17,48,128]{3,2,1,0:T(8,128)} %pad.13.base, f32[3,17,48,128]{3,2,1,0:T(8,128)} %pad.14.up_y, f32[3,17,48,128]{3,2,1,0:T(8,128)} %pad.15.up_z, f32[3,17,48,128]{3,2,1,0:T(8,128)} %pad.16.up_yz), custom_call_target="tpu_custom_call" | custom-call | tf_op jit(solution)/shard_map/pallas_call | solution.py:97
  92.1 4.6 %collective-permute-start.6 = (f32[2,3,44,128]{3,2,1,0:T(8,128)S(1)}, f32[2,3,44,128]{3,2,1,0:T(8,128)S(1)}, u32[]{:S(2)}, u32[]{:S(2)}) collective-permute-start(f32[2,3,44,128]{3,2,1,0:T(8,128)S(1)} %get-tuple-element.44), channel_id=1, source_target_pairs={{0,64},{64,128},{128,192},{1,65},{65,129},{129,193},{2,66},{66,130... | collective-permute-start | bytes 405512 | tf_op jit(solution)/shard_map/ppermute | solution.py:23
  96.7 1.9 %collective-permute-start.7 = (f32[2,3,44,128]{3,2,1,0:T(8,128)S(1)}, f32[2,3,44,128]{3,2,1,0:T(8,128)S(1)}, u32[]{:S(2)}, u32[]{:S(2)}) collective-permute-start(f32[2,3,44,128]{3,2,1,0:T(8,128)S(1)} %get-tuple-element.45), channel_id=1, source_target_pairs={{64,0},{128,64},{192,128},{65,1},{129,65},{193,129},{66,2},{130,66... | collective-permute-start | bytes 405512 | tf_op jit(solution)/shard_map/ppermute | solution.py:24
  98.8 8.3 %collective-permute-done.7 = f32[2,3,44,128]{3,2,1,0:T(8,128)S(1)} collective-permute-done((f32[2,3,44,128]{3,2,1,0:T(8,128)S(1)}, f32[2,3,44,128]{3,2,1,0:T(8,128)S(1)}, u32[]{:S(2)}, u32[]{:S(2)}) %collective-permute-start.7) | collective-permute-done | bytes 135200 | tf_op jit(solution)/shard_map/ppermute | solution.py:24
  107.6 1.9 %collective-permute-start.8 = (f32[2,16,3,128]{3,2,1,0:T(4,128)S(1)}, f32[2,16,3,128]{3,2,1,0:T(4,128)S(1)}, u32[]{:S(2)}, u32[]{:S(2)}) collective-permute-start(f32[2,16,3,128]{3,2,1,0:T(4,128)S(1)} %get-tuple-element.40), channel_id=1, source_target_pairs={{0,16},{16,32},{32,48},{1,17},{17,33},{33,49},{2,18},{18,34},{34,5... | collective-permute-start | bytes 147464 | tf_op jit(solution)/shard_map/ppermute | solution.py:23
  109.5 3.4 %collective-permute-start.9 = (f32[2,16,3,128]{3,2,1,0:T(4,128)S(1)}, f32[2,16,3,128]{3,2,1,0:T(4,128)S(1)}, u32[]{:S(2)}, u32[]{:S(2)}) collective-permute-start(f32[2,16,3,128]{3,2,1,0:T(4,128)S(1)} %get-tuple-element.41), channel_id=1, source_target_pairs={{16,0},{32,16},{48,32},{17,1},{33,17},{49,33},{18,2},{34,18},{50,3... | collective-permute-start | bytes 147464 | tf_op jit(solution)/shard_map/ppermute | solution.py:24
  112.9 1.6 %collective-permute-done.9 = f32[2,16,3,128]{3,2,1,0:T(4,128)S(1)} collective-permute-done((f32[2,16,3,128]{3,2,1,0:T(4,128)S(1)}, f32[2,16,3,128]{3,2,1,0:T(4,128)S(1)}, u32[]{:S(2)}, u32[]{:S(2)}) %collective-permute-start.9) | collective-permute-done | bytes 49184 | tf_op jit(solution)/shard_map/ppermute | solution.py:24
  115.8 1.9 %collective-permute-start.10 = (f32[2,16,44,3]{2,1,3,0:T(8,128)S(1)}, f32[2,16,44,3]{2,1,3,0:T(8,128)S(1)}, u32[]{:S(2)}, u32[]{:S(2)}) collective-permute-start(f32[2,16,44,3]{2,1,3,0:T(8,128)S(1)} %copy.85), channel_id=1, source_target_pairs={{0,1},{1,2},{2,3},{3,4},{4,5},{5,6},{6,7},{7,8},{8,9},{9,10},{10,1... | collective-permute-start | bytes 50696 | tf_op jit(solution)/shard_map/ppermute | solution.py:23
  118.1 6.2 %collective-permute-start.11 = (f32[2,16,44,3]{2,1,3,0:T(8,128)S(1)}, f32[2,16,44,3]{2,1,3,0:T(8,128)S(1)}, u32[]{:S(2)}, u32[]{:S(2)}) collective-permute-start(f32[2,16,44,3]{2,1,3,0:T(8,128)S(1)} %copy.87), channel_id=1, source_target_pairs={{1,0},{2,1},{3,2},{4,3},{5,4},{6,5},{7,6},{8,7},{9,8},{10,9},{11,1... | collective-permute-start | bytes 50696 | tf_op jit(solution)/shard_map/ppermute | solution.py:24
  125.7 2.3 %fusion.30 = f32[2,16,44,128]{3,2,1,0:T(8,128)S(1)} fusion(f32[2,16,44,128]{3,2,1,0:T(8,128)S(1)} %fusion.17, f32[2,16,44,3]{3,2,1,0:T(8,128)S(1)} %copy.88, f32[2,16,44,3]{3,2,1,0:T(8,128)S(1)} %copy.86), kind=kLoop, calls=%fused_computation.55 | loop fusion | flops 3063808 | bytes 1475584 | tf_op jit(solution)/shard_map/add | solution.py:111
  (61 shorter events, 14.1 us)
Async XLA Ops:
  2.0 16.8 %all-to-all-start = ((f32[16,3,512]{2,1,0:T(4,128)}), f32[16,3,512]{2,1,0:T(4,128)S(1)}, u32[]{:S(2)}, u32[]{:S(2)}) async-start(f32[16,3,512]{2,1,0:T(4,128)} %broadcast_in_dim.219), calls=%async_computation | async-start | bytes 262144 | tf_op jit(solution)/shard_map/all_to_all | solution.py:146
  15.8 3.0 %copy-start = (f32[24,24]{1,0:T(8,128)S(1)}, f32[24,24]{1,0:T(8,128)}, u32[]{:S(2)}) copy-start(f32[24,24]{1,0:T(8,128)} %param.11) | copy-start | bytes 6916
  23.6 9.3 %collective-permute-start = (f32[3,1,45,129]{3,2,1,0:T(8,128)S(1)}, f32[3,1,45,129]{3,2,1,0:T(8,128)S(1)}, u32[]{:S(2)}, u32[]{:S(2)}) collective-permute-start(f32[3,1,45,129]{3,2,1,0:T(8,128)S(1)} %get-tuple-element.34), channel_id=1, source_target_pairs={{0,64},{64,128},{128,192},{1,65},{65,129},{129,193},{2,66},{66,130... | collective-permute-start | bytes 208988 | tf_op jit(solution)/shard_map/ppermute | solution.py:23
  30.8 10.9 %collective-permute-start.1 = (f32[3,1,45,129]{3,2,1,0:T(8,128)S(1)}, f32[3,1,45,129]{3,2,1,0:T(8,128)S(1)}, u32[]{:S(2)}, u32[]{:S(2)}) collective-permute-start(f32[3,1,45,129]{3,2,1,0:T(8,128)S(1)} %get-tuple-element.35), channel_id=1, source_target_pairs={{64,0},{128,64},{192,128},{65,1},{129,65},{193,129},{66,2},{130,66... | collective-permute-start | bytes 208988 | tf_op jit(solution)/shard_map/ppermute | solution.py:24
  41.8 5.3 %collective-permute-start.2 = (f32[3,19,1,129]{3,2,1,0:T(1,128)S(1)}, f32[3,19,1,129]{3,2,1,0:T(1,128)S(1)}, u32[]{:S(2)}, u32[]{:S(2)}) collective-permute-start(f32[3,19,1,129]{3,2,1,0:T(1,128)S(1)} %get-tuple-element.24), channel_id=1, source_target_pairs={{0,16},{16,32},{32,48},{1,17},{17,33},{33,49},{2,18},{18,34},{34,5... | collective-permute-start | bytes 88244 | tf_op jit(solution)/shard_map/ppermute | solution.py:23
  44.6 4.9 %collective-permute-start.3 = (f32[3,19,1,129]{3,2,1,0:T(1,128)S(1)}, f32[3,19,1,129]{3,2,1,0:T(1,128)S(1)}, u32[]{:S(2)}, u32[]{:S(2)}) collective-permute-start(f32[3,19,1,129]{3,2,1,0:T(1,128)S(1)} %get-tuple-element.25), channel_id=1, source_target_pairs={{16,0},{32,16},{48,32},{17,1},{33,17},{49,33},{18,2},{34,18},{50,3... | collective-permute-start | bytes 88244 | tf_op jit(solution)/shard_map/ppermute | solution.py:24
  55.2 9.2 %collective-permute-start.5 = (f32[3,17,45,1]{2,3,1,0:T(1,128)S(1)}, f32[3,17,45,1]{2,3,1,0:T(1,128)S(1)}, u32[]{:S(2)}, u32[]{:S(2)}) collective-permute-start(f32[3,17,45,1]{2,3,1,0:T(1,128)S(1)} %copy.82), channel_id=1, source_target_pairs={{1,0},{2,1},{3,2},{4,3},{5,4},{6,5},{7,6},{8,7},{9,8},{10,9},{11,1... | collective-permute-start | bytes 27548 | tf_op jit(solution)/shard_map/ppermute | solution.py:24
  61.7 7.3 %collective-permute-start.4 = (f32[3,17,45,1]{2,3,1,0:T(1,128)S(1)}, f32[3,17,45,1]{2,3,1,0:T(1,128)S(1)}, u32[]{:S(2)}, u32[]{:S(2)}) collective-permute-start(f32[3,17,45,1]{2,3,1,0:T(1,128)S(1)} %copy.81), channel_id=1, source_target_pairs={{0,1},{1,2},{2,3},{3,4},{4,5},{5,6},{6,7},{7,8},{8,9},{9,10},{10,1... | collective-permute-start | bytes 27548 | tf_op jit(solution)/shard_map/ppermute | solution.py:23
  75.7 15.2 %copy-start.1 = (f32[16,44,128]{2,0,1:T(8,128)S(1)}, f32[16,44,128]{2,0,1:T(8,128)}, u32[]{:S(2)}) copy-start(f32[16,44,128]{2,0,1:T(8,128)} %param.10) | copy-start | bytes 1081348
  92.1 6.7 %collective-permute-start.6 = (f32[2,3,44,128]{3,2,1,0:T(8,128)S(1)}, f32[2,3,44,128]{3,2,1,0:T(8,128)S(1)}, u32[]{:S(2)}, u32[]{:S(2)}) collective-permute-start(f32[2,3,44,128]{3,2,1,0:T(8,128)S(1)} %get-tuple-element.44), channel_id=1, source_target_pairs={{0,64},{64,128},{128,192},{1,65},{65,129},{129,193},{2,66},{66,130... | collective-permute-start | bytes 405512 | tf_op jit(solution)/shard_map/ppermute | solution.py:23
  96.7 10.4 %collective-permute-start.7 = (f32[2,3,44,128]{3,2,1,0:T(8,128)S(1)}, f32[2,3,44,128]{3,2,1,0:T(8,128)S(1)}, u32[]{:S(2)}, u32[]{:S(2)}) collective-permute-start(f32[2,3,44,128]{3,2,1,0:T(8,128)S(1)} %get-tuple-element.45), channel_id=1, source_target_pairs={{64,0},{128,64},{192,128},{65,1},{129,65},{193,129},{66,2},{130,66... | collective-permute-start | bytes 405512 | tf_op jit(solution)/shard_map/ppermute | solution.py:24
  107.6 5.4 %collective-permute-start.8 = (f32[2,16,3,128]{3,2,1,0:T(4,128)S(1)}, f32[2,16,3,128]{3,2,1,0:T(4,128)S(1)}, u32[]{:S(2)}, u32[]{:S(2)}) collective-permute-start(f32[2,16,3,128]{3,2,1,0:T(4,128)S(1)} %get-tuple-element.40), channel_id=1, source_target_pairs={{0,16},{16,32},{32,48},{1,17},{17,33},{33,49},{2,18},{18,34},{34,5... | collective-permute-start | bytes 147464 | tf_op jit(solution)/shard_map/ppermute | solution.py:23
  109.5 5.0 %collective-permute-start.9 = (f32[2,16,3,128]{3,2,1,0:T(4,128)S(1)}, f32[2,16,3,128]{3,2,1,0:T(4,128)S(1)}, u32[]{:S(2)}, u32[]{:S(2)}) collective-permute-start(f32[2,16,3,128]{3,2,1,0:T(4,128)S(1)} %get-tuple-element.41), channel_id=1, source_target_pairs={{16,0},{32,16},{48,32},{17,1},{33,17},{49,33},{18,2},{34,18},{50,3... | collective-permute-start | bytes 147464 | tf_op jit(solution)/shard_map/ppermute | solution.py:24
  115.8 8.5 %collective-permute-start.10 = (f32[2,16,44,3]{2,1,3,0:T(8,128)S(1)}, f32[2,16,44,3]{2,1,3,0:T(8,128)S(1)}, u32[]{:S(2)}, u32[]{:S(2)}) collective-permute-start(f32[2,16,44,3]{2,1,3,0:T(8,128)S(1)} %copy.85), channel_id=1, source_target_pairs={{0,1},{1,2},{2,3},{3,4},{4,5},{5,6},{6,7},{7,8},{8,9},{9,10},{10,1... | collective-permute-start | bytes 50696 | tf_op jit(solution)/shard_map/ppermute | solution.py:23
  118.1 7.2 %collective-permute-start.11 = (f32[2,16,44,3]{2,1,3,0:T(8,128)S(1)}, f32[2,16,44,3]{2,1,3,0:T(8,128)S(1)}, u32[]{:S(2)}, u32[]{:S(2)}) collective-permute-start(f32[2,16,44,3]{2,1,3,0:T(8,128)S(1)} %copy.87), channel_id=1, source_target_pairs={{1,0},{2,1},{3,2},{4,3},{5,4},{6,5},{7,6},{8,7},{9,8},{10,9},{11,1... | collective-permute-start | bytes 50696 | tf_op jit(solution)/shard_map/ppermute | solution.py:24

commit v4 on v3

--- a/solution.py
+++ b/solution.py
@@ -13,15 +13,100 @@
 penal_scale = -3.0 / 96.0
 
 
+def halo_kernel(low, high, before, after, landed_before, landed_after, send_sem, recv_sem, *, axis, count):
+    me = lax.axis_index(axis)
+    has_lower = me > 0
+    has_upper = me < count - 1
+    mesh_ids = pl.DeviceIdType.MESH
+    barrier = pltpu.get_barrier_semaphore()
+
+    @pl.when(has_lower)
+    def _():
+        pl.semaphore_signal(barrier, 1, device_id={axis: me - 1}, device_id_type=mesh_ids)
+
+    @pl.when(has_upper)
+    def _():
+        pl.semaphore_signal(barrier, 1, device_id={axis: me + 1}, device_id_type=mesh_ids)
+
+    pl.semaphore_wait(barrier, has_lower.astype(jnp.int32) + has_upper.astype(jnp.int32))
+
+    to_upper = pltpu.make_async_remote_copy(
+        src_ref=high,
+        dst_ref=landed_before,
+        send_sem=send_sem.at[0],
+        recv_sem=recv_sem.at[0],
+        device_id={axis: me + 1},
+        device_id_type=mesh_ids,
+    )
+    to_lower = pltpu.make_async_remote_copy(
+        src_ref=low,
+        dst_ref=landed_after,
+        send_sem=send_sem.at[1],
+        recv_sem=recv_sem.at[1],
+        device_id={axis: me - 1},
+        device_id_type=mesh_ids,
+    )
+
+    @pl.when(has_upper)
+    def _():
+        to_upper.start()
+
+    @pl.when(has_lower)
+    def _():
+        to_lower.start()
+
+    @pl.when(has_upper)
+    def _():
+        to_upper.wait_send()
+        to_lower.wait_recv()
+        after[...] = landed_after[...]
+
+    @pl.when(has_lower)
+    def _():
+        to_lower.wait_send()
+        to_upper.wait_recv()
+        before[...] = landed_before[...]
+
+    @pl.when(jnp.logical_not(has_upper))
+    def _():
+        after[...] = jnp.zeros(after.shape, after.dtype)
+
+    @pl.when(jnp.logical_not(has_lower))
+    def _():
+        before[...] = jnp.zeros(before.shape, before.dtype)
+
+
+HALO_IDS = {}
+
+
+def exchange(low, high, axis):
+    key = (axis, low.shape)
+    if key not in HALO_IDS:
+        HALO_IDS[key] = len(HALO_IDS)
+    kernel = functools.partial(halo_kernel, axis=axis, count=lax.axis_size(axis))
+    vmem = pl.BlockSpec(memory_space=pltpu.VMEM)
+    slab = jax.ShapeDtypeStruct(low.shape, low.dtype)
+    return pl.pallas_call(
+        kernel,
+        out_shape=(slab, slab),
+        in_specs=[vmem, vmem],
+        out_specs=(vmem, vmem),
+        scratch_shapes=[
+            pltpu.VMEM(low.shape, low.dtype),
+            pltpu.VMEM(low.shape, low.dtype),
+            pltpu.SemaphoreType.DMA((2,)),
+            pltpu.SemaphoreType.DMA((2,)),
+        ],
+        compiler_params=pltpu.CompilerParams(collective_id=HALO_IDS[key], has_side_effects=True),
+    )(low, high)
+
+
 def with_halo(shard, sides, width):
     for axis, dim in sides:
-        count, length = (lax.axis_size(axis), shard.shape[dim])
-        up = [(i, (i + 1) % count) for i in range(count - 1)]
-        down = [(j, i) for i, j in up]
+        length = shard.shape[dim]
         last = lax.slice_in_dim(shard, length - width, length, axis=dim)
         initial = lax.slice_in_dim(shard, 0, width, axis=dim)
-        before = lax.ppermute(last, axis, up)
-        after = lax.ppermute(initial, axis, down)
+        before, after = exchange(initial, last, axis)
         shard = jnp.concatenate([before, shard, after], axis=dim)
     return shard
 

time: 132 us -> 194 us (1.47)
  Pallas kernels: 15.2 us -> 136 us
  starting transfers between devices: 49.3 us -> 8.21 us
  waiting for transfers between devices: 26.4 us -> 0.01 us
  other arithmetic: 16.7 us -> 28.2 us
  local copies, waits for them, and re-layouts: 21.3 us -> 18.7 us
    pallas_call x0 -> x6, Pallas kernels: none -> 121 us  [exchange(): pl.pallas_call(kernel, out_shape=(slab, slab), in_specs=[vmem, vmem], out...]
    ppermute x12 -> x0, starting transfers between devices: 41 us -> none  [the longest x6 20.6 us: with_halo(): after = lax.ppermute(initial, axis, down)]
    ppermute x12 -> x0, waiting for transfers between devices: 26.4 us -> none  [the longest x6 21.6 us: with_halo(): after = lax.ppermute(initial, axis, down)]
    add x3, other arithmetic: 3.29 us -> 6.81 us  [smooth(): summed = term_value if summed is None else summed + term_value]
    pallas_call x0 -> x2, other arithmetic: none -> 3.39 us  [exchange(): pl.pallas_call(kernel, out_shape=(slab, slab), in_specs=[vmem, vmem], out...]
    concatenate x2 -> x3, other arithmetic: 0.61 us -> 3.17 us  [with_halo(): shard = jnp.concatenate([before, shard, after], axis=dim)]
    slice x2 -> x0, local copies, waits for them, and re-layouts: 2.14 us -> none  [with_halo(): initial = lax.slice_in_dim(shard, 0, width, axis=dim)]
    slice x6 -> x4, local copies, waits for them, and re-layouts: 4.12 us -> 4.44 us  [with_halo(): last = lax.slice_in_dim(shard, length - width, length, axis=dim)]
  transfers between devices with their start and end apart: 13 -> 1, of which waited for: 8 -> 0; matrix products, arithmetic and copies ran while one was open for 9% -> 5% of each run, Pallas kernels for 0% -> 0%
where the time goes in v4:
time: 194 us; the launch traced here: 192 us
  Pallas kernels  136 us (70%)
  other arithmetic  28.2 us (15%)
  local copies, waits for them, and re-layouts  18.7 us (10%)
  starting transfers between devices  8.21 us (4%)
    pallas_call x6, Pallas kernels, exchange(): pl.pallas_call(kernel, out_shape=(slab, slab), in_specs=[vmem, vmem], out...  121 us
    pallas_call x1, Pallas kernels, element_energy(): pl.pallas_call(kernel, out_shape=jax.ShapeDtypeStruct((count_x, rows, cou...  15.2 us
    all_to_all x1, starting transfers between devices, local(): gathered = lax.all_to_all(spread, 'gz', 0, 0, tiled=True)  8.21 us
    add x3, other arithmetic, smooth(): summed = term_value if summed is None else summed + term_value  6.81 us
    unnamed x16, local copies, waits for them, and re-layouts  4.88 us
    pad x4, local copies, waits for them, and re-layouts, element_energy(): jnp.pad(nodes[:, :, dy:dy + count_y, dz:dz + count_z], pad)  4.55 us
    slice x4, local copies, waits for them, and re-layouts, with_halo(): last = lax.slice_in_dim(shard, length - width, length, axis=dim)  4.44 us
    add x1, other arithmetic, recover(): summed = summed + basis[None] * corner_vals[:, corner][:, None, None, None]  4.24 us
  transfers between devices with their start and end apart: 1, of which 0 were waited for; matrix products, arithmetic and copies ran while one was open for 5% of the time, Pallas kernels for 0%

profile of v4, /device:TPU:29, one launch (start us, length us, event | category | flops | bytes accessed | tf_op | source)
XLA Modules:
  0.0 192.0 jit_solution(11000908311441293807)
XLA Ops:
  0.6 1.4 broadcast_in_dim.219
  2.0 8.2 %all-to-all-start = ((f32[16,3,512]{2,1,0:T(4,128)}), f32[16,3,512]{2,1,0:T(4,128)S(1)}, u32[]{:S(2)}, u32[]{:S(2)}) async-start(f32[16,3,512]{2,1,0:T(4,128)} %broadcast_in_dim.219), calls=%async_computation | async-start | bytes 262144 | tf_op jit(solution)/shard_map/all_to_all | solution.py:231
  11.1 2.3 %copy.62 = f32[3,17,45,1]{3,2,1,0:T(8,128)} copy(f32[3,17,45,1]{2,3,1,0:T(1,128)} %param.7) | data formatting | bytes 18360 | tf_op args[1]
  13.4 0.8 copy.60
  14.2 1.5 gather_fusion
  17.4 3.0 %broadcast_multiply_fusion.1 = (f32[17,45,129]{2,1,0:T(8,128)S(1)}, f32[17,45,129]{2,1,0:T(8,128)}, f32[17,45,129]{2,1,0:T(8,128)}, f32[17,45,129]{2,1,0:T(8,128...) fusion(f32[17,45]{1,0:T(8,128)S(1)} %get-tuple-element.88, ...), kind=kLoop, calls=%fused_computation.82 | loop fusion | flops 789480 | bytes 3171192 | tf_op jit(solution)/shard_map/mul | solution.py:124
  20.9 4.2 %fusion.8 = f32[3,17,45,129]{3,2,1,0:T(8,128)S(1)} fusion(f32[3,17,45,1]{3,2,1,0:T(8,128)} %copy.62, f32[3,17,45,128]{3,2,1,0:T(8,128)} %param.6, f32[3]{0:T(128)S(1)} %get-tuple-element.39, f32[17,45,129]{2,1,0:T(8,128)} %get-tuple-element.79, f32[3]{0:T(128)S(1)} %get-tuple-element.40, f32[17,45,129]{2,1,0:T(8,128)S(1)} %get-tuple-element.78, ...), kind=kLoop, calls=%fused_computation.13 | loop fusion | flops 5032935 | bytes 5526456 | tf_op jit(solution)/shard_map/add | solution.py:125
  25.9 10.3 %shard_map.77 = (f32[3,1,45,129]{3,2,1,0:T(8,128)}, f32[3,1,45,129]{3,2,1,0:T(8,128)}) custom-call(f32[3,1,45,129]{3,2,1,0:T(8,128)} %get-tuple-element.59.low, f32[3,1,45,129]{3,2,1,0:T(8,128)} %get-tuple-element.58.high), custom_call_target="tpu_custom_call" | custom-call | tf_op jit(solution)/shard_map/pallas_call | solution.py:89
  36.3 1.6 pad_maximum_fusion.7
  37.8 4.6 %shard_map.78 = (f32[3,19,1,129]{3,2,1,0:T(1,128)}, f32[3,19,1,129]{3,2,1,0:T(1,128)}) custom-call(f32[3,19,1,129]{3,2,1,0:T(1,128)} %get-tuple-element.49.low, f32[3,19,1,129]{3,2,1,0:T(1,128)} %get-tuple-element.48.high), custom_call_target="tpu_custom_call" | custom-call | tf_op jit(solution)/shard_map/pallas_call | solution.py:89
  44.6 0.8 fusion
  45.4 1.6 fusion.71
  47.0 57.2 %shard_map.79 = (f32[3,17,45,1]{3,2,1,0:T(8,128)}, f32[3,17,45,1]{3,2,1,0:T(8,128)}) custom-call(f32[3,17,45,1]{3,2,1,0:T(8,128)} %get-tuple-element.55.low, f32[3,17,45,1]{3,2,1,0:T(8,128)} %get-tuple-element.54.high), custom_call_target="tpu_custom_call" | custom-call | tf_op jit(solution)/shard_map/pallas_call | solution.py:89
  104.2 1.7 reduce.8
  105.9 1.7 reduce.9
  107.6 1.3 multiply_add_fusion
  109.0 0.9 fusion.70
  109.8 1.1 pad.13.base
  110.9 1.1 pad.14.up_y
  112.1 1.1 pad.15.up_z
  113.2 1.2 pad.16.up_yz
  114.4 15.2 %shard_map.80 = f32[16,48,128]{2,1,0:T(8,128)} custom-call(f32[576]{0:T(1024)} %reshape.412.weights, f32[3,17,48,128]{3,2,1,0:T(8,128)} %pad.13.base, f32[3,17,48,128]{3,2,1,0:T(8,128)} %pad.14.up_y, f32[3,17,48,128]{3,2,1,0:T(8,128)} %pad.15.up_z, f32[3,17,48,128]{3,2,1,0:T(8,128)} %pad.16.up_yz), custom_call_target="tpu_custom_call" | custom-call | tf_op jit(solution)/shard_map/pallas_call | solution.py:182
  129.6 1.1 fusion.47
  131.5 10.2 %shard_map.81 = (f32[2,3,44,128]{3,2,1,0:T(8,128)}, f32[2,3,44,128]{3,2,1,0:T(8,128)}) custom-call(f32[2,3,44,128]{3,2,1,0:T(8,128)} %get-tuple-element.69.low, f32[2,3,44,128]{3,2,1,0:T(8,128)} %get-tuple-element.68.high), custom_call_target="tpu_custom_call" | custom-call | tf_op jit(solution)/shard_map/pallas_call | solution.py:89
  141.7 1.1 maximum_maximum_fusion
  143.8 4.7 %shard_map.82 = (f32[2,16,3,128]{3,2,1,0:T(4,128)}, f32[2,16,3,128]{3,2,1,0:T(4,128)}) custom-call(f32[2,16,3,128]{3,2,1,0:T(4,128)} %get-tuple-element.65.low, f32[2,16,3,128]{3,2,1,0:T(4,128)} %get-tuple-element.64.high), custom_call_target="tpu_custom_call" | custom-call | tf_op jit(solution)/shard_map/pallas_call | solution.py:89
  148.5 1.7 fusion.17
  150.2 1.4 fusion.74
  151.6 33.7 %shard_map.83 = (f32[2,16,44,3]{3,2,1,0:T(8,128)}, f32[2,16,44,3]{3,2,1,0:T(8,128)}) custom-call(f32[2,16,44,3]{3,2,1,0:T(8,128)} %get-tuple-element.63.low, f32[2,16,44,3]{3,2,1,0:T(8,128)} %get-tuple-element.62.high), custom_call_target="tpu_custom_call" | custom-call | tf_op jit(solution)/shard_map/pallas_call | solution.py:89
  185.3 4.8 %fusion.30 = f32[2,16,44,128]{3,2,1,0:T(8,128)S(1)} fusion(f32[2,16,44,128]{3,2,1,0:T(8,128)S(1)} %fusion.17, f32[2,16,44,3]{3,2,1,0:T(8,128)} %get-tuple-element.25, f32[2,16,44,3]{3,2,1,0:T(8,128)} %get-tuple-element.24), kind=kLoop, calls=%fused_computation.55 | loop fusion | flops 3063808 | bytes 1475584 | tf_op jit(solution)/shard_map/add | solution.py:196
  190.3 0.8 copy.66
  191.2 0.8 copy.67
  (43 shorter events, 7.7 us)
Async XLA Ops:
  2.0 18.4 %all-to-all-start = ((f32[16,3,512]{2,1,0:T(4,128)}), f32[16,3,512]{2,1,0:T(4,128)S(1)}, u32[]{:S(2)}, u32[]{:S(2)}) async-start(f32[16,3,512]{2,1,0:T(4,128)} %broadcast_in_dim.219), calls=%async_computation | async-start | bytes 262144 | tf_op jit(solution)/shard_map/all_to_all | solution.py:231
  36.2 6.3 %copy-start.1 = (f32[3,1,45,129]{3,2,1,0:T(8,128)S(1)}, f32[3,1,45,129]{3,2,1,0:T(8,128)}, u32[]{:S(2)}) copy-start(f32[3,1,45,129]{3,2,1,0:T(8,128)} %get-tuple-element.14) | copy-start | bytes 208984
  36.3 6.3 %copy-start.2 = (f32[3,1,45,129]{3,2,1,0:T(8,128)S(1)}, f32[3,1,45,129]{3,2,1,0:T(8,128)}, u32[]{:S(2)}) copy-start(f32[3,1,45,129]{3,2,1,0:T(8,128)} %get-tuple-element.15) | copy-start | bytes 208984
  42.5 0.8 copy-start.3
  42.5 0.8 copy-start.4
  114.4 15.2 %copy-start = (f32[16,44,128]{2,0,1:T(8,128)S(1)}, f32[16,44,128]{2,0,1:T(8,128)}, u32[]{:S(2)}) copy-start(f32[16,44,128]{2,0,1:T(8,128)} %param.10) | copy-start | bytes 1081348

commit v5 on v4

--- a/solution.py
+++ b/solution.py
@@ -106,7 +106,13 @@
         length = shard.shape[dim]
         last = lax.slice_in_dim(shard, length - width, length, axis=dim)
         initial = lax.slice_in_dim(shard, 0, width, axis=dim)
-        before, after = exchange(initial, last, axis)
+        moved = jnp.moveaxis(initial, dim, 0).shape
+        rows = (-1, moved[-1])
+        before, after = exchange(
+            jnp.moveaxis(initial, dim, 0).reshape(rows), jnp.moveaxis(last, dim, 0).reshape(rows), axis
+        )
+        before = jnp.moveaxis(before.reshape(moved), 0, dim)
+        after = jnp.moveaxis(after.reshape(moved), 0, dim)
         shard = jnp.concatenate([before, shard, after], axis=dim)
     return shard
 

time: 194 us -> 127 us (0.65)
  the two profiles are of different devices: /device:TPU:29 before, /device:TPU:224 now
where the time goes in v5:
time: 127 us; the launch traced here: 126 us
  Pallas kernels  64.8 us (51%)
  local copies, waits for them, and re-layouts  34.7 us (27%)
  other arithmetic  17.7 us (14%)
  starting transfers between devices  7.74 us (6%)
    pallas_call x6, Pallas kernels, exchange(): pl.pallas_call(kernel, out_shape=(slab, slab), in_specs=[vmem, vmem], out...  49.6 us
    pallas_call x1, Pallas kernels, element_energy(): pl.pallas_call(kernel, out_shape=jax.ShapeDtypeStruct((count_x, rows, cou...  15.2 us
    all_to_all x1, starting transfers between devices, local(): gathered = lax.all_to_all(spread, 'gz', 0, 0, tiled=True)  7.74 us
    unnamed x8, local copies, waits for them, and re-layouts  4.81 us
    pad x4, local copies, waits for them, and re-layouts, element_energy(): jnp.pad(nodes[:, :, dy:dy + count_y, dz:dz + count_z], pad)  4.56 us
    add x1, other arithmetic, recover(): summed = summed + basis[None] * corner_vals[:, corner][:, None, None, None]  4.24 us
    add x3, other arithmetic, smooth(): summed = term_value if summed is None else summed + term_value  3.29 us
    mul x2, other arithmetic, recover(): along_x[:, None, None] * along_y[None, :, None] * along_z[None, None, :]  3.09 us
  transfers between devices with their start and end apart: 1, of which 0 were waited for; matrix products, arithmetic and copies ran while one was open for 8% of the time, Pallas kernels for 0%

profile of v5, /device:TPU:224, one launch (start us, length us, event | category | flops | bytes accessed | tf_op | source)
XLA Modules:
  0.0 125.9 jit_solution(348451761163266925)
XLA Ops:
  0.6 1.4 %broadcast_in_dim.219 = f32[16,3,512]{2,1,0:T(4,128)} broadcast(f32[3,512]{1,0:T(4,128)} %param.8), dimensions={1,2} | broadcast | bytes 104448 | tf_op jit(solution)/shard_map/broadcast_in_dim | solution.py:236
  2.0 7.7 %all-to-all-start = ((f32[16,3,512]{2,1,0:T(4,128)}), f32[16,3,512]{2,1,0:T(4,128)S(1)}, u32[]{:S(2)}, u32[]{:S(2)}) async-start(f32[16,3,512]{2,1,0:T(4,128)} %broadcast_in_dim.219), calls=%async_computation | async-start | bytes 262144 | tf_op jit(solution)/shard_map/all_to_all | solution.py:237
  10.6 2.3 %copy.130 = f32[3,17,45,1]{3,2,1,0:T(8,128)} copy(f32[3,17,45,1]{2,3,1,0:T(1,128)} %param.7) | data formatting | bytes 18360 | tf_op args[1]
  13.7 1.5 %gather_fusion = f32[24]{0:T(128)S(1)} fusion(f32[24,24]{1,0:T(8,128)} %param.11, s32[24]{0:T(128)S(1)} %or_bitcast_fusion), kind=kCustom, calls=%fused_computation | custom fusion | bytes 384 | tf_op jit(solution)/shard_map/jit(diagonal)/cond/branch_0_fun/gather | solution.py:184
  16.9 3.0 %broadcast_multiply_fusion.1 = (f32[17,45,129]{2,1,0:T(8,128)S(1)}, f32[17,45,129]{2,1,0:T(8,128)}, f32[17,45,129]{2,1,0:T(8,128)}, f32[17,45,129]{2,1,0:T(8,128...) fusion(f32[17,45]{1,0:T(8,128)S(1)} %get-tuple-element.88, ...), kind=kLoop, calls=%fused_computation.86 | loop fusion | flops 789480 | bytes 3171192 | tf_op jit(solution)/shard_map/mul | solution.py:130
  20.5 4.2 %fusion.8 = f32[3,17,45,129]{3,2,1,0:T(8,128)S(1)} fusion(f32[3,17,45,1]{3,2,1,0:T(8,128)} %copy.130, f32[3,17,45,128]{3,2,1,0:T(8,128)} %param.6, f32[3]{0:T(128)S(1)} %get-tuple-element.43, f32[17,45,129]{2,1,0:T(8,128)} %get-tuple-element.79, f32[3]{0:T(128)S(1)} %get-tuple-element.44, f32[17,45,129]{2,1,0:T(8,128)S(1)} %get-tuple-element.78, ...), kind=kLoop, calls=%fused_computation.13 | loop fusion | flops 5032935 | bytes 5526456 | tf_op jit(solution)/shard_map/add | solution.py:131
  26.1 10.1 %shard_map.77 = (f32[135,129]{1,0:T(8,128)}, f32[135,129]{1,0:T(8,128)}) custom-call(f32[135,129]{1,0:T(8,128)} %reshape_transpose.18.low, f32[135,129]{1,0:T(8,128)} %reshape_transpose.19.high), custom_call_target="tpu_custom_call" | custom-call | tf_op jit(solution)/shard_map/pallas_call | solution.py:89
  36.2 0.9 transpose_reshape.14
  37.2 0.9 transpose_reshape.15
  39.7 6.8 %shard_map.78 = (f32[57,129]{1,0:T(8,128)}, f32[57,129]{1,0:T(8,128)}) custom-call(f32[57,129]{1,0:T(8,128)} %reshape_transpose.20.low, f32[57,129]{1,0:T(8,128)} %reshape_transpose.21.high), custom_call_target="tpu_custom_call" | custom-call | tf_op jit(solution)/shard_map/pallas_call | solution.py:89
  46.5 0.9 transpose_reshape.16
  47.4 0.9 transpose_reshape.17
  52.4 8.2 %shard_map.79 = (f32[51,45]{1,0:T(8,128)}, f32[51,45]{1,0:T(8,128)}) custom-call(f32[51,45]{1,0:T(8,128)} %reshape_transpose.22.low, f32[51,45]{1,0:T(8,128)} %reshape_transpose.23.high), custom_call_target="tpu_custom_call" | custom-call | tf_op jit(solution)/shard_map/pallas_call | solution.py:89
  62.2 1.3 %multiply_add_fusion = f32[3,17,45,129]{3,2,1,0:T(8,128)S(1)} fusion(f32[3,17,45]{2,1,0:T(8,128)S(1)} %broadcast_in_dim.244, f32[3,17,45]{2,1,0:T(8,128)S(1)} %broadcast_in_dim.241, f32[129]{0:T(256)S(1)} %and_select_fusion.16, pred[129]{0:T(512)(128)(4,1)S(1)} %get-tuple-element.100, pred[129]{0:T(512)(128)(4,1)S(1)} %get-tuple-element.101, ...), kind=kLoop, calls=%fused_computation.14 | loop fusion | flops 3552660 | bytes 2440476 | tf_op jit(solution)/shard_map/add | solution.py:147
  63.5 0.9 fusion.73
  64.3 1.1 pad.13.base
  65.5 1.1 pad.14.up_y
  66.6 1.1 pad.15.up_z
  67.8 1.1 pad.16.up_yz
  68.9 15.2 %shard_map.80 = f32[16,48,128]{2,1,0:T(8,128)} custom-call(f32[576]{0:T(1024)} %reshape.450.weights, f32[3,17,48,128]{3,2,1,0:T(8,128)} %pad.13.base, f32[3,17,48,128]{3,2,1,0:T(8,128)} %pad.14.up_y, f32[3,17,48,128]{3,2,1,0:T(8,128)} %pad.15.up_z, f32[3,17,48,128]{3,2,1,0:T(8,128)} %pad.16.up_yz), custom_call_target="tpu_custom_call" | custom-call | tf_op jit(solution)/shard_map/pallas_call | solution.py:188
  84.1 1.1 fusion.47
  86.7 10.1 %shard_map.81 = (f32[264,128]{1,0:T(8,128)}, f32[264,128]{1,0:T(8,128)}) custom-call(f32[264,128]{1,0:T(8,128)} %reshape.451.low, f32[264,128]{1,0:T(8,128)} %reshape.452.high), custom_call_target="tpu_custom_call" | custom-call | tf_op jit(solution)/shard_map/pallas_call | solution.py:89
  96.7 0.9 reshape.454
  97.7 0.9 reshape.453
  100.4 5.6 %shard_map.82 = (f32[96,128]{1,0:T(8,128)}, f32[96,128]{1,0:T(8,128)}) custom-call(f32[96,128]{1,0:T(8,128)} %bitcast.87, f32[96,128]{1,0:T(8,128)} %bitcast.89), custom_call_target="tpu_custom_call" | custom-call | tf_op jit(solution)/shard_map/pallas_call | solution.py:89
  108.6 1.0 copy.143
  109.5 1.0 copy.144
  110.5 8.8 %shard_map.83 = (f32[96,44]{1,0:T(8,128)}, f32[96,44]{1,0:T(8,128)}) custom-call(f32[96,44]{1,0:T(8,128)} %bitcast.88, f32[96,44]{1,0:T(8,128)} %bitcast.90), custom_call_target="tpu_custom_call" | custom-call | tf_op jit(solution)/shard_map/pallas_call | solution.py:89
  119.3 1.2 copy.145
  120.5 1.2 copy.146
  121.7 2.3 %fusion.30 = f32[2,16,44,128]{3,2,1,0:T(8,128)S(1)} fusion(f32[2,16,44,128]{3,2,1,0:T(8,128)S(1)} %fusion.17, f32[2,16,44,3]{3,2,1,0:T(8,128)S(1)} %bitcast.71, f32[2,16,44,3]{3,2,1,0:T(8,128)S(1)} %bitcast.70), kind=kLoop, calls=%fused_computation.57 | loop fusion | flops 3063808 | bytes 1475584 | tf_op jit(solution)/shard_map/add | solution.py:202
  124.3 0.8 copy.148
  (61 shorter events, 19.1 us)
Async XLA Ops:
  2.0 18.0 %all-to-all-start = ((f32[16,3,512]{2,1,0:T(4,128)}), f32[16,3,512]{2,1,0:T(4,128)S(1)}, u32[]{:S(2)}, u32[]{:S(2)}) async-start(f32[16,3,512]{2,1,0:T(4,128)} %broadcast_in_dim.219), calls=%async_computation | async-start | bytes 262144 | tf_op jit(solution)/shard_map/all_to_all | solution.py:237
  68.9 15.2 %copy-start = (f32[16,44,128]{2,0,1:T(8,128)S(1)}, f32[16,44,128]{2,0,1:T(8,128)}, u32[]{:S(2)}) copy-start(f32[16,44,128]{2,0,1:T(8,128)} %param.10) | copy-start | bytes 1081348

commit v6 on v5

--- a/solution.py
+++ b/solution.py
@@ -101,6 +101,72 @@
     )(low, high)
 
 
+def gather_kernel(shard, out, landed, send_sem, recv_sem, *, axis, count):
+    me = lax.axis_index(axis)
+    mesh_ids = pl.DeviceIdType.MESH
+    barrier = pltpu.get_barrier_semaphore()
+    for peer in range(count):
+
+        @pl.when(peer != me)
+        def _():
+            pl.semaphore_signal(barrier, 1, device_id={axis: peer}, device_id_type=mesh_ids)
+
+    pl.semaphore_wait(barrier, count - 1)
+    copies = []
+    for peer in range(count):
+        copies.append(
+            pltpu.make_async_remote_copy(
+                src_ref=shard,
+                dst_ref=landed.at[me],
+                send_sem=send_sem.at[peer],
+                recv_sem=recv_sem.at[me],
+                device_id={axis: peer},
+                device_id_type=mesh_ids,
+            )
+        )
+
+        @pl.when(peer != me)
+        def _():
+            copies[peer].start()
+
+    for peer in range(count):
+        incoming = pltpu.make_async_remote_copy(
+            src_ref=shard,
+            dst_ref=landed.at[peer],
+            send_sem=send_sem.at[peer],
+            recv_sem=recv_sem.at[peer],
+            device_id={axis: peer},
+            device_id_type=mesh_ids,
+        )
+
+        @pl.when(peer != me)
+        def _():
+            copies[peer].wait_send()
+            incoming.wait_recv()
+            out[peer] = landed[peer]
+
+    out[me] = shard[...]
+
+
+def gather_peers(shard, axis):
+    count = lax.axis_size(axis)
+    kernel = functools.partial(gather_kernel, axis=axis, count=count)
+    vmem = pl.BlockSpec(memory_space=pltpu.VMEM)
+    stacked = (count,) + shard.shape
+    return pl.pallas_call(
+        kernel,
+        out_shape=jax.ShapeDtypeStruct(stacked, shard.dtype),
+        in_specs=[vmem],
+        out_specs=vmem,
+        scratch_shapes=[
+            pltpu.VMEM(stacked, shard.dtype),
+            pltpu.SemaphoreType.DMA((count,)),
+            pltpu.SemaphoreType.DMA((count,)),
+        ],
+        compiler_params=pltpu.CompilerParams(collective_id=100, has_side_effects=True),
+    )(shard)
+
+
 def with_halo(shard, sides, width):
     for axis, dim in sides:
         length = shard.shape[dim]
@@ -147,8 +213,8 @@
     return own_rows * factor + rim_part * 0.5
 
 
-def energy_kernel(weights, base, up_y, up_z, up_yz, out, *, count_x, chunks):
-    sources = (base, up_z, up_y, up_yz)
+def energy_kernel(weights, shifted, out, *, count_x, chunks):
+    sources = (shifted.at[0], shifted.at[2], shifted.at[1], shifted.at[3])
 
     def row(i, carry):
         for first in chunks:
@@ -177,10 +243,12 @@
     count_z = nodes.shape[3] - 1
     rows = -(-count_y // 8) * 8
     pad = ((0, 0), (0, 0), (0, rows - count_y), (0, 0))
-    shifted = [
-        jnp.pad(nodes[:, :, dy : dy + count_y, dz : dz + count_z], pad)
-        for dy, dz in ((0, 0), (1, 0), (0, 1), (1, 1))
-    ]
+    shifted = jnp.stack(
+        [
+            jnp.pad(nodes[:, :, dy : dy + count_y, dz : dz + count_z], pad)
+            for dy, dz in ((0, 0), (1, 0), (0, 1), (1, 1))
+        ]
+    )
     upper = jnp.triu(stiffness + stiffness.T, 1) + jnp.diag(jnp.diagonal(stiffness))
     weights = upper.reshape(-1)
     kernel = functools.partial(energy_kernel, count_x=count_x, chunks=tuple(range(0, rows, 8)))
@@ -188,9 +256,9 @@
     energy = pl.pallas_call(
         kernel,
         out_shape=jax.ShapeDtypeStruct((count_x, rows, count_z), jnp.float32),
-        in_specs=[pl.BlockSpec(memory_space=pltpu.SMEM)] + [vmem] * 4,
+        in_specs=[pl.BlockSpec(memory_space=pltpu.SMEM), vmem],
         out_specs=vmem,
-    )(weights, *shifted)
+    )(weights, shifted)
     return energy[:, :count_y, :]
 
 
@@ -232,9 +300,7 @@
     )
     sides = (("gx", 1), ("gy", 2), ("gz", 3))
     wanted = corner_dofs.reshape(8)
-    parts = lax.axis_size("gz")
-    spread = jnp.broadcast_to(coarse_solution[None], (parts,) + coarse_solution.shape)
-    gathered = lax.all_to_all(spread, "gz", 0, 0, tiled=True)
+    gathered = gather_peers(coarse_solution, "gz")
     columns = gathered.transpose(1, 0, 2).reshape(coarse_solution.shape[0], -1)
     matches = wanted[:, None] == jnp.arange(columns.shape[1], dtype=jnp.int32)[None, :]
     corner_vals = jnp.sum(jnp.where(matches[None], columns[:, None, :], 0.0), axis=2)

time: 127 us -> 127 us (level)
  Pallas kernels: 64.8 us -> 75.3 us
  starting transfers between devices: 7.74 us -> 0 us
  local copies, waits for them, and re-layouts: 34.7 us -> 27 us
  other arithmetic: 17.7 us -> 23 us
    pallas_call x0 -> x1, Pallas kernels: none -> 10.7 us  [gather_peers(): pl.pallas_call(kernel, out_shape=jax.ShapeDtypeStruct(stacked, shard.dtyp...]
    all_to_all x1 -> x0, starting transfers between devices: 7.74 us -> none  [local(): gathered = lax.all_to_all(spread, 'gz', 0, 0, tiled=True)]
    pad x4 -> x0, local copies, waits for them, and re-layouts: 4.56 us -> none  [element_energy(): jnp.pad(nodes[:, :, dy:dy + count_y, dz:dz + count_z], pad)]
    another operation x0 -> x1, other arithmetic: none -> 2.67 us  [element_energy(): jnp.stack([jnp.pad(nodes[:, :, dy:dy + count_y, dz:dz + count_z], pad) fo...]
    add x3, other arithmetic: 2.78 us -> 4.49 us  [average_rows(): return own_rows * factor + rim_part * 0.5]
    concatenate x2, other arithmetic: 0.61 us -> 2.2 us  [with_halo(): shard = jnp.concatenate([before, shard, after], axis=dim)]
    unnamed x8 -> x14, local copies, waits for them, and re-layouts: 4.81 us -> 3.39 us
    broadcast_in_dim x1 -> x0, local copies, waits for them, and re-layouts: 1.37 us -> none  [local(): jnp.broadcast_to(coarse_solution[None], (parts,) + coarse_solution.shape)]
  transfers between devices with their start and end apart: 1 -> 0, of which waited for: 0 -> 0; matrix products, arithmetic and copies ran while one was open for 8% -> 0% of each run, Pallas kernels for 0% -> 0%
where the time goes in v6:
time: 127 us; the launch traced here: 126 us
  Pallas kernels  75.3 us (59%)
  local copies, waits for them, and re-layouts  27 us (21%)
  other arithmetic  23 us (18%)
    pallas_call x6, Pallas kernels, exchange(): pl.pallas_call(kernel, out_shape=(slab, slab), in_specs=[vmem, vmem], out...  49.6 us
    pallas_call x1, Pallas kernels, element_energy(): pl.pallas_call(kernel, out_shape=jax.ShapeDtypeStruct((count_x, rows, cou...  15 us
    pallas_call x1, Pallas kernels, gather_peers(): pl.pallas_call(kernel, out_shape=jax.ShapeDtypeStruct(stacked, shard.dtyp...  10.7 us
    add x3, other arithmetic, average_rows(): return own_rows * factor + rim_part * 0.5  4.49 us
    add x1, other arithmetic, recover(): summed = summed + basis[None] * corner_vals[:, corner][:, None, None, None]  4.21 us
    unnamed x14, local copies, waits for them, and re-layouts  3.39 us
    add x3, other arithmetic, smooth(): summed = term_value if summed is None else summed + term_value  3.29 us
    mul x2, other arithmetic, recover(): along_x[:, None, None] * along_y[None, :, None] * along_z[None, None, :]  3.03 us

profile of v6, /device:TPU:224, one launch (start us, length us, event | category | flops | bytes accessed | tf_op | source)
XLA Modules:
  0.0 126.3 jit_solution(18026471060522740822)
XLA Ops:
  0.8 3.0 %broadcast_multiply_fusion.1 = (f32[17,45,129]{2,1,0:T(8,128)S(1)}, f32[17,45,129]{2,1,0:T(8,128)}, f32[17,45,129]{2,1,0:T(8,128)}, f32[17,45,129]{2,1,0:T(8,128...) fusion(f32[17,45]{1,0:T(8,128)S(1)} %get-tuple-element.86, ...), kind=kLoop, calls=%fused_computation.91 | loop fusion | flops 789480 | bytes 3171192 | tf_op jit(solution)/shard_map/mul | solution.py:196
  3.7 10.7 %shard_map.77 = f32[16,3,512]{2,1,0:T(4,128)} custom-call(f32[3,512]{1,0:T(4,128)} %shard.1), custom_call_target="tpu_custom_call" | custom-call | tf_op jit(solution)/shard_map/pallas_call | solution.py:156
  14.5 1.1 select_reduce_fusion
  15.9 1.6 %copy.106 = f32[3,17,45,1]{3,2,1,0:T(8,128)} copy(f32[3,17,45,1]{2,3,1,0:T(1,128)S(1)} %copy-done.2) | data formatting | bytes 18360 | tf_op args[1]
  17.5 4.2 %fusion.8 = f32[3,17,45,129]{3,2,1,0:T(8,128)S(1)} fusion(f32[3,17,45,1]{3,2,1,0:T(8,128)} %copy.106, f32[3,17,45,128]{3,2,1,0:T(8,128)} %param.6, f32[3]{0:T(128)S(1)} %get-tuple-element.41, f32[17,45,129]{2,1,0:T(8,128)} %get-tuple-element.77, f32[3]{0:T(128)S(1)} %get-tuple-element.42, f32[17,45,129]{2,1,0:T(8,128)S(1)} %get-tuple-element.76, ...), kind=kLoop, calls=%fused_computation.14 | loop fusion | flops 5032935 | bytes 5526456 | tf_op jit(solution)/shard_map/add | solution.py:197
  23.1 10.1 %shard_map.78 = (f32[135,129]{1,0:T(8,128)}, f32[135,129]{1,0:T(8,128)}) custom-call(f32[135,129]{1,0:T(8,128)} %reshape_transpose.18.low, f32[135,129]{1,0:T(8,128)} %reshape_transpose.19.high), custom_call_target="tpu_custom_call" | custom-call | tf_op jit(solution)/shard_map/pallas_call | solution.py:89
  33.3 0.9 transpose_reshape.14
  34.2 0.9 transpose_reshape.15
  36.7 6.8 %shard_map.79 = (f32[57,129]{1,0:T(8,128)}, f32[57,129]{1,0:T(8,128)}) custom-call(f32[57,129]{1,0:T(8,128)} %reshape_transpose.20.low, f32[57,129]{1,0:T(8,128)} %reshape_transpose.21.high), custom_call_target="tpu_custom_call" | custom-call | tf_op jit(solution)/shard_map/pallas_call | solution.py:89
  43.5 0.9 transpose_reshape.16
  44.4 0.9 transpose_reshape.17
  45.4 2.1 %pad_maximum_fusion.1 = f32[3,19,47,129]{3,2,1,0:T(8,128)} fusion(f32[3,19,1,129]{3,2,1,0:T(1,128)S(1)} %transpose_reshape.17, f32[3,1,45,129]{3,2,1,0:T(8,128)S(1)} %bitcast.85, f32[3,17,45,129]{3,2,1,0:T(8,128)S(1)} %fusion.8, f32[3,1,45,129]{3,2,1,0:T(8,128)S(1)} %bitcast.82, f32[3,19,1,129]{3,2,1,0:T(1,128)S(1)} %transpose_reshape.16), kind=kLoop, calls=%fused_computation.2 | loop fusion | flops 1382364 | bytes 2764728 | tf_op jit(solution)/shard_map/concatenate | solution.py:182
  47.5 2.4 %fusion.1 = f32[3,17,47,129]{3,2,1,0:T(8,128)S(1)} fusion(f32[3,19,47,129]{3,2,1,0:T(8,128)} %pad_maximum_fusion.1, f32[3,47,129]{2,1,0:T(8,128)S(1)} %get-tuple-element.49, f32[3,47,129]{2,1,0:T(8,128)S(1)} %get-tuple-element.48, f32[17]{0:T(128)S(1)} %and_select_fusion.20, pred[17]{0:T(512)(128)(4,1)S(1)} %get-tuple-element.94, ...), kind=kLoop, calls=%fused_computation.6 | loop fusion | flops 1855278 | bytes 2619318 | tf_op jit(solution)/shard_map/add | solution.py:213
  52.8 8.2 %shard_map.80 = (f32[51,45]{1,0:T(8,128)}, f32[51,45]{1,0:T(8,128)}) custom-call(f32[51,45]{1,0:T(8,128)} %reshape_transpose.22.low, f32[51,45]{1,0:T(8,128)} %reshape_transpose.23.high), custom_call_target="tpu_custom_call" | custom-call | tf_op jit(solution)/shard_map/pallas_call | solution.py:89
  62.5 1.3 %multiply_add_fusion = f32[3,17,45,129]{3,2,1,0:T(8,128)S(1)} fusion(f32[3,17,45]{2,1,0:T(8,128)S(1)} %broadcast_in_dim.237, f32[3,17,45]{2,1,0:T(8,128)S(1)} %broadcast_in_dim.234, f32[129]{0:T(256)S(1)} %and_select_fusion.16, pred[129]{0:T(512)(128)(4,1)S(1)} %get-tuple-element.98, pred[129]{0:T(512)(128)(4,1)S(1)} %get-tuple-element.99, ...), kind=kLoop, calls=%fused_computation.15 | loop fusion | flops 3552660 | bytes 2440476 | tf_op jit(solution)/shard_map/add | solution.py:213
  63.9 0.9 fusion.73
  65.1 2.7 %pad_maximum_fusion.shifted = f32[4,3,17,48,128]{4,3,2,1,0:T(8,128)} fusion(f32[1,3,17,48,128]{4,3,2,1,0:T(8,128)S(1)} %pad_bitcast_fusion, f32[1,3,17,48,128]{4,3,2,1,0:T(8,128)S(1)} %pad_bitcast_fusion.1, f32[1,3,17,48,128]{4,3,2,1,0:T(8,128)S(1)} %pad_bitcast_fusion.2, f32[1,3,17,48,128]{4,3,2,1,0:T(8,128)S(1)} %pad_bitcast_fusion.3), kind=kLoop, calls=%fused_computation.1 | loop fusion | flops 3760128 | bytes 10027008 | tf_op jit(solution)/shard_map/stack | solution.py:246
  69.4 15.0 %shard_map.81 = f32[16,48,128]{2,1,0:T(8,128)} custom-call(f32[576]{0:T(1024)} %reshape.449.weights, f32[4,3,17,48,128]{4,3,2,1,0:T(8,128)} %pad_maximum_fusion.shifted), custom_call_target="tpu_custom_call" | custom-call | tf_op jit(solution)/shard_map/pallas_call | solution.py:256
  84.4 1.1 fusion.47
  87.0 10.1 %shard_map.82 = (f32[264,128]{1,0:T(8,128)}, f32[264,128]{1,0:T(8,128)}) custom-call(f32[264,128]{1,0:T(8,128)} %reshape.450.low, f32[264,128]{1,0:T(8,128)} %reshape.451.high), custom_call_target="tpu_custom_call" | custom-call | tf_op jit(solution)/shard_map/pallas_call | solution.py:89
  97.0 0.9 reshape.453
  98.0 0.9 reshape.452
  100.7 5.6 %shard_map.83 = (f32[96,128]{1,0:T(8,128)}, f32[96,128]{1,0:T(8,128)}) custom-call(f32[96,128]{1,0:T(8,128)} %bitcast.95, f32[96,128]{1,0:T(8,128)} %bitcast.97), custom_call_target="tpu_custom_call" | custom-call | tf_op jit(solution)/shard_map/pallas_call | solution.py:89
  106.2 0.8 copy.143
  108.9 1.0 copy.119
  109.8 1.0 copy.120
  110.8 8.8 %shard_map.84 = (f32[96,44]{1,0:T(8,128)}, f32[96,44]{1,0:T(8,128)}) custom-call(f32[96,44]{1,0:T(8,128)} %bitcast.96, f32[96,44]{1,0:T(8,128)} %bitcast.98), custom_call_target="tpu_custom_call" | custom-call | tf_op jit(solution)/shard_map/pallas_call | solution.py:89
  119.6 1.2 copy.121
  120.8 1.2 copy.122
  122.0 2.3 %fusion.30 = f32[2,16,44,128]{3,2,1,0:T(8,128)S(1)} fusion(f32[2,16,44,128]{3,2,1,0:T(8,128)S(1)} %fusion.17, f32[2,16,44,3]{3,2,1,0:T(8,128)S(1)} %bitcast.79, f32[2,16,44,3]{3,2,1,0:T(8,128)S(1)} %bitcast.78), kind=kLoop, calls=%fused_computation.62 | loop fusion | flops 3063808 | bytes 1475584 | tf_op jit(solution)/shard_map/add | solution.py:270
  124.6 0.8 copy.124
  125.5 0.8 copy.125
  (66 shorter events, 15.1 us)
Async XLA Ops:
  0.7 13.7 %copy-start.3 = (s32[1,1,1,8]{3,2,1,0:T(1,128)S(1)}, s32[1,1,1,8]{3,2,1,0:T(1,128)}, u32[]{:S(2)}) copy-start(s32[1,1,1,8]{3,2,1,0:T(1,128)} %param.9) | copy-start | bytes 100
  0.8 15.2 %copy-start.2 = (f32[3,17,45,1]{2,3,1,0:T(1,128)S(1)}, f32[3,17,45,1]{2,3,1,0:T(1,128)}, u32[]{:S(2)}) copy-start(f32[3,17,45,1]{2,3,1,0:T(1,128)} %param.7) | copy-start | bytes 27544
  65.1 2.7 %copy-start = (f32[24,24]{1,0:T(8,128)S(1)}, f32[24,24]{1,0:T(8,128)}, u32[]{:S(2)}) copy-start(f32[24,24]{1,0:T(8,128)} %param.11) | copy-start | bytes 6916
  69.4 15.0 %copy-start.1 = (f32[16,44,128]{2,0,1:T(8,128)S(1)}, f32[16,44,128]{2,0,1:T(8,128)}, u32[]{:S(2)}) copy-start(f32[16,44,128]{2,0,1:T(8,128)} %param.10) | copy-start | bytes 1081348

commit v7 on v6

--- a/solution.py
+++ b/solution.py
@@ -1,4 +1,5 @@
 import functools
+import math
 
 import jax
 import jax.numpy as jnp
@@ -172,13 +173,17 @@
         length = shard.shape[dim]
         last = lax.slice_in_dim(shard, length - width, length, axis=dim)
         initial = lax.slice_in_dim(shard, 0, width, axis=dim)
-        moved = jnp.moveaxis(initial, dim, 0).shape
-        rows = (-1, moved[-1])
-        before, after = exchange(
-            jnp.moveaxis(initial, dim, 0).reshape(rows), jnp.moveaxis(last, dim, 0).reshape(rows), axis
-        )
-        before = jnp.moveaxis(before.reshape(moved), 0, dim)
-        after = jnp.moveaxis(after.reshape(moved), 0, dim)
+        tiled = math.prod(initial.shape[:-2]) * -(-initial.shape[-2] // 8) * 8 * -(-initial.shape[-1] // 128) * 128
+        if tiled <= 3 * initial.size:
+            before, after = exchange(initial, last, axis)
+        else:
+            moved = jnp.moveaxis(initial, dim, 0).shape
+            rows = (-1, moved[-1])
+            before, after = exchange(
+                jnp.moveaxis(initial, dim, 0).reshape(rows), jnp.moveaxis(last, dim, 0).reshape(rows), axis
+            )
+            before = jnp.moveaxis(before.reshape(moved), 0, dim)
+            after = jnp.moveaxis(after.reshape(moved), 0, dim)
         shard = jnp.concatenate([before, shard, after], axis=dim)
     return shard
 

time: 127 us -> 124 us (0.976)
  local copies, waits for them, and re-layouts: 27 us -> 19 us
  other arithmetic: 23 us -> 27.3 us
    reshape x4 -> x1, local copies, waits for them, and re-layouts: 2.97 us -> 1.2 us  [with_halo(): after = jnp.moveaxis(after.reshape(moved), 0, dim)]
    reshape x4 -> x1, local copies, waits for them, and re-layouts: 2.96 us -> 1.2 us  [with_halo(): before = jnp.moveaxis(before.reshape(moved), 0, dim)]
    slice x2 -> x3, local copies, waits for them, and re-layouts: 0.74 us -> 2.13 us  [with_halo(): last = lax.slice_in_dim(shard, length - width, length, axis=dim)]
    reshape x2 -> x0, local copies, waits for them, and re-layouts: 1.33 us -> none  [the longest x1 0.67 us: with_halo(): jnp.moveaxis(initial, dim, 0).reshape(rows)]
    unnamed x14 -> x18, local copies, waits for them, and re-layouts: 3.39 us -> 3.4 us
where the time goes in v7:
time: 124 us; the launch traced here: 123 us
  Pallas kernels  75.8 us (61%)
  other arithmetic  27.3 us (22%)
  local copies, waits for them, and re-layouts  19 us (15%)
    pallas_call x6, Pallas kernels, exchange(): pl.pallas_call(kernel, out_shape=(slab, slab), in_specs=[vmem, vmem], out...  50.1 us
    pallas_call x1, Pallas kernels, element_energy(): pl.pallas_call(kernel, out_shape=jax.ShapeDtypeStruct((count_x, rows, cou...  15 us
    pallas_call x1, Pallas kernels, gather_peers(): pl.pallas_call(kernel, out_shape=jax.ShapeDtypeStruct(stacked, shard.dtyp...  10.7 us
    add x3, other arithmetic, average_rows(): return own_rows * factor + rim_part * 0.5  4.5 us
    add x3, other arithmetic, smooth(): summed = term_value if summed is None else summed + term_value  4.31 us
    add x1, other arithmetic, recover(): summed = summed + basis[None] * corner_vals[:, corner][:, None, None, None]  4.21 us
    unnamed x18, local copies, waits for them, and re-layouts  3.4 us
    concatenate x2, other arithmetic, with_halo(): shard = jnp.concatenate([before, shard, after], axis=dim)  3.18 us

profile of v7, /device:TPU:224, one launch (start us, length us, event | category | flops | bytes accessed | tf_op | source)
XLA Modules:
  0.0 123.0 jit_solution(12739342087432952503)
XLA Ops:
  0.8 3.0 %broadcast_multiply_fusion.1 = (f32[17,45,129]{2,1,0:T(8,128)S(1)}, f32[17,45,129]{2,1,0:T(8,128)}, f32[17,45,129]{2,1,0:T(8,128)}, f32[17,45,129]{2,1,0:T(8,128...) fusion(f32[17,45]{1,0:T(8,128)S(1)} %get-tuple-element.86, ...), kind=kLoop, calls=%fused_computation.91 | loop fusion | flops 789480 | bytes 3171192 | tf_op jit(solution)/shard_map/mul | solution.py:201
  3.7 10.7 %shard_map.77 = f32[16,3,512]{2,1,0:T(4,128)} custom-call(f32[3,512]{1,0:T(4,128)} %shard.1), custom_call_target="tpu_custom_call" | custom-call | tf_op jit(solution)/shard_map/pallas_call | solution.py:157
  14.5 1.1 select_reduce_fusion
  15.9 1.6 %copy.68 = f32[3,17,45,1]{3,2,1,0:T(8,128)} copy(f32[3,17,45,1]{2,3,1,0:T(1,128)S(1)} %copy-done.4) | data formatting | bytes 18360 | tf_op args[1]
  17.5 4.2 %fusion.8 = f32[3,17,45,129]{3,2,1,0:T(8,128)S(1)} fusion(f32[3,17,45,1]{3,2,1,0:T(8,128)} %copy.68, f32[3,17,45,128]{3,2,1,0:T(8,128)} %param.6, f32[3]{0:T(128)S(1)} %get-tuple-element.41, f32[17,45,129]{2,1,0:T(8,128)} %get-tuple-element.77, f32[3]{0:T(128)S(1)} %get-tuple-element.42, f32[17,45,129]{2,1,0:T(8,128)S(1)} %get-tuple-element.76, ...), kind=kLoop, calls=%fused_computation.14 | loop fusion | flops 5032935 | bytes 5526456 | tf_op jit(solution)/shard_map/add | solution.py:202
  22.5 10.3 %shard_map.78 = (f32[3,1,45,129]{3,2,1,0:T(8,128)}, f32[3,1,45,129]{3,2,1,0:T(8,128)}) custom-call(f32[3,1,45,129]{3,2,1,0:T(8,128)} %get-tuple-element.57.low, f32[3,1,45,129]{3,2,1,0:T(8,128)} %get-tuple-element.56.high), custom_call_target="tpu_custom_call" | custom-call | tf_op jit(solution)/shard_map/pallas_call | solution.py:90
  32.8 1.2 fusion.50
  35.3 6.8 %shard_map.79 = (f32[57,129]{1,0:T(8,128)}, f32[57,129]{1,0:T(8,128)}) custom-call(f32[57,129]{1,0:T(8,128)} %reshape_transpose.12.low, f32[57,129]{1,0:T(8,128)} %reshape_transpose.13.high), custom_call_target="tpu_custom_call" | custom-call | tf_op jit(solution)/shard_map/pallas_call | solution.py:90
  42.1 0.9 transpose_reshape.8
  43.0 0.9 transpose_reshape.9
  44.6 2.1 %pad_maximum_fusion.1 = f32[3,19,47,129]{3,2,1,0:T(8,128)} fusion(f32[3,19,1,129]{3,2,1,0:T(1,128)S(1)} %transpose_reshape.9, f32[3,1,45,129]{3,2,1,0:T(8,128)S(1)} %copy-done.3, f32[3,17,45,129]{3,2,1,0:T(8,128)S(1)} %fusion.8, f32[3,1,45,129]{3,2,1,0:T(8,128)S(1)} %copy-done.2, f32[3,19,1,129]{3,2,1,0:T(1,128)S(1)} %transpose_reshape.8), kind=kLoop, calls=%fused_computation.2 | loop fusion | flops 1382364 | bytes 2764728 | tf_op jit(solution)/shard_map/concatenate | solution.py:187
  46.7 2.4 %fusion.1 = f32[3,17,47,129]{3,2,1,0:T(8,128)S(1)} fusion(f32[3,19,47,129]{3,2,1,0:T(8,128)} %pad_maximum_fusion.1, f32[3,47,129]{2,1,0:T(8,128)} %get-tuple-element.49, f32[3,47,129]{2,1,0:T(8,128)S(1)} %get-tuple-element.48, f32[17]{0:T(128)S(1)} %and_select_fusion.20, pred[17]{0:T(512)(128)(4,1)S(1)} %get-tuple-element.94, ...), kind=kLoop, calls=%fused_computation.6 | loop fusion | flops 1855278 | bytes 2619318 | tf_op jit(solution)/shard_map/add | solution.py:218
  49.2 0.8 fusion
  52.0 8.2 %shard_map.80 = (f32[51,45]{1,0:T(8,128)}, f32[51,45]{1,0:T(8,128)}) custom-call(f32[51,45]{1,0:T(8,128)} %reshape_transpose.14.low, f32[51,45]{1,0:T(8,128)} %reshape_transpose.15.high), custom_call_target="tpu_custom_call" | custom-call | tf_op jit(solution)/shard_map/pallas_call | solution.py:90
  61.8 1.3 %multiply_add_fusion = f32[3,17,45,129]{3,2,1,0:T(8,128)S(1)} fusion(f32[3,17,45]{2,1,0:T(8,128)S(1)} %broadcast_in_dim.237, f32[3,17,45]{2,1,0:T(8,128)S(1)} %broadcast_in_dim.234, f32[129]{0:T(256)S(1)} %and_select_fusion.16, pred[129]{0:T(512)(128)(4,1)S(1)} %get-tuple-element.98, pred[129]{0:T(512)(128)(4,1)S(1)} %get-tuple-element.99, ...), kind=kLoop, calls=%fused_computation.15 | loop fusion | flops 3552660 | bytes 2440476 | tf_op jit(solution)/shard_map/add | solution.py:218
  63.1 0.9 fusion.71
  64.3 2.7 %pad_maximum_fusion.shifted = f32[4,3,17,48,128]{4,3,2,1,0:T(8,128)} fusion(f32[1,3,17,48,128]{4,3,2,1,0:T(8,128)S(1)} %pad_bitcast_fusion, f32[1,3,17,48,128]{4,3,2,1,0:T(8,128)S(1)} %pad_bitcast_fusion.1, f32[1,3,17,48,128]{4,3,2,1,0:T(8,128)S(1)} %pad_bitcast_fusion.2, f32[1,3,17,48,128]{4,3,2,1,0:T(8,128)S(1)} %pad_bitcast_fusion.3), kind=kLoop, calls=%fused_computation.1 | loop fusion | flops 3760128 | bytes 10027008 | tf_op jit(solution)/shard_map/stack | solution.py:251
  67.1 0.8 gather_fusion
  68.6 15.0 %shard_map.81 = f32[16,48,128]{2,1,0:T(8,128)} custom-call(f32[576]{0:T(1024)} %reshape.425.weights, f32[4,3,17,48,128]{4,3,2,1,0:T(8,128)} %pad_maximum_fusion.shifted), custom_call_target="tpu_custom_call" | custom-call | tf_op jit(solution)/shard_map/pallas_call | solution.py:261
  83.7 1.1 fusion.47
  85.5 10.3 %shard_map.82 = (f32[2,3,44,128]{3,2,1,0:T(8,128)}, f32[2,3,44,128]{3,2,1,0:T(8,128)}) custom-call(f32[2,3,44,128]{3,2,1,0:T(8,128)} %get-tuple-element.67.low, f32[2,3,44,128]{3,2,1,0:T(8,128)} %get-tuple-element.66.high), custom_call_target="tpu_custom_call" | custom-call | tf_op jit(solution)/shard_map/pallas_call | solution.py:90
  95.8 1.1 maximum_maximum_fusion
  97.9 5.7 %shard_map.83 = (f32[2,16,3,128]{3,2,1,0:T(4,128)}, f32[2,16,3,128]{3,2,1,0:T(4,128)}) custom-call(f32[2,16,3,128]{3,2,1,0:T(4,128)} %get-tuple-element.63.low, f32[2,16,3,128]{3,2,1,0:T(4,128)} %get-tuple-element.62.high), custom_call_target="tpu_custom_call" | custom-call | tf_op jit(solution)/shard_map/pallas_call | solution.py:90
  103.6 1.7 %fusion.17 = f32[2,16,44,128]{3,2,1,0:T(8,128)S(1)} fusion(f32[2,16,3,128]{3,2,1,0:T(4,128)} %get-tuple-element.23, f32[2,16,3,128]{3,2,1,0:T(4,128)} %get-tuple-element.22, f32[2,16,44,128]{3,2,1,0:T(8,128)S(1)} %fusion.13), kind=kLoop, calls=%fused_computation.49 | loop fusion | flops 3063808 | bytes 1540096 | tf_op jit(solution)/shard_map/add | solution.py:275
  105.6 1.0 copy.71
  106.5 1.0 copy.72
  107.5 8.8 %shard_map.84 = (f32[96,44]{1,0:T(8,128)}, f32[96,44]{1,0:T(8,128)}) custom-call(f32[96,44]{1,0:T(8,128)} %bitcast.59, f32[96,44]{1,0:T(8,128)} %bitcast.60), custom_call_target="tpu_custom_call" | custom-call | tf_op jit(solution)/shard_map/pallas_call | solution.py:90
  116.3 1.2 copy.73
  117.5 1.2 copy.74
  118.7 2.3 %fusion.30 = f32[2,16,44,128]{3,2,1,0:T(8,128)S(1)} fusion(f32[2,16,44,128]{3,2,1,0:T(8,128)S(1)} %fusion.17, f32[2,16,44,3]{3,2,1,0:T(8,128)S(1)} %bitcast.53, f32[2,16,44,3]{3,2,1,0:T(8,128)S(1)} %bitcast.52), kind=kLoop, calls=%fused_computation.62 | loop fusion | flops 3063808 | bytes 1475584 | tf_op jit(solution)/shard_map/add | solution.py:275
  121.3 0.8 copy.76
  122.2 0.8 copy.77
  (54 shorter events, 10.3 us)
Async XLA Ops:
  0.7 13.7 %copy-start.5 = (s32[1,1,1,8]{3,2,1,0:T(1,128)S(1)}, s32[1,1,1,8]{3,2,1,0:T(1,128)}, u32[]{:S(2)}) copy-start(s32[1,1,1,8]{3,2,1,0:T(1,128)} %param.9) | copy-start | bytes 100
  0.8 15.2 %copy-start.4 = (f32[3,17,45,1]{2,3,1,0:T(1,128)S(1)}, f32[3,17,45,1]{2,3,1,0:T(1,128)}, u32[]{:S(2)}) copy-start(f32[3,17,45,1]{2,3,1,0:T(1,128)} %param.7) | copy-start | bytes 27544
  32.8 11.1 %copy-start.2 = (f32[3,1,45,129]{3,2,1,0:T(8,128)S(1)}, f32[3,1,45,129]{3,2,1,0:T(8,128)}, u32[]{:S(2)}) copy-start(f32[3,1,45,129]{3,2,1,0:T(8,128)} %get-tuple-element.14) | copy-start | bytes 208984
  32.8 11.1 %copy-start.3 = (f32[3,1,45,129]{3,2,1,0:T(8,128)S(1)}, f32[3,1,45,129]{3,2,1,0:T(8,128)}, u32[]{:S(2)}) copy-start(f32[3,1,45,129]{3,2,1,0:T(8,128)} %get-tuple-element.15) | copy-start | bytes 208984
  64.3 2.7 %copy-start = (f32[24,24]{1,0:T(8,128)S(1)}, f32[24,24]{1,0:T(8,128)}, u32[]{:S(2)}) copy-start(f32[24,24]{1,0:T(8,128)} %param.11) | copy-start | bytes 6916
  68.6 15.0 %copy-start.1 = (f32[16,44,128]{2,0,1:T(8,128)S(1)}, f32[16,44,128]{2,0,1:T(8,128)}, u32[]{:S(2)}) copy-start(f32[16,44,128]{2,0,1:T(8,128)} %param.10) | copy-start | bytes 1081348

commit v8 on v7

--- a/solution.py
+++ b/solution.py
@@ -228,7 +228,7 @@
                 for corner in range(8):
                     shift_x = corner // 4
                     source = sources[corner % 4]
-                    vectors.append(source[component, i + shift_x, pl.ds(first, 8), :])
+                    vectors.append(source[component, i + shift_x, pl.ds(first, 16), :])
             total = None
             for a in range(24):
                 inner = weights[a * 24 + a] * vectors[a]
@@ -236,7 +236,7 @@
                     inner = inner + weights[a * 24 + b] * vectors[b]
                 term = vectors[a] * inner
                 total = term if total is None else total + term
-            out[i, pl.ds(first, 8), :] = total
+            out[i, pl.ds(first, 16), :] = total
         return carry
 
     lax.fori_loop(0, count_x, row, 0)
@@ -246,7 +246,7 @@
     count_x = nodes.shape[1] - 1
     count_y = nodes.shape[2] - 1
     count_z = nodes.shape[3] - 1
-    rows = -(-count_y // 8) * 8
+    rows = -(-count_y // 16) * 16
     pad = ((0, 0), (0, 0), (0, rows - count_y), (0, 0))
     shifted = jnp.stack(
         [
@@ -256,7 +256,7 @@
     )
     upper = jnp.triu(stiffness + stiffness.T, 1) + jnp.diag(jnp.diagonal(stiffness))
     weights = upper.reshape(-1)
-    kernel = functools.partial(energy_kernel, count_x=count_x, chunks=tuple(range(0, rows, 8)))
+    kernel = functools.partial(energy_kernel, count_x=count_x, chunks=tuple(range(0, rows, 16)))
     vmem = pl.BlockSpec(memory_space=pltpu.VMEM)
     energy = pl.pallas_call(
         kernel,

time: 124 us -> 125 us (level)
  Pallas kernels: 75.8 us -> 77.1 us
    pallas_call x1, Pallas kernels: 15 us -> 16.3 us  [element_energy(): pl.pallas_call(kernel, out_shape=jax.ShapeDtypeStruct((count_x, rows, cou...]
where the time goes in v8:
time: 125 us; the launch traced here: 124 us
  Pallas kernels  77.1 us (62%)
  other arithmetic  27.3 us (22%)
  local copies, waits for them, and re-layouts  19 us (15%)
    pallas_call x6, Pallas kernels, exchange(): pl.pallas_call(kernel, out_shape=(slab, slab), in_specs=[vmem, vmem], out...  50.1 us
    pallas_call x1, Pallas kernels, element_energy(): pl.pallas_call(kernel, out_shape=jax.ShapeDtypeStruct((count_x, rows, cou...  16.3 us
    pallas_call x1, Pallas kernels, gather_peers(): pl.pallas_call(kernel, out_shape=jax.ShapeDtypeStruct(stacked, shard.dtyp...  10.7 us
    add x3, other arithmetic, average_rows(): return own_rows * factor + rim_part * 0.5  4.5 us
    add x3, other arithmetic, smooth(): summed = term_value if summed is None else summed + term_value  4.31 us
    add x1, other arithmetic, recover(): summed = summed + basis[None] * corner_vals[:, corner][:, None, None, None]  4.21 us
    unnamed x18, local copies, waits for them, and re-layouts  3.4 us
    concatenate x2, other arithmetic, with_halo(): shard = jnp.concatenate([before, shard, after], axis=dim)  3.18 us

profile of v8, /device:TPU:224, one launch (start us, length us, event | category | flops | bytes accessed | tf_op | source)
XLA Modules:
  0.0 124.3 jit_solution(6383126350496617937)
XLA Ops:
  0.8 3.0 %broadcast_multiply_fusion.1 = (f32[17,45,129]{2,1,0:T(8,128)S(1)}, f32[17,45,129]{2,1,0:T(8,128)}, f32[17,45,129]{2,1,0:T(8,128)}, f32[17,45,129]{2,1,0:T(8,128...) fusion(f32[17,45]{1,0:T(8,128)S(1)} %get-tuple-element.86, ...), kind=kLoop, calls=%fused_computation.91 | loop fusion | flops 789480 | bytes 3171192 | tf_op jit(solution)/shard_map/mul | solution.py:201
  3.7 10.7 %shard_map.77 = f32[16,3,512]{2,1,0:T(4,128)} custom-call(f32[3,512]{1,0:T(4,128)} %shard.1), custom_call_target="tpu_custom_call" | custom-call | tf_op jit(solution)/shard_map/pallas_call | solution.py:157
  14.5 1.1 select_reduce_fusion
  15.9 1.6 %copy.68 = f32[3,17,45,1]{3,2,1,0:T(8,128)} copy(f32[3,17,45,1]{2,3,1,0:T(1,128)S(1)} %copy-done.4) | data formatting | bytes 18360 | tf_op args[1]
  17.5 4.2 %fusion.8 = f32[3,17,45,129]{3,2,1,0:T(8,128)S(1)} fusion(f32[3,17,45,1]{3,2,1,0:T(8,128)} %copy.68, f32[3,17,45,128]{3,2,1,0:T(8,128)} %param.6, f32[3]{0:T(128)S(1)} %get-tuple-element.41, f32[17,45,129]{2,1,0:T(8,128)} %get-tuple-element.77, f32[3]{0:T(128)S(1)} %get-tuple-element.42, f32[17,45,129]{2,1,0:T(8,128)S(1)} %get-tuple-element.76, ...), kind=kLoop, calls=%fused_computation.14 | loop fusion | flops 5032935 | bytes 5526456 | tf_op jit(solution)/shard_map/add | solution.py:202
  22.5 10.3 %shard_map.78 = (f32[3,1,45,129]{3,2,1,0:T(8,128)}, f32[3,1,45,129]{3,2,1,0:T(8,128)}) custom-call(f32[3,1,45,129]{3,2,1,0:T(8,128)} %get-tuple-element.57.low, f32[3,1,45,129]{3,2,1,0:T(8,128)} %get-tuple-element.56.high), custom_call_target="tpu_custom_call" | custom-call | tf_op jit(solution)/shard_map/pallas_call | solution.py:90
  32.8 1.2 fusion.50
  35.3 6.8 %shard_map.79 = (f32[57,129]{1,0:T(8,128)}, f32[57,129]{1,0:T(8,128)}) custom-call(f32[57,129]{1,0:T(8,128)} %reshape_transpose.12.low, f32[57,129]{1,0:T(8,128)} %reshape_transpose.13.high), custom_call_target="tpu_custom_call" | custom-call | tf_op jit(solution)/shard_map/pallas_call | solution.py:90
  42.1 0.9 transpose_reshape.8
  43.0 0.9 transpose_reshape.9
  44.6 2.1 %pad_maximum_fusion.1 = f32[3,19,47,129]{3,2,1,0:T(8,128)} fusion(f32[3,19,1,129]{3,2,1,0:T(1,128)S(1)} %transpose_reshape.9, f32[3,1,45,129]{3,2,1,0:T(8,128)S(1)} %copy-done.3, f32[3,17,45,129]{3,2,1,0:T(8,128)S(1)} %fusion.8, f32[3,1,45,129]{3,2,1,0:T(8,128)S(1)} %copy-done.2, f32[3,19,1,129]{3,2,1,0:T(1,128)S(1)} %transpose_reshape.8), kind=kLoop, calls=%fused_computation.2 | loop fusion | flops 1382364 | bytes 2764728 | tf_op jit(solution)/shard_map/concatenate | solution.py:187
  46.7 2.4 %fusion.1 = f32[3,17,47,129]{3,2,1,0:T(8,128)S(1)} fusion(f32[3,19,47,129]{3,2,1,0:T(8,128)} %pad_maximum_fusion.1, f32[3,47,129]{2,1,0:T(8,128)} %get-tuple-element.49, f32[3,47,129]{2,1,0:T(8,128)S(1)} %get-tuple-element.48, f32[17]{0:T(128)S(1)} %and_select_fusion.20, pred[17]{0:T(512)(128)(4,1)S(1)} %get-tuple-element.94, ...), kind=kLoop, calls=%fused_computation.6 | loop fusion | flops 1855278 | bytes 2619318 | tf_op jit(solution)/shard_map/add | solution.py:218
  49.2 0.8 fusion
  52.0 8.2 %shard_map.80 = (f32[51,45]{1,0:T(8,128)}, f32[51,45]{1,0:T(8,128)}) custom-call(f32[51,45]{1,0:T(8,128)} %reshape_transpose.14.low, f32[51,45]{1,0:T(8,128)} %reshape_transpose.15.high), custom_call_target="tpu_custom_call" | custom-call | tf_op jit(solution)/shard_map/pallas_call | solution.py:90
  61.8 1.3 %multiply_add_fusion = f32[3,17,45,129]{3,2,1,0:T(8,128)S(1)} fusion(f32[3,17,45]{2,1,0:T(8,128)S(1)} %broadcast_in_dim.237, f32[3,17,45]{2,1,0:T(8,128)S(1)} %broadcast_in_dim.234, f32[129]{0:T(256)S(1)} %and_select_fusion.16, pred[129]{0:T(512)(128)(4,1)S(1)} %get-tuple-element.98, pred[129]{0:T(512)(128)(4,1)S(1)} %get-tuple-element.99, ...), kind=kLoop, calls=%fused_computation.15 | loop fusion | flops 3552660 | bytes 2440476 | tf_op jit(solution)/shard_map/add | solution.py:218
  63.1 0.9 fusion.71
  64.3 2.7 %pad_maximum_fusion.shifted = f32[4,3,17,48,128]{4,3,2,1,0:T(8,128)} fusion(f32[1,3,17,48,128]{4,3,2,1,0:T(8,128)S(1)} %pad_bitcast_fusion, f32[1,3,17,48,128]{4,3,2,1,0:T(8,128)S(1)} %pad_bitcast_fusion.1, f32[1,3,17,48,128]{4,3,2,1,0:T(8,128)S(1)} %pad_bitcast_fusion.2, f32[1,3,17,48,128]{4,3,2,1,0:T(8,128)S(1)} %pad_bitcast_fusion.3), kind=kLoop, calls=%fused_computation.1 | loop fusion | flops 3760128 | bytes 10027008 | tf_op jit(solution)/shard_map/stack | solution.py:251
  67.1 0.8 gather_fusion
  68.6 16.3 %shard_map.81 = f32[16,48,128]{2,1,0:T(8,128)} custom-call(f32[576]{0:T(1024)} %reshape.425.weights, f32[4,3,17,48,128]{4,3,2,1,0:T(8,128)} %pad_maximum_fusion.shifted), custom_call_target="tpu_custom_call" | custom-call | tf_op jit(solution)/shard_map/pallas_call | solution.py:261
  84.9 1.1 fusion.47
  86.8 10.3 %shard_map.82 = (f32[2,3,44,128]{3,2,1,0:T(8,128)}, f32[2,3,44,128]{3,2,1,0:T(8,128)}) custom-call(f32[2,3,44,128]{3,2,1,0:T(8,128)} %get-tuple-element.67.low, f32[2,3,44,128]{3,2,1,0:T(8,128)} %get-tuple-element.66.high), custom_call_target="tpu_custom_call" | custom-call | tf_op jit(solution)/shard_map/pallas_call | solution.py:90
  97.1 1.1 maximum_maximum_fusion
  99.2 5.7 %shard_map.83 = (f32[2,16,3,128]{3,2,1,0:T(4,128)}, f32[2,16,3,128]{3,2,1,0:T(4,128)}) custom-call(f32[2,16,3,128]{3,2,1,0:T(4,128)} %get-tuple-element.63.low, f32[2,16,3,128]{3,2,1,0:T(4,128)} %get-tuple-element.62.high), custom_call_target="tpu_custom_call" | custom-call | tf_op jit(solution)/shard_map/pallas_call | solution.py:90
  104.9 1.7 %fusion.17 = f32[2,16,44,128]{3,2,1,0:T(8,128)S(1)} fusion(f32[2,16,3,128]{3,2,1,0:T(4,128)} %get-tuple-element.23, f32[2,16,3,128]{3,2,1,0:T(4,128)} %get-tuple-element.22, f32[2,16,44,128]{3,2,1,0:T(8,128)S(1)} %fusion.13), kind=kLoop, calls=%fused_computation.49 | loop fusion | flops 3063808 | bytes 1540096 | tf_op jit(solution)/shard_map/add | solution.py:275
  106.9 1.0 copy.71
  107.8 1.0 copy.72
  108.8 8.8 %shard_map.84 = (f32[96,44]{1,0:T(8,128)}, f32[96,44]{1,0:T(8,128)}) custom-call(f32[96,44]{1,0:T(8,128)} %bitcast.59, f32[96,44]{1,0:T(8,128)} %bitcast.60), custom_call_target="tpu_custom_call" | custom-call | tf_op jit(solution)/shard_map/pallas_call | solution.py:90
  117.6 1.2 copy.73
  118.8 1.2 copy.74
  120.0 2.3 %fusion.30 = f32[2,16,44,128]{3,2,1,0:T(8,128)S(1)} fusion(f32[2,16,44,128]{3,2,1,0:T(8,128)S(1)} %fusion.17, f32[2,16,44,3]{3,2,1,0:T(8,128)S(1)} %bitcast.53, f32[2,16,44,3]{3,2,1,0:T(8,128)S(1)} %bitcast.52), kind=kLoop, calls=%fused_computation.62 | loop fusion | flops 3063808 | bytes 1475584 | tf_op jit(solution)/shard_map/add | solution.py:275
  122.6 0.8 copy.76
  123.5 0.8 copy.77
  (54 shorter events, 10.3 us)
Async XLA Ops:
  0.7 13.7 %copy-start.5 = (s32[1,1,1,8]{3,2,1,0:T(1,128)S(1)}, s32[1,1,1,8]{3,2,1,0:T(1,128)}, u32[]{:S(2)}) copy-start(s32[1,1,1,8]{3,2,1,0:T(1,128)} %param.9) | copy-start | bytes 100
  0.8 15.2 %copy-start.4 = (f32[3,17,45,1]{2,3,1,0:T(1,128)S(1)}, f32[3,17,45,1]{2,3,1,0:T(1,128)}, u32[]{:S(2)}) copy-start(f32[3,17,45,1]{2,3,1,0:T(1,128)} %param.7) | copy-start | bytes 27544
  32.8 11.1 %copy-start.2 = (f32[3,1,45,129]{3,2,1,0:T(8,128)S(1)}, f32[3,1,45,129]{3,2,1,0:T(8,128)}, u32[]{:S(2)}) copy-start(f32[3,1,45,129]{3,2,1,0:T(8,128)} %get-tuple-element.14) | copy-start | bytes 208984
  32.8 11.1 %copy-start.3 = (f32[3,1,45,129]{3,2,1,0:T(8,128)S(1)}, f32[3,1,45,129]{3,2,1,0:T(8,128)}, u32[]{:S(2)}) copy-start(f32[3,1,45,129]{3,2,1,0:T(8,128)} %get-tuple-element.15) | copy-start | bytes 208984
  64.3 2.7 %copy-start = (f32[24,24]{1,0:T(8,128)S(1)}, f32[24,24]{1,0:T(8,128)}, u32[]{:S(2)}) copy-start(f32[24,24]{1,0:T(8,128)} %param.11) | copy-start | bytes 6916
  68.6 16.3 %copy-start.1 = (f32[16,44,128]{2,0,1:T(8,128)S(1)}, f32[16,44,128]{2,0,1:T(8,128)}, u32[]{:S(2)}) copy-start(f32[16,44,128]{2,0,1:T(8,128)} %param.10) | copy-start | bytes 1081348

commit v9 on v7

--- a/solution.py
+++ b/solution.py
@@ -166,6 +166,134 @@
         ],
         compiler_params=pltpu.CompilerParams(collective_id=100, has_side_effects=True),
     )(shard)
+
+
+def plane_kernel(*refs, axes, sizes, offsets):
+    count = len(offsets)
+    sends = refs[:count]
+    outs = refs[count : 2 * count]
+    landed = refs[2 * count : 3 * count]
+    send_sem, recv_sem = refs[3 * count :]
+    me = [lax.axis_index(axis) for axis in axes]
+    mesh_ids = pl.DeviceIdType.MESH
+
+    def exists(offset):
+        inside = None
+        for position, step, size in zip(me, offset, sizes):
+            if step == 0:
+                continue
+            here = (position + step >= 0) & (position + step < size)
+            inside = here if inside is None else inside & here
+        return inside
+
+    def target(offset):
+        return {axis: position + step for axis, position, step in zip(axes, me, offset)}
+
+    barrier = pltpu.get_barrier_semaphore()
+    expected = 0
+    for offset in offsets:
+
+        @pl.when(exists(offset))
+        def _():
+            pl.semaphore_signal(barrier, 1, device_id=target(offset), device_id_type=mesh_ids)
+
+        expected = expected + exists(offset).astype(jnp.int32)
+    pl.semaphore_wait(barrier, expected)
+    slot = {offset: k for k, offset in enumerate(offsets)}
+    outgoing = []
+    for k, offset in enumerate(offsets):
+        back = slot[tuple(-step for step in offset)]
+        outgoing.append(
+            pltpu.make_async_remote_copy(
+                src_ref=sends[k],
+                dst_ref=landed[back],
+                send_sem=send_sem.at[k],
+                recv_sem=recv_sem.at[back],
+                device_id=target(offset),
+                device_id_type=mesh_ids,
+            )
+        )
+
+        @pl.when(exists(offset))
+        def _():
+            outgoing[k].start()
+
+    for k, offset in enumerate(offsets):
+        back = slot[tuple(-step for step in offset)]
+        incoming = pltpu.make_async_remote_copy(
+            src_ref=sends[back],
+            dst_ref=landed[k],
+            send_sem=send_sem.at[back],
+            recv_sem=recv_sem.at[k],
+            device_id=target(offset),
+            device_id_type=mesh_ids,
+        )
+
+        @pl.when(exists(offset))
+        def _():
+            outgoing[k].wait_send()
+            incoming.wait_recv()
+            outs[k][...] = landed[k][...]
+
+        @pl.when(jnp.logical_not(exists(offset)))
+        def _():
+            outs[k][...] = jnp.zeros(outs[k].shape, outs[k].dtype)
+
+
+def as_rows(piece, thin):
+    tiled = math.prod(piece.shape[:-2]) * -(-piece.shape[-2] // 8) * 8 * -(-piece.shape[-1] // 128) * 128
+    if tiled <= 3 * piece.size:
+        return piece, None
+    moved = jnp.moveaxis(piece, thin, tuple(range(len(thin))))
+    return moved.reshape(-1, moved.shape[-1]), moved.shape
+
+
+def from_rows(piece, moved, thin):
+    if moved is None:
+        return piece
+    return jnp.moveaxis(piece.reshape(moved), tuple(range(len(thin))), thin)
+
+
+def with_plane_halo(shard, axes, dims, width):
+    offsets = [(ox, oy) for ox in (-1, 0, 1) for oy in (-1, 0, 1) if (ox, oy) != (0, 0)]
+    pieces = []
+    layouts = []
+    for offset in offsets:
+        piece = shard
+        thin = []
+        for step, dim in zip(offset, dims):
+            length = piece.shape[dim]
+            if step == 1:
+                piece = lax.slice_in_dim(piece, length - width, length, axis=dim)
+            elif step == -1:
+                piece = lax.slice_in_dim(piece, 0, width, axis=dim)
+            if step != 0:
+                thin.append(dim)
+        piece, moved = as_rows(piece, thin)
+        pieces.append(piece)
+        layouts.append((moved, thin))
+    key = ("plane",) + tuple(piece.shape for piece in pieces)
+    if key not in HALO_IDS:
+        HALO_IDS[key] = len(HALO_IDS)
+    sizes = tuple(lax.axis_size(axis) for axis in axes)
+    kernel = functools.partial(plane_kernel, axes=axes, sizes=sizes, offsets=tuple(offsets))
+    vmem = pl.BlockSpec(memory_space=pltpu.VMEM)
+    shapes = tuple(jax.ShapeDtypeStruct(piece.shape, piece.dtype) for piece in pieces)
+    received = pl.pallas_call(
+        kernel,
+        out_shape=shapes,
+        in_specs=[vmem] * len(pieces),
+        out_specs=tuple([vmem] * len(pieces)),
+        scratch_shapes=[pltpu.VMEM(piece.shape, piece.dtype) for piece in pieces]
+        + [pltpu.SemaphoreType.DMA((len(pieces),)), pltpu.SemaphoreType.DMA((len(pieces),))],
+        compiler_params=pltpu.CompilerParams(collective_id=HALO_IDS[key], has_side_effects=True),
+    )(*pieces)
+    got = {offset: from_rows(piece, *layout) for offset, piece, layout in zip(offsets, received, layouts)}
+    got[(0, 0)] = shard
+    rows = []
+    for ox in (-1, 0, 1):
+        rows.append(jnp.concatenate([got[(ox, oy)] for oy in (-1, 0, 1)], axis=dims[1]))
+    return jnp.concatenate(rows, axis=dims[0])
 
 
 def with_halo(shard, sides, width):
@@ -287,10 +415,12 @@
 
 
 def filter_field(field, sides):
-    for axis, dim in sides:
-        padded = with_halo(field, ((axis, dim),), RADIUS)
-        field = smooth(padded, dim, field.shape[dim])
-    return field
+    (axis_x, dim_x), (axis_y, dim_y), (axis_z, dim_z) = sides
+    count_x, count_y = field.shape[dim_x], field.shape[dim_y]
+    padded = with_plane_halo(field, (axis_x, axis_y), (dim_x, dim_y), RADIUS)
+    field = smooth(smooth(padded, dim_x, count_x), dim_y, count_y)
+    padded = with_halo(field, ((axis_z, dim_z),), RADIUS)
+    return smooth(padded, dim_z, field.shape[dim_z])
 
 
 def local(local_solution, top_nodes, coarse_solution, corner_dofs, density, element_stiffness):
@@ -318,7 +448,7 @@
     upper_y = index_y < lax.axis_size("gy") - 1
     lower_z = index_z > 0
     upper_z = index_z < lax.axis_size("gz") - 1
-    extended = with_halo(nodes, (("gx", 1), ("gy", 2)), 1)
+    extended = with_plane_halo(nodes, ("gx", "gy"), (1, 2), 1)
     extended = average_rows(extended, 1, lower_x, upper_x)
     averaged = average_rows(extended, 2, lower_y, upper_y)
     extended = with_halo(averaged, (("gz", 3),), 1)

time: 124 us -> 120 us (0.968)
  the two profiles are of different devices: /device:TPU:224 before, /device:TPU:29 now
where the time goes in v9:
time: 120 us; the launch traced here: 119 us
  Pallas kernels  68.3 us (57%)
  other arithmetic  26.2 us (22%)
  local copies, waits for them, and re-layouts  23.8 us (20%)
    pallas_call x2, Pallas kernels, with_plane_halo(): pl.pallas_call(kernel, out_shape=shapes, in_specs=[vmem] * len(pieces), o...  27.4 us
    pallas_call x1, Pallas kernels, element_energy(): pl.pallas_call(kernel, out_shape=jax.ShapeDtypeStruct((count_x, rows, cou...  15 us
    pallas_call x2, Pallas kernels, exchange(): pl.pallas_call(kernel, out_shape=(slab, slab), in_specs=[vmem, vmem], out...  13.9 us
    pallas_call x1, Pallas kernels, gather_peers(): pl.pallas_call(kernel, out_shape=jax.ShapeDtypeStruct(stacked, shard.dtyp...  12 us
    unnamed x24, local copies, waits for them, and re-layouts  5.77 us
    add x3, other arithmetic, average_rows(): return own_rows * factor + rim_part * 0.5  4.87 us
    another operation x6, local copies, waits for them, and re-layouts, from_rows(): return jnp.moveaxis(piece.reshape(moved), tuple(range(len(thin))), thin)  4.48 us
    add x1, other arithmetic, recover(): summed = summed + basis[None] * corner_vals[:, corner][:, None, None, None]  4.21 us

profile of v9, /device:TPU:29, one launch (start us, length us, event | category | flops | bytes accessed | tf_op | source)
XLA Modules:
  0.0 119.3 jit_solution(911800627064038236)
XLA Ops:
  0.8 3.0 %broadcast_multiply_fusion.1 = (f32[17,45,129]{2,1,0:T(8,128)S(1)}, f32[17,45,129]{2,1,0:T(8,128)}, f32[17,45,129]{2,1,0:T(8,128)}, f32[17,45,129]{2,1,0:T(8,128...) fusion(f32[17,45]{1,0:T(8,128)S(1)} %get-tuple-element.108, ...), kind=kLoop, calls=%fused_computation.88 | loop fusion | flops 789480 | bytes 3171192 | tf_op jit(solution)/shard_map/mul | solution.py:329
  3.7 12.0 %shard_map.77 = f32[16,3,512]{2,1,0:T(4,128)} custom-call(f32[3,512]{1,0:T(4,128)} %shard.1), custom_call_target="tpu_custom_call" | custom-call | tf_op jit(solution)/shard_map/pallas_call | solution.py:157
  15.8 1.1 select_reduce_fusion
  17.3 1.6 %copy.76 = f32[3,17,45,1]{3,2,1,0:T(8,128)} copy(f32[3,17,45,1]{2,3,1,0:T(1,128)S(1)} %copy-done.5) | data formatting | bytes 18360 | tf_op args[1]
  18.8 4.2 %fusion.7 = f32[3,17,45,129]{3,2,1,0:T(8,128)S(1)} fusion(f32[3,17,45,1]{3,2,1,0:T(8,128)} %copy.76, f32[3,17,45,128]{3,2,1,0:T(8,128)} %param.6, f32[3]{0:T(128)S(1)} %get-tuple-element.57, f32[17,45,129]{2,1,0:T(8,128)} %get-tuple-element.99, f32[3]{0:T(128)S(1)} %get-tuple-element.58, f32[17,45,129]{2,1,0:T(8,128)S(1)} %get-tuple-element.98, ...), kind=kLoop, calls=%fused_computation.11 | loop fusion | flops 5032935 | bytes 5526456 | tf_op jit(solution)/shard_map/add | solution.py:330
  23.1 0.8 fusion.66
  27.8 12.3 %shard_map.78 = (f32[3,129]{1,0:T(4,128)}, f32[3,1,45,129]{3,2,1,0:T(8,128)}, f32[3,129]{1,0:T(4,128)}, f32[51,129]{1,0:T(8,128)}, f32[51,129]{1,0:T(8,128)}, /*...) custom-call(f32[3,129]{1,0:T(4,128)} %bitcast.80, f32[3,1,45,129]{3,2,1,0:T(8,128)} %get-tuple-element.75.refs_1_, ...), custom_call_target="tpu_custom_call" | custom-call | tf_op jit(solution)/shard_map/pallas_call | solution.py:282
  41.5 0.9 maximum_bitcast_fusion
  43.8 0.9 maximum_bitcast_fusion.1
  44.7 0.9 transpose_reshape.20
  45.6 0.9 transpose_reshape.21
  46.6 2.7 %fusion.8 = f32[3,17,47,129]{3,2,1,0:T(8,128)S(1)} fusion(f32[3,17,1,129]{3,2,1,0:T(1,128)S(1)} %transpose_reshape.21, f32[3,17,45,129]{3,2,1,0:T(8,128)} %copy-done.1, f32[3,17,1,129]{3,2,1,0:T(1,128)S(1)} %transpose_reshape.20, f32[3,47,129]{2,1,0:T(8,128)S(1)} %maximum_bitcast_fusion.1, f32[3,47,129]{2,1,0:T(8,128)S(1)} %maximum_bitcast_fusion, ...), kind=kLoop, calls=%fused_computation.13 | loop fusion | flops 2473704 | bytes 2619318 | tf_op jit(solution)/shard_map/add | solution.py:346
  49.5 0.8 fusion
  52.2 6.8 %shard_map.79 = (f32[51,45]{1,0:T(8,128)}, f32[51,45]{1,0:T(8,128)}) custom-call(f32[51,45]{1,0:T(8,128)} %reshape_transpose.30.low, f32[51,45]{1,0:T(8,128)} %reshape_transpose.31.high), custom_call_target="tpu_custom_call" | custom-call | tf_op jit(solution)/shard_map/pallas_call | solution.py:90
  59.0 0.8 broadcast_in_dim.234
  59.8 0.8 broadcast_in_dim.237
  60.6 1.3 %multiply_add_fusion = f32[3,17,45,129]{3,2,1,0:T(8,128)S(1)} fusion(f32[3,17,45]{2,1,0:T(8,128)S(1)} %broadcast_in_dim.237, f32[3,17,45]{2,1,0:T(8,128)S(1)} %broadcast_in_dim.234, f32[129]{0:T(256)S(1)} %and_select_fusion.16, pred[129]{0:T(512)(128)(4,1)S(1)} %get-tuple-element.120, pred[129]{0:T(512)(128)(4,1)S(1)} %get-tuple-element.121, ...), kind=kLoop, calls=%fused_computation.14 | loop fusion | flops 3552660 | bytes 2440476 | tf_op jit(solution)/shard_map/add | solution.py:346
  61.9 0.9 fusion.63
  63.1 2.7 %pad_maximum_fusion.shifted = f32[4,3,17,48,128]{4,3,2,1,0:T(8,128)} fusion(f32[1,3,17,48,128]{4,3,2,1,0:T(8,128)S(1)} %pad_bitcast_fusion, f32[1,3,17,48,128]{4,3,2,1,0:T(8,128)S(1)} %pad_bitcast_fusion.1, f32[1,3,17,48,128]{4,3,2,1,0:T(8,128)S(1)} %pad_bitcast_fusion.2, f32[1,3,17,48,128]{4,3,2,1,0:T(8,128)S(1)} %pad_bitcast_fusion.3), kind=kLoop, calls=%fused_computation.1 | loop fusion | flops 3760128 | bytes 10027008 | tf_op jit(solution)/shard_map/stack | solution.py:379
  65.9 0.8 gather_fusion
  67.4 15.0 %shard_map.80 = f32[16,48,128]{2,1,0:T(8,128)} custom-call(f32[576]{0:T(1024)} %reshape.425.weights, f32[4,3,17,48,128]{4,3,2,1,0:T(8,128)} %pad_maximum_fusion.shifted), custom_call_target="tpu_custom_call" | custom-call | tf_op jit(solution)/shard_map/pallas_call | solution.py:389
  82.4 1.1 fusion.36
  85.6 15.1 %shard_map.81 = (f32[2,3,3,128]{3,2,1,0:T(4,128)}, f32[2,3,44,128]{3,2,1,0:T(8,128)}, f32[2,3,3,128]{3,2,1,0:T(4,128)}, f32[2,16,3,128]{3,2,1,0:T(4,128)}, f32[2...) custom-call(f32[2,3,3,128]{3,2,1,0:T(4,128)} %get-tuple-element.85.refs_0, ...), custom_call_target="tpu_custom_call" | custom-call | tf_op jit(solution)/shard_map/pallas_call | solution.py:282
  100.8 1.4 %maximum_maximum_fusion = (f32[2,19,50,128]{3,2,1,0:T(8,128)S(1)}, f32[2,19,50,128]{3,2,1,0:T(8,128)S(1)}) fusion(f32[2,16,3,128]{3,2,1,0:T(4,128)} %get-tuple-element.36, f32[1,16,44,128]{3,2,1,0:T(8,128)S(1)} %get-tuple-element.91, f32[1,16,44,128]{3,2,1,0:T(8,128)S(1)} %get-tuple-element.90, f32[2,16,3,128]{3,2,1,0:T(4,128)} %get-tuple-element.35, ...), kind=kLoop, calls=%fused_computation.41 | loop fusion | flops 2918400 | bytes 3072000 | tf_op jit(solution)/shard_map/concatenate | solution.py:296
  103.6 1.0 copy.81
  104.5 1.0 copy.82
  105.5 7.1 %shard_map.82 = (f32[96,44]{1,0:T(8,128)}, f32[96,44]{1,0:T(8,128)}) custom-call(f32[96,44]{1,0:T(8,128)} %bitcast.73, f32[96,44]{1,0:T(8,128)} %bitcast.74), custom_call_target="tpu_custom_call" | custom-call | tf_op jit(solution)/shard_map/pallas_call | solution.py:90
  112.6 1.2 %copy.83 = f32[3,2,16,44]{0,3,2,1:T(8,128)S(1)} copy(f32[3,2,16,44]{3,2,1,0:T(8,128)} %bitcast.76) | data formatting | bytes 33792 | tf_op jit(solution)/shard_map/reshape | solution.py:313
  113.8 1.2 %copy.84 = f32[3,2,16,44]{0,3,2,1:T(8,128)S(1)} copy(f32[3,2,16,44]{3,2,1,0:T(8,128)} %bitcast.75) | data formatting | bytes 33792 | tf_op jit(solution)/shard_map/reshape | solution.py:314
  115.0 2.3 %fusion.17 = f32[2,16,44,128]{3,2,1,0:T(8,128)S(1)} fusion(f32[2,16,44,128]{3,2,1,0:T(8,128)S(1)} %slice_add_fusion.1, f32[2,16,44,3]{3,2,1,0:T(8,128)S(1)} %bitcast.67, f32[2,16,44,3]{3,2,1,0:T(8,128)S(1)} %bitcast.66), kind=kLoop, calls=%fused_computation.57 | loop fusion | flops 3063808 | bytes 1475584 | tf_op jit(solution)/shard_map/add | solution.py:403
  117.6 0.8 copy.86
  118.5 0.8 copy.87
  (64 shorter events, 14.1 us)
Async XLA Ops:
  0.7 15.0 %copy-start.6 = (s32[1,1,1,8]{3,2,1,0:T(1,128)S(1)}, s32[1,1,1,8]{3,2,1,0:T(1,128)}, u32[]{:S(2)}) copy-start(s32[1,1,1,8]{3,2,1,0:T(1,128)} %param.9) | copy-start | bytes 100
  0.8 16.5 %copy-start.5 = (f32[3,17,45,1]{2,3,1,0:T(1,128)S(1)}, f32[3,17,45,1]{2,3,1,0:T(1,128)}, u32[]{:S(2)}) copy-start(f32[3,17,45,1]{2,3,1,0:T(1,128)} %param.7) | copy-start | bytes 27544
  23.1 23.5 %copy-start.1 = (f32[3,17,45,129]{3,2,1,0:T(8,128)}, f32[3,17,45,129]{3,2,1,0:T(8,128)S(1)}, u32[]{:S(2)}) copy-start(f32[3,17,45,129]{3,2,1,0:T(8,128)S(1)} %fusion.7) | copy-start | bytes 3552664
  63.1 2.7 %copy-start = (f32[24,24]{1,0:T(8,128)S(1)}, f32[24,24]{1,0:T(8,128)}, u32[]{:S(2)}) copy-start(f32[24,24]{1,0:T(8,128)} %param.11) | copy-start | bytes 6916
  67.4 15.0 %copy-start.2 = (f32[16,44,128]{2,0,1:T(8,128)S(1)}, f32[16,44,128]{2,0,1:T(8,128)}, u32[]{:S(2)}) copy-start(f32[16,44,128]{2,0,1:T(8,128)} %param.10) | copy-start | bytes 1081348
  100.8 1.4 %copy-start.3 = (f32[2,16,3,128]{3,2,1,0:T(4,128)S(1)}, f32[2,16,3,128]{3,2,1,0:T(4,128)}, u32[]{:S(2)}) copy-start(f32[2,16,3,128]{3,2,1,0:T(4,128)} %get-tuple-element.35) | copy-start | bytes 147460
  100.8 1.4 %copy-start.4 = (f32[2,16,3,128]{3,2,1,0:T(4,128)S(1)}, f32[2,16,3,128]{3,2,1,0:T(4,128)}, u32[]{:S(2)}) copy-start(f32[2,16,3,128]{3,2,1,0:T(4,128)} %get-tuple-element.36) | copy-start | bytes 147460

commit v10 on v9

--- a/solution.py
+++ b/solution.py
@@ -321,14 +321,17 @@
     ey = local_nodes.shape[2] - 1
     ratio_x = jnp.arange(ex + 1, dtype=jnp.float32) / ex
     ratio_y = jnp.arange(ey + 1, dtype=jnp.float32) / ey
-    summed = local_nodes
-    for corner in range(8):
-        along_x = ratio_x if corner // 4 == 1 else 1.0 - ratio_x
-        along_y = ratio_y if corner // 2 % 2 == 1 else 1.0 - ratio_y
-        along_z = ratio_z if corner % 2 == 1 else 1.0 - ratio_z
-        basis = along_x[:, None, None] * along_y[None, :, None] * along_z[None, None, :]
-        summed = summed + basis[None] * corner_vals[:, corner][:, None, None, None]
-    return summed
+    planes = []
+    for high_z in (0, 1):
+        plane = None
+        for corner in range(high_z, 8, 2):
+            along_x = ratio_x if corner // 4 == 1 else 1.0 - ratio_x
+            along_y = ratio_y if corner // 2 % 2 == 1 else 1.0 - ratio_y
+            basis = along_x[:, None] * along_y[None, :]
+            term = basis[None] * corner_vals[:, corner][:, None, None]
+            plane = term if plane is None else plane + term
+        planes.append(plane[:, :, :, None])
+    return local_nodes + planes[0] * (1.0 - ratio_z) + planes[1] * ratio_z
 
 
 def average_rows(extended, dim, has_lower, has_upper):

time: 120 us -> 115 us (0.958)
  other arithmetic: 26.2 us -> 20.7 us
    add x1 -> x2, other arithmetic: 4.21 us -> 1.03 us  [the longest x1 0.93 us: recover(): return local_nodes + planes[0] * (1.0 - ratio_z) + planes[1] * ratio_z]
    mul x2 -> x1, other arithmetic: 3.03 us -> 0.08 us  [recover(): basis = along_x[:, None] * along_y[None, :]]
    unnamed x24 -> x22, local copies, waits for them, and re-layouts: 5.77 us -> 5.75 us
where the time goes in v10:
time: 115 us; the launch traced here: 114 us
  Pallas kernels  68.5 us (60%)
  local copies, waits for them, and re-layouts  23.7 us (21%)
  other arithmetic  20.7 us (18%)
    pallas_call x2, Pallas kernels, with_plane_halo(): pl.pallas_call(kernel, out_shape=shapes, in_specs=[vmem] * len(pieces), o...  27.4 us
    pallas_call x1, Pallas kernels, element_energy(): pl.pallas_call(kernel, out_shape=jax.ShapeDtypeStruct((count_x, rows, cou...  15 us
    pallas_call x2, Pallas kernels, exchange(): pl.pallas_call(kernel, out_shape=(slab, slab), in_specs=[vmem, vmem], out...  13.9 us
    pallas_call x1, Pallas kernels, gather_peers(): pl.pallas_call(kernel, out_shape=jax.ShapeDtypeStruct(stacked, shard.dtyp...  12.2 us
    unnamed x22, local copies, waits for them, and re-layouts  5.75 us
    add x3, other arithmetic, average_rows(): return own_rows * factor + rim_part * 0.5  4.87 us
    another operation x6, local copies, waits for them, and re-layouts, from_rows(): return jnp.moveaxis(piece.reshape(moved), tuple(range(len(thin))), thin)  4.48 us
    add x3, other arithmetic, smooth(): summed = term_value if summed is None else summed + term_value  3.36 us

profile of v10, /device:TPU:29, one launch (start us, length us, event | category | flops | bytes accessed | tf_op | source)
XLA Modules:
  0.0 113.9 jit_solution(6636804089574519068)
XLA Ops:
  0.6 12.2 %shard_map.77 = f32[16,3,512]{2,1,0:T(4,128)} custom-call(f32[3,512]{1,0:T(4,128)} %shard.1), custom_call_target="tpu_custom_call" | custom-call | tf_op jit(solution)/shard_map/pallas_call | solution.py:157
  12.8 0.8 iota_compare_fusion
  13.6 1.1 select_reduce_fusion
  15.2 1.3 %copy.76 = f32[3,17,45,1]{3,2,1,0:T(8,128)S(1)} copy(f32[3,17,45,1]{2,3,1,0:T(1,128)} %param.7) | data formatting | bytes 18360 | tf_op args[1]
  16.5 0.9 fusion.1
  18.1 0.8 copy.108
  22.4 12.3 %shard_map.78 = (f32[3,129]{1,0:T(4,128)}, f32[3,1,45,129]{3,2,1,0:T(8,128)}, f32[3,129]{1,0:T(4,128)}, f32[51,129]{1,0:T(8,128)}, f32[51,129]{1,0:T(8,128)}, /*...) custom-call(f32[3,129]{1,0:T(4,128)} %bitcast.80, f32[3,1,45,129]{3,2,1,0:T(8,128)} %get-tuple-element.75.refs_1_, ...), custom_call_target="tpu_custom_call" | custom-call | tf_op jit(solution)/shard_map/pallas_call | solution.py:282
  36.1 0.9 maximum_bitcast_fusion
  38.4 0.9 maximum_bitcast_fusion.1
  39.3 0.9 transpose_reshape.20
  40.2 0.9 transpose_reshape.21
  41.1 2.7 %fusion.2 = f32[3,17,47,129]{3,2,1,0:T(8,128)S(1)} fusion(f32[3,17,1,129]{3,2,1,0:T(1,128)S(1)} %transpose_reshape.21, f32[3,17,45,129]{3,2,1,0:T(8,128)} %copy-done.1, f32[3,17,1,129]{3,2,1,0:T(1,128)S(1)} %transpose_reshape.20, f32[3,47,129]{2,1,0:T(8,128)S(1)} %maximum_bitcast_fusion.1, f32[3,47,129]{2,1,0:T(8,128)S(1)} %maximum_bitcast_fusion, ...), kind=kLoop, calls=%fused_computation.7 | loop fusion | flops 2473704 | bytes 2619318 | tf_op jit(solution)/shard_map/add | solution.py:349
  44.0 0.8 fusion
  46.8 6.8 %shard_map.79 = (f32[51,45]{1,0:T(8,128)}, f32[51,45]{1,0:T(8,128)}) custom-call(f32[51,45]{1,0:T(8,128)} %reshape_transpose.30.low, f32[51,45]{1,0:T(8,128)} %reshape_transpose.31.high), custom_call_target="tpu_custom_call" | custom-call | tf_op jit(solution)/shard_map/pallas_call | solution.py:90
  53.6 0.8 broadcast_in_dim.230
  54.4 0.8 broadcast_in_dim.233
  55.1 1.3 %multiply_add_fusion = f32[3,17,45,129]{3,2,1,0:T(8,128)S(1)} fusion(f32[3,17,45]{2,1,0:T(8,128)S(1)} %broadcast_in_dim.233, f32[3,17,45]{2,1,0:T(8,128)S(1)} %broadcast_in_dim.230, f32[129]{0:T(256)S(1)} %and_select_fusion.16, pred[129]{0:T(512)(128)(4,1)S(1)} %get-tuple-element.108, pred[129]{0:T(512)(128)(4,1)S(1)} %get-tuple-element.109, ...), kind=kLoop, calls=%fused_computation.8 | loop fusion | flops 3552660 | bytes 2440476 | tf_op jit(solution)/shard_map/add | solution.py:349
  56.4 0.9 fusion.57
  57.7 2.7 %pad_maximum_fusion.shifted = f32[4,3,17,48,128]{4,3,2,1,0:T(8,128)} fusion(f32[1,3,17,48,128]{4,3,2,1,0:T(8,128)S(1)} %pad_bitcast_fusion, f32[1,3,17,48,128]{4,3,2,1,0:T(8,128)S(1)} %pad_bitcast_fusion.1, f32[1,3,17,48,128]{4,3,2,1,0:T(8,128)S(1)} %pad_bitcast_fusion.2, f32[1,3,17,48,128]{4,3,2,1,0:T(8,128)S(1)} %pad_bitcast_fusion.3), kind=kLoop, calls=%fused_computation.1 | loop fusion | flops 3760128 | bytes 10027008 | tf_op jit(solution)/shard_map/stack | solution.py:382
  60.4 0.8 gather_fusion
  62.0 15.0 %shard_map.80 = f32[16,48,128]{2,1,0:T(8,128)} custom-call(f32[576]{0:T(1024)} %reshape.419.weights, f32[4,3,17,48,128]{4,3,2,1,0:T(8,128)} %pad_maximum_fusion.shifted), custom_call_target="tpu_custom_call" | custom-call | tf_op jit(solution)/shard_map/pallas_call | solution.py:392
  77.0 1.1 fusion.30
  80.2 15.1 %shard_map.81 = (f32[2,3,3,128]{3,2,1,0:T(4,128)}, f32[2,3,44,128]{3,2,1,0:T(8,128)}, f32[2,3,3,128]{3,2,1,0:T(4,128)}, f32[2,16,3,128]{3,2,1,0:T(4,128)}, f32[2...) custom-call(f32[2,3,3,128]{3,2,1,0:T(4,128)} %get-tuple-element.85.refs_0, ...), custom_call_target="tpu_custom_call" | custom-call | tf_op jit(solution)/shard_map/pallas_call | solution.py:282
  95.3 1.4 %maximum_maximum_fusion = (f32[2,19,50,128]{3,2,1,0:T(8,128)S(1)}, f32[2,19,50,128]{3,2,1,0:T(8,128)S(1)}) fusion(f32[2,16,3,128]{3,2,1,0:T(4,128)} %get-tuple-element.36, f32[1,16,44,128]{3,2,1,0:T(8,128)S(1)} %get-tuple-element.91, f32[1,16,44,128]{3,2,1,0:T(8,128)S(1)} %get-tuple-element.90, f32[2,16,3,128]{3,2,1,0:T(4,128)} %get-tuple-element.35, ...), kind=kLoop, calls=%fused_computation.35 | loop fusion | flops 2918400 | bytes 3072000 | tf_op jit(solution)/shard_map/concatenate | solution.py:296
  98.1 1.0 copy.81
  99.1 1.0 copy.82
  100.0 7.1 %shard_map.82 = (f32[96,44]{1,0:T(8,128)}, f32[96,44]{1,0:T(8,128)}) custom-call(f32[96,44]{1,0:T(8,128)} %bitcast.73, f32[96,44]{1,0:T(8,128)} %bitcast.74), custom_call_target="tpu_custom_call" | custom-call | tf_op jit(solution)/shard_map/pallas_call | solution.py:90
  107.2 1.2 %copy.83 = f32[3,2,16,44]{0,3,2,1:T(8,128)S(1)} copy(f32[3,2,16,44]{3,2,1,0:T(8,128)} %bitcast.76) | data formatting | bytes 33792 | tf_op jit(solution)/shard_map/reshape | solution.py:313
  108.4 1.2 %copy.84 = f32[3,2,16,44]{0,3,2,1:T(8,128)S(1)} copy(f32[3,2,16,44]{3,2,1,0:T(8,128)} %bitcast.75) | data formatting | bytes 33792 | tf_op jit(solution)/shard_map/reshape | solution.py:314
  109.6 2.3 %fusion.11 = f32[2,16,44,128]{3,2,1,0:T(8,128)S(1)} fusion(f32[2,16,44,128]{3,2,1,0:T(8,128)S(1)} %slice_add_fusion.1, f32[2,16,44,3]{3,2,1,0:T(8,128)S(1)} %bitcast.67, f32[2,16,44,3]{3,2,1,0:T(8,128)S(1)} %bitcast.66), kind=kLoop, calls=%fused_computation.51 | loop fusion | flops 3063808 | bytes 1475584 | tf_op jit(solution)/shard_map/add | solution.py:406
  112.2 0.8 copy.86
  113.1 0.8 copy.87
  (62 shorter events, 14.3 us)
Async XLA Ops:
  0.6 15.9 %copy-start.3 = (f32[3,17,45,128]{3,2,1,0:T(8,128)S(1)}, f32[3,17,45,128]{3,2,1,0:T(8,128)}, u32[]{:S(2)}) copy-start(f32[3,17,45,128]{3,2,1,0:T(8,128)} %param.6) | copy-start | bytes 3525124
  17.4 3.4 %copy-start.1 = (f32[3,17,45,129]{3,2,1,0:T(8,128)}, f32[3,17,45,129]{3,2,1,0:T(8,128)S(1)}, u32[]{:S(2)}) copy-start(f32[3,17,45,129]{3,2,1,0:T(8,128)S(1)} %fusion.1) | copy-start | bytes 3552664
  57.7 2.7 %copy-start = (f32[24,24]{1,0:T(8,128)S(1)}, f32[24,24]{1,0:T(8,128)}, u32[]{:S(2)}) copy-start(f32[24,24]{1,0:T(8,128)} %param.11) | copy-start | bytes 6916
  62.0 15.0 %copy-start.2 = (f32[16,44,128]{2,0,1:T(8,128)S(1)}, f32[16,44,128]{2,0,1:T(8,128)}, u32[]{:S(2)}) copy-start(f32[16,44,128]{2,0,1:T(8,128)} %param.10) | copy-start | bytes 1081348
  95.3 1.4 %copy-start.4 = (f32[2,16,3,128]{3,2,1,0:T(4,128)S(1)}, f32[2,16,3,128]{3,2,1,0:T(4,128)}, u32[]{:S(2)}) copy-start(f32[2,16,3,128]{3,2,1,0:T(4,128)} %get-tuple-element.35) | copy-start | bytes 147460
  95.3 1.4 %copy-start.5 = (f32[2,16,3,128]{3,2,1,0:T(4,128)S(1)}, f32[2,16,3,128]{3,2,1,0:T(4,128)}, u32[]{:S(2)}) copy-start(f32[2,16,3,128]{3,2,1,0:T(4,128)} %get-tuple-element.36) | copy-start | bytes 147460

commit v11 on v10

--- a/solution.py
+++ b/solution.py
@@ -242,7 +242,7 @@
 
 def as_rows(piece, thin):
     tiled = math.prod(piece.shape[:-2]) * -(-piece.shape[-2] // 8) * 8 * -(-piece.shape[-1] // 128) * 128
-    if tiled <= 3 * piece.size:
+    if tiled <= 3 * piece.size or tiled <= 65536:
         return piece, None
     moved = jnp.moveaxis(piece, thin, tuple(range(len(thin))))
     return moved.reshape(-1, moved.shape[-1]), moved.shape
@@ -349,8 +349,12 @@
     return own_rows * factor + rim_part * 0.5
 
 
-def energy_kernel(weights, shifted, out, *, count_x, chunks):
+def energy_kernel(stiffness, shifted, out, weights, *, count_x, chunks):
     sources = (shifted.at[0], shifted.at[2], shifted.at[1], shifted.at[3])
+    for a in range(24):
+        weights[a * 24 + a] = stiffness[a, a]
+        for b in range(a + 1, 24):
+            weights[a * 24 + b] = stiffness[a, b] + stiffness[b, a]
 
     def row(i, carry):
         for first in chunks:
@@ -385,8 +389,6 @@
             for dy, dz in ((0, 0), (1, 0), (0, 1), (1, 1))
         ]
     )
-    upper = jnp.triu(stiffness + stiffness.T, 1) + jnp.diag(jnp.diagonal(stiffness))
-    weights = upper.reshape(-1)
     kernel = functools.partial(energy_kernel, count_x=count_x, chunks=tuple(range(0, rows, 8)))
     vmem = pl.BlockSpec(memory_space=pltpu.VMEM)
     energy = pl.pallas_call(
@@ -394,7 +396,8 @@
         out_shape=jax.ShapeDtypeStruct((count_x, rows, count_z), jnp.float32),
         in_specs=[pl.BlockSpec(memory_space=pltpu.SMEM), vmem],
         out_specs=vmem,
-    )(weights, shifted)
+        scratch_shapes=[pltpu.SMEM((24 * 24,), jnp.float32)],
+    )(stiffness, shifted)
     return energy[:, :count_y, :]
 
 

time: 115 us -> 109 us (0.948)
  local copies, waits for them, and re-layouts: 23.7 us -> 17.5 us
    another operation x6 -> x2, local copies, waits for them, and re-layouts: 4.48 us -> 1.75 us  [from_rows(): return jnp.moveaxis(piece.reshape(moved), tuple(range(len(thin))), thin)]
    unnamed x22 -> x15, local copies, waits for them, and re-layouts: 5.75 us -> 3.03 us
where the time goes in v11:
time: 109 us; the launch traced here: 108 us
  Pallas kernels  68.8 us (63%)
  other arithmetic  20.7 us (19%)
  local copies, waits for them, and re-layouts  17.5 us (16%)
    pallas_call x2, Pallas kernels, with_plane_halo(): pl.pallas_call(kernel, out_shape=shapes, in_specs=[vmem] * len(pieces), o...  27.4 us
    pallas_call x1, Pallas kernels, element_energy(): pl.pallas_call(kernel, out_shape=jax.ShapeDtypeStruct((count_x, rows, cou...  15.3 us
    pallas_call x2, Pallas kernels, exchange(): pl.pallas_call(kernel, out_shape=(slab, slab), in_specs=[vmem, vmem], out...  13.9 us
    pallas_call x1, Pallas kernels, gather_peers(): pl.pallas_call(kernel, out_shape=jax.ShapeDtypeStruct(stacked, shard.dtyp...  12.2 us
    add x3, other arithmetic, average_rows(): return own_rows * factor + rim_part * 0.5  4.87 us
    add x3, other arithmetic, smooth(): summed = term_value if summed is None else summed + term_value  3.36 us
    another operation x4, other arithmetic, local(): smoothed = filter_field(jnp.stack([density * sens, density]), sides)  3.18 us
    unnamed x15, local copies, waits for them, and re-layouts  3.03 us

profile of v11, /device:TPU:29, one launch (start us, length us, event | category | flops | bytes accessed | tf_op | source)
XLA Modules:
  0.0 108.0 jit_solution(5941720199279670365)
XLA Ops:
  0.6 12.2 %shard_map.77 = f32[16,3,512]{2,1,0:T(4,128)} custom-call(f32[3,512]{1,0:T(4,128)} %shard.1), custom_call_target="tpu_custom_call" | custom-call | tf_op jit(solution)/shard_map/pallas_call | solution.py:157
  12.8 0.8 iota_compare_fusion
  13.6 1.1 %select_reduce_fusion = f32[3,8]{1,0:T(4,128)S(1)} fusion(f32[3,8192]{1,0:T(4,128)} %bitcast.50, pred[8,8192]{1,0:T(8,128)(4,1)S(1)} %iota_compare_fusion), kind=kLoop, calls=%fused_computation.76 | loop fusion | flops 393192 | bytes 163936 | tf_op jit(solution)/shard_map/reduce_sum | solution.py:447
  15.2 1.3 %copy.59 = f32[3,17,45,1]{3,2,1,0:T(8,128)S(1)} copy(f32[3,17,45,1]{2,3,1,0:T(1,128)} %param.7) | data formatting | bytes 18360 | tf_op args[1]
  16.5 0.9 fusion.1
  18.1 0.9 fusion.58
  20.5 12.3 %shard_map.78 = (f32[3,1,1,129]{3,2,1,0:T(1,128)}, f32[3,1,45,129]{3,2,1,0:T(8,128)}, f32[3,1,1,129]{3,2,1,0:T(1,128)}, f32[51,129]{1,0:T(8,128)}, f32[51,129]{1...) custom-call(f32[3,1,1,129]{3,2,1,0:T(1,128)} %get-tuple-element.73.refs_0_, ...), custom_call_target="tpu_custom_call" | custom-call | tf_op jit(solution)/shard_map/pallas_call | solution.py:282
  32.8 0.9 maximum_bitcast_fusion
  33.8 0.9 maximum_bitcast_fusion.1
  34.7 0.9 transpose_reshape.8
  35.6 0.9 transpose_reshape.9
  36.5 2.7 %fusion.2 = f32[3,17,47,129]{3,2,1,0:T(8,128)S(1)} fusion(f32[3,17,1,129]{3,2,1,0:T(1,128)S(1)} %transpose_reshape.9, f32[3,17,45,129]{3,2,1,0:T(8,128)} %copy-done, f32[3,17,1,129]{3,2,1,0:T(1,128)S(1)} %transpose_reshape.8, f32[3,47,129]{2,1,0:T(8,128)S(1)} %maximum_bitcast_fusion.1, f32[3,47,129]{2,1,0:T(8,128)S(1)} %maximum_bitcast_fusion, ...), kind=kLoop, calls=%fused_computation.6 | loop fusion | flops 2473704 | bytes 2619318 | tf_op jit(solution)/shard_map/add | solution.py:349
  39.4 0.8 fusion
  42.2 6.8 %shard_map.79 = (f32[51,45]{1,0:T(8,128)}, f32[51,45]{1,0:T(8,128)}) custom-call(f32[51,45]{1,0:T(8,128)} %reshape_transpose.14.low, f32[51,45]{1,0:T(8,128)} %reshape_transpose.15.high), custom_call_target="tpu_custom_call" | custom-call | tf_op jit(solution)/shard_map/pallas_call | solution.py:90
  49.0 0.8 broadcast_in_dim.204
  49.8 0.8 broadcast_in_dim.207
  50.5 1.3 %multiply_add_fusion = f32[3,17,45,129]{3,2,1,0:T(8,128)S(1)} fusion(f32[3,17,45]{2,1,0:T(8,128)S(1)} %broadcast_in_dim.207, f32[3,17,45]{2,1,0:T(8,128)S(1)} %broadcast_in_dim.204, f32[129]{0:T(256)S(1)} %and_select_fusion.16, pred[129]{0:T(512)(128)(4,1)S(1)} %get-tuple-element.108, pred[129]{0:T(512)(128)(4,1)S(1)} %get-tuple-element.109, ...), kind=kLoop, calls=%fused_computation.7 | loop fusion | flops 3552660 | bytes 2440476 | tf_op jit(solution)/shard_map/add | solution.py:349
  51.9 0.9 fusion.55
  53.1 2.7 %pad_maximum_fusion.shifted = f32[4,3,17,48,128]{4,3,2,1,0:T(8,128)} fusion(f32[1,3,17,48,128]{4,3,2,1,0:T(8,128)S(1)} %pad_bitcast_fusion, f32[1,3,17,48,128]{4,3,2,1,0:T(8,128)S(1)} %pad_bitcast_fusion.1, f32[1,3,17,48,128]{4,3,2,1,0:T(8,128)S(1)} %pad_bitcast_fusion.2, f32[1,3,17,48,128]{4,3,2,1,0:T(8,128)S(1)} %pad_bitcast_fusion.3), kind=kLoop, calls=%fused_computation | loop fusion | flops 3760128 | bytes 10027008 | tf_op jit(solution)/shard_map/stack | solution.py:386
  55.8 15.3 %shard_map.80 = f32[16,48,128]{2,1,0:T(8,128)} custom-call(f32[24,24]{1,0:T(8,128)} %stiffness.1, f32[4,3,17,48,128]{4,3,2,1,0:T(8,128)} %pad_maximum_fusion.shifted), custom_call_target="tpu_custom_call" | custom-call | tf_op jit(solution)/shard_map/pallas_call | solution.py:394
  71.1 1.1 %fusion.30 = (f32[1,16,44,128]{3,2,1,0:T(8,128)S(1)}, f32[1,16,44,128]{3,2,1,0:T(8,128)S(1)}) fusion(f32[16,48,128]{2,1,0:T(8,128)} %shard_map.80, f32[16,44,128]{2,0,1:T(8,128)S(1)} %copy-done.1), kind=kLoop, calls=%fused_computation.83 | loop fusion | flops 360448 | bytes 1441792 | tf_op jit(solution)/shard_map/stack | solution.py:464
  72.9 0.7 fusion.31
  74.3 15.1 %shard_map.81 = (f32[2,3,3,128]{3,2,1,0:T(4,128)}, f32[2,3,44,128]{3,2,1,0:T(8,128)}, f32[2,3,3,128]{3,2,1,0:T(4,128)}, f32[2,16,3,128]{3,2,1,0:T(4,128)}, f32[2...) custom-call(f32[2,3,3,128]{3,2,1,0:T(4,128)} %get-tuple-element.85.refs_0, ...), custom_call_target="tpu_custom_call" | custom-call | tf_op jit(solution)/shard_map/pallas_call | solution.py:282
  89.4 1.4 %maximum_maximum_fusion = (f32[2,19,50,128]{3,2,1,0:T(8,128)S(1)}, f32[2,19,50,128]{3,2,1,0:T(8,128)S(1)}) fusion(f32[2,16,3,128]{3,2,1,0:T(4,128)} %get-tuple-element.36, f32[1,16,44,128]{3,2,1,0:T(8,128)S(1)} %get-tuple-element.91, f32[1,16,44,128]{3,2,1,0:T(8,128)S(1)} %get-tuple-element.90, f32[2,16,3,128]{3,2,1,0:T(4,128)} %get-tuple-element.35, ...), kind=kLoop, calls=%fused_computation.34 | loop fusion | flops 2918400 | bytes 3072000 | tf_op jit(solution)/shard_map/concatenate | solution.py:296
  92.2 1.0 copy.62
  93.2 1.0 copy.63
  94.1 7.1 %shard_map.82 = (f32[96,44]{1,0:T(8,128)}, f32[96,44]{1,0:T(8,128)}) custom-call(f32[96,44]{1,0:T(8,128)} %bitcast.51, f32[96,44]{1,0:T(8,128)} %bitcast.52), custom_call_target="tpu_custom_call" | custom-call | tf_op jit(solution)/shard_map/pallas_call | solution.py:90
  101.2 1.2 %copy.64 = f32[3,2,16,44]{0,3,2,1:T(8,128)S(1)} copy(f32[3,2,16,44]{3,2,1,0:T(8,128)} %bitcast.54) | data formatting | bytes 33792 | tf_op jit(solution)/shard_map/reshape | solution.py:313
  102.4 1.2 %copy.65 = f32[3,2,16,44]{0,3,2,1:T(8,128)S(1)} copy(f32[3,2,16,44]{3,2,1,0:T(8,128)} %bitcast.53) | data formatting | bytes 33792 | tf_op jit(solution)/shard_map/reshape | solution.py:314
  103.6 2.3 %fusion.11 = f32[2,16,44,128]{3,2,1,0:T(8,128)S(1)} fusion(f32[2,16,44,128]{3,2,1,0:T(8,128)S(1)} %slice_add_fusion.1, f32[2,16,44,3]{3,2,1,0:T(8,128)S(1)} %bitcast.45, f32[2,16,44,3]{3,2,1,0:T(8,128)S(1)} %bitcast.44), kind=kLoop, calls=%fused_computation.50 | loop fusion | flops 3063808 | bytes 1475584 | tf_op jit(solution)/shard_map/add | solution.py:409
  106.3 0.8 copy.67
  107.1 0.8 copy.68
  (46 shorter events, 8.1 us)
Async XLA Ops:
  0.6 15.9 %copy-start.2 = (f32[3,17,45,128]{3,2,1,0:T(8,128)S(1)}, f32[3,17,45,128]{3,2,1,0:T(8,128)}, u32[]{:S(2)}) copy-start(f32[3,17,45,128]{3,2,1,0:T(8,128)} %param.6) | copy-start | bytes 3525124
  17.4 1.6 %copy-start = (f32[3,17,45,129]{3,2,1,0:T(8,128)}, f32[3,17,45,129]{3,2,1,0:T(8,128)S(1)}, u32[]{:S(2)}) copy-start(f32[3,17,45,129]{3,2,1,0:T(8,128)S(1)} %fusion.1) | copy-start | bytes 3552664
  55.8 15.3 %copy-start.1 = (f32[16,44,128]{2,0,1:T(8,128)S(1)}, f32[16,44,128]{2,0,1:T(8,128)}, u32[]{:S(2)}) copy-start(f32[16,44,128]{2,0,1:T(8,128)} %param.10) | copy-start | bytes 1081348
  89.4 1.4 %copy-start.3 = (f32[2,16,3,128]{3,2,1,0:T(4,128)S(1)}, f32[2,16,3,128]{3,2,1,0:T(4,128)}, u32[]{:S(2)}) copy-start(f32[2,16,3,128]{3,2,1,0:T(4,128)} %get-tuple-element.35) | copy-start | bytes 147460
  89.4 1.4 %copy-start.4 = (f32[2,16,3,128]{3,2,1,0:T(4,128)S(1)}, f32[2,16,3,128]{3,2,1,0:T(4,128)}, u32[]{:S(2)}) copy-start(f32[2,16,3,128]{3,2,1,0:T(4,128)} %get-tuple-element.36) | copy-start | bytes 147460

commit v12 on v11

--- a/solution.py
+++ b/solution.py
@@ -371,7 +371,11 @@
                     inner = inner + weights[a * 24 + b] * vectors[b]
                 term = vectors[a] * inner
                 total = term if total is None else total + term
-            out[i, pl.ds(first, 8), :] = total
+            if first % 8 == 0:
+                out[i, pl.ds(first, 8), :] = total
+            else:
+                keep = 8 - first % 8
+                out[i, pl.ds(first + 8 - keep, keep), :] = total[8 - keep :]
         return carry
 
     lax.fori_loop(0, count_x, row, 0)
@@ -381,24 +385,22 @@
     count_x = nodes.shape[1] - 1
     count_y = nodes.shape[2] - 1
     count_z = nodes.shape[3] - 1
-    rows = -(-count_y // 8) * 8
-    pad = ((0, 0), (0, 0), (0, rows - count_y), (0, 0))
     shifted = jnp.stack(
-        [
-            jnp.pad(nodes[:, :, dy : dy + count_y, dz : dz + count_z], pad)
-            for dy, dz in ((0, 0), (1, 0), (0, 1), (1, 1))
-        ]
+        [nodes[:, :, dy : dy + count_y, dz : dz + count_z] for dy, dz in ((0, 0), (1, 0), (0, 1), (1, 1))]
     )
-    kernel = functools.partial(energy_kernel, count_x=count_x, chunks=tuple(range(0, rows, 8)))
+    chunks = tuple(range(0, count_y - 7, 8))
+    if count_y % 8:
+        chunks = chunks + (count_y - 8,)
+    kernel = functools.partial(energy_kernel, count_x=count_x, chunks=chunks)
     vmem = pl.BlockSpec(memory_space=pltpu.VMEM)
     energy = pl.pallas_call(
         kernel,
-        out_shape=jax.ShapeDtypeStruct((count_x, rows, count_z), jnp.float32),
+        out_shape=jax.ShapeDtypeStruct((count_x, count_y, count_z), jnp.float32),
         in_specs=[pl.BlockSpec(memory_space=pltpu.SMEM), vmem],
         out_specs=vmem,
         scratch_shapes=[pltpu.SMEM((24 * 24,), jnp.float32)],
     )(stiffness, shifted)
-    return energy[:, :count_y, :]
+    return energy
 
 
 def smooth(field, axis, count):

time: 109 us -> 109 us (level)
  no operation moved by 1% of the time
where the time goes in v12:
time: 109 us; the launch traced here: 108 us
  Pallas kernels  68.8 us (63%)
  other arithmetic  20.9 us (19%)
  local copies, waits for them, and re-layouts  17.1 us (16%)
    pallas_call x2, Pallas kernels, with_plane_halo(): pl.pallas_call(kernel, out_shape=shapes, in_specs=[vmem] * len(pieces), o...  27.4 us
    pallas_call x1, Pallas kernels, element_energy(): pl.pallas_call(kernel, out_shape=jax.ShapeDtypeStruct((count_x, count_y,...  15.3 us
    pallas_call x2, Pallas kernels, exchange(): pl.pallas_call(kernel, out_shape=(slab, slab), in_specs=[vmem, vmem], out...  13.9 us
    pallas_call x1, Pallas kernels, gather_peers(): pl.pallas_call(kernel, out_shape=jax.ShapeDtypeStruct(stacked, shard.dtyp...  12.2 us
    add x3, other arithmetic, average_rows(): return own_rows * factor + rim_part * 0.5  4.87 us
    add x3, other arithmetic, smooth(): summed = term_value if summed is None else summed + term_value  3.36 us
    another operation x4, other arithmetic, local(): smoothed = filter_field(jnp.stack([density * sens, density]), sides)  3.18 us
    unnamed x15, local copies, waits for them, and re-layouts  3.03 us

profile of v12, /device:TPU:29, one launch (start us, length us, event | category | flops | bytes accessed | tf_op | source)
XLA Modules:
  0.0 107.7 jit_solution(5330773024020632318)
XLA Ops:
  0.6 12.2 %shard_map.77 = f32[16,3,512]{2,1,0:T(4,128)} custom-call(f32[3,512]{1,0:T(4,128)} %shard.1), custom_call_target="tpu_custom_call" | custom-call | tf_op jit(solution)/shard_map/pallas_call | solution.py:157
  12.8 0.8 iota_compare_fusion
  13.6 1.1 %select_reduce_fusion = f32[3,8]{1,0:T(4,128)S(1)} fusion(f32[3,8192]{1,0:T(4,128)} %bitcast.50, pred[8,8192]{1,0:T(8,128)(4,1)S(1)} %iota_compare_fusion), kind=kLoop, calls=%fused_computation.76 | loop fusion | flops 393192 | bytes 163936 | tf_op jit(solution)/shard_map/reduce_sum | solution.py:449
  15.2 1.3 %copy.59 = f32[3,17,45,1]{3,2,1,0:T(8,128)S(1)} copy(f32[3,17,45,1]{2,3,1,0:T(1,128)} %param.7) | data formatting | bytes 18360 | tf_op args[1]
  16.5 0.9 fusion.1
  18.1 0.9 fusion.57
  20.5 12.3 %shard_map.78 = (f32[3,1,1,129]{3,2,1,0:T(1,128)}, f32[3,1,45,129]{3,2,1,0:T(8,128)}, f32[3,1,1,129]{3,2,1,0:T(1,128)}, f32[51,129]{1,0:T(8,128)}, f32[51,129]{1...) custom-call(f32[3,1,1,129]{3,2,1,0:T(1,128)} %get-tuple-element.73.refs_0_, ...), custom_call_target="tpu_custom_call" | custom-call | tf_op jit(solution)/shard_map/pallas_call | solution.py:282
  32.8 0.9 maximum_bitcast_fusion
  33.8 0.9 maximum_bitcast_fusion.1
  34.7 0.9 transpose_reshape.8
  35.6 0.9 transpose_reshape.9
  36.5 2.7 %fusion.2 = f32[3,17,47,129]{3,2,1,0:T(8,128)S(1)} fusion(f32[3,17,1,129]{3,2,1,0:T(1,128)S(1)} %transpose_reshape.9, f32[3,17,45,129]{3,2,1,0:T(8,128)} %copy-done, f32[3,17,1,129]{3,2,1,0:T(1,128)S(1)} %transpose_reshape.8, f32[3,47,129]{2,1,0:T(8,128)S(1)} %maximum_bitcast_fusion.1, f32[3,47,129]{2,1,0:T(8,128)S(1)} %maximum_bitcast_fusion, ...), kind=kLoop, calls=%fused_computation.6 | loop fusion | flops 2473704 | bytes 2619318 | tf_op jit(solution)/shard_map/add | solution.py:349
  39.4 0.8 fusion
  42.2 6.8 %shard_map.79 = (f32[51,45]{1,0:T(8,128)}, f32[51,45]{1,0:T(8,128)}) custom-call(f32[51,45]{1,0:T(8,128)} %reshape_transpose.14.low, f32[51,45]{1,0:T(8,128)} %reshape_transpose.15.high), custom_call_target="tpu_custom_call" | custom-call | tf_op jit(solution)/shard_map/pallas_call | solution.py:90
  49.0 0.8 broadcast_in_dim.204
  49.8 0.8 broadcast_in_dim.207
  50.5 1.3 %multiply_add_fusion = f32[3,17,45,129]{3,2,1,0:T(8,128)S(1)} fusion(f32[3,17,45]{2,1,0:T(8,128)S(1)} %broadcast_in_dim.207, f32[3,17,45]{2,1,0:T(8,128)S(1)} %broadcast_in_dim.204, f32[129]{0:T(256)S(1)} %and_select_fusion.16, pred[129]{0:T(512)(128)(4,1)S(1)} %get-tuple-element.108, pred[129]{0:T(512)(128)(4,1)S(1)} %get-tuple-element.109, ...), kind=kLoop, calls=%fused_computation.7 | loop fusion | flops 3552660 | bytes 2440476 | tf_op jit(solution)/shard_map/add | solution.py:349
  51.9 0.9 slice_bitcast_fusion.3
  52.7 2.8 %pad_maximum_fusion.shifted = f32[4,3,17,44,128]{4,3,2,1,0:T(8,128)} fusion(f32[1,3,17,44,128]{4,3,2,1,0:T(8,128)S(1)} %get-tuple-element.65, f32[1,3,17,44,128]{4,3,2,1,0:T(8,128)S(1)} %get-tuple-element.66, f32[1,3,17,44,128]{4,3,2,1,0:T(8,128)S(1)} %get-tuple-element.67, f32[1,3,17,44,128]{4,3,2,1,0:T(8,128)S(1)} %get-tuple-element.64), kind=kLoop, calls=%fused_computation | loop fusion | flops 3446784 | bytes 9191424 | tf_op jit(solution)/shard_map/stack | solution.py:388
  55.5 15.3 %shard_map.80 = f32[16,44,128]{2,1,0:T(8,128)} custom-call(f32[24,24]{1,0:T(8,128)} %stiffness.1, f32[4,3,17,44,128]{4,3,2,1,0:T(8,128)} %pad_maximum_fusion.shifted), custom_call_target="tpu_custom_call" | custom-call | tf_op jit(solution)/shard_map/pallas_call | solution.py:396
  70.8 1.1 %fusion.30 = (f32[1,16,44,128]{3,2,1,0:T(8,128)S(1)}, f32[1,16,44,128]{3,2,1,0:T(8,128)S(1)}) fusion(f32[16,44,128]{2,1,0:T(8,128)} %shard_map.80, f32[16,44,128]{2,0,1:T(8,128)S(1)} %copy-done.1), kind=kLoop, calls=%fused_computation.83 | loop fusion | flops 360448 | bytes 1441792 | tf_op jit(solution)/shard_map/stack | solution.py:466
  72.7 0.7 fusion.31
  74.0 15.1 %shard_map.81 = (f32[2,3,3,128]{3,2,1,0:T(4,128)}, f32[2,3,44,128]{3,2,1,0:T(8,128)}, f32[2,3,3,128]{3,2,1,0:T(4,128)}, f32[2,16,3,128]{3,2,1,0:T(4,128)}, f32[2...) custom-call(f32[2,3,3,128]{3,2,1,0:T(4,128)} %get-tuple-element.85.refs_0, ...), custom_call_target="tpu_custom_call" | custom-call | tf_op jit(solution)/shard_map/pallas_call | solution.py:282
  89.2 1.4 %maximum_maximum_fusion = (f32[2,19,50,128]{3,2,1,0:T(8,128)S(1)}, f32[2,19,50,128]{3,2,1,0:T(8,128)S(1)}) fusion(f32[2,16,3,128]{3,2,1,0:T(4,128)} %get-tuple-element.36, f32[1,16,44,128]{3,2,1,0:T(8,128)S(1)} %get-tuple-element.91, f32[1,16,44,128]{3,2,1,0:T(8,128)S(1)} %get-tuple-element.90, f32[2,16,3,128]{3,2,1,0:T(4,128)} %get-tuple-element.35, ...), kind=kLoop, calls=%fused_computation.34 | loop fusion | flops 2918400 | bytes 3072000 | tf_op jit(solution)/shard_map/concatenate | solution.py:296
  92.0 1.0 copy.62
  92.9 1.0 copy.63
  93.9 7.1 %shard_map.82 = (f32[96,44]{1,0:T(8,128)}, f32[96,44]{1,0:T(8,128)}) custom-call(f32[96,44]{1,0:T(8,128)} %bitcast.51, f32[96,44]{1,0:T(8,128)} %bitcast.52), custom_call_target="tpu_custom_call" | custom-call | tf_op jit(solution)/shard_map/pallas_call | solution.py:90
  101.0 1.2 %copy.64 = f32[3,2,16,44]{0,3,2,1:T(8,128)S(1)} copy(f32[3,2,16,44]{3,2,1,0:T(8,128)} %bitcast.54) | data formatting | bytes 33792 | tf_op jit(solution)/shard_map/reshape | solution.py:313
  102.2 1.2 %copy.65 = f32[3,2,16,44]{0,3,2,1:T(8,128)S(1)} copy(f32[3,2,16,44]{3,2,1,0:T(8,128)} %bitcast.53) | data formatting | bytes 33792 | tf_op jit(solution)/shard_map/reshape | solution.py:314
  103.4 2.3 %fusion.11 = f32[2,16,44,128]{3,2,1,0:T(8,128)S(1)} fusion(f32[2,16,44,128]{3,2,1,0:T(8,128)S(1)} %slice_add_fusion.1, f32[2,16,44,3]{3,2,1,0:T(8,128)S(1)} %bitcast.45, f32[2,16,44,3]{3,2,1,0:T(8,128)S(1)} %bitcast.44), kind=kLoop, calls=%fused_computation.50 | loop fusion | flops 3063808 | bytes 1475584 | tf_op jit(solution)/shard_map/add | solution.py:411
  106.0 0.8 copy.67
  106.9 0.8 copy.68
  (42 shorter events, 7.8 us)
Async XLA Ops:
  0.6 15.9 %copy-start.2 = (f32[3,17,45,128]{3,2,1,0:T(8,128)S(1)}, f32[3,17,45,128]{3,2,1,0:T(8,128)}, u32[]{:S(2)}) copy-start(f32[3,17,45,128]{3,2,1,0:T(8,128)} %param.6) | copy-start | bytes 3525124
  17.4 1.6 %copy-start = (f32[3,17,45,129]{3,2,1,0:T(8,128)}, f32[3,17,45,129]{3,2,1,0:T(8,128)S(1)}, u32[]{:S(2)}) copy-start(f32[3,17,45,129]{3,2,1,0:T(8,128)S(1)} %fusion.1) | copy-start | bytes 3552664
  55.5 15.3 %copy-start.1 = (f32[16,44,128]{2,0,1:T(8,128)S(1)}, f32[16,44,128]{2,0,1:T(8,128)}, u32[]{:S(2)}) copy-start(f32[16,44,128]{2,0,1:T(8,128)} %param.10) | copy-start | bytes 1081348
  89.2 1.4 %copy-start.3 = (f32[2,16,3,128]{3,2,1,0:T(4,128)S(1)}, f32[2,16,3,128]{3,2,1,0:T(4,128)}, u32[]{:S(2)}) copy-start(f32[2,16,3,128]{3,2,1,0:T(4,128)} %get-tuple-element.35) | copy-start | bytes 147460
  89.2 1.4 %copy-start.4 = (f32[2,16,3,128]{3,2,1,0:T(4,128)S(1)}, f32[2,16,3,128]{3,2,1,0:T(4,128)}, u32[]{:S(2)}) copy-start(f32[2,16,3,128]{3,2,1,0:T(4,128)} %get-tuple-element.36) | copy-start | bytes 147460

commit v13 on v12

--- a/solution.py
+++ b/solution.py
@@ -349,8 +349,8 @@
     return own_rows * factor + rim_part * 0.5
 
 
-def energy_kernel(stiffness, shifted, out, weights, *, count_x, chunks):
-    sources = (shifted.at[0], shifted.at[2], shifted.at[1], shifted.at[3])
+def energy_kernel(stiffness, base, up_y, up_z, up_yz, out, weights, *, count_x, chunks):
+    sources = (base, up_z, up_y, up_yz)
     for a in range(24):
         weights[a * 24 + a] = stiffness[a, a]
         for b in range(a + 1, 24):
@@ -385,9 +385,7 @@
     count_x = nodes.shape[1] - 1
     count_y = nodes.shape[2] - 1
     count_z = nodes.shape[3] - 1
-    shifted = jnp.stack(
-        [nodes[:, :, dy : dy + count_y, dz : dz + count_z] for dy, dz in ((0, 0), (1, 0), (0, 1), (1, 1))]
-    )
+    shifted = [nodes[:, :, dy : dy + count_y, dz : dz + count_z] for dy, dz in ((0, 0), (1, 0), (0, 1), (1, 1))]
     chunks = tuple(range(0, count_y - 7, 8))
     if count_y % 8:
         chunks = chunks + (count_y - 8,)
@@ -396,10 +394,10 @@
     energy = pl.pallas_call(
         kernel,
         out_shape=jax.ShapeDtypeStruct((count_x, count_y, count_z), jnp.float32),
-        in_specs=[pl.BlockSpec(memory_space=pltpu.SMEM), vmem],
+        in_specs=[pl.BlockSpec(memory_space=pltpu.SMEM)] + [vmem] * 4,
         out_specs=vmem,
         scratch_shapes=[pltpu.SMEM((24 * 24,), jnp.float32)],
-    )(stiffness, shifted)
+    )(stiffness, *shifted)
     return energy
 
 

time: 109 us -> 108 us (level)
  other arithmetic: 20.9 us -> 18 us
  local copies, waits for them, and re-layouts: 17.1 us -> 19.3 us
    slice x0 -> x1, local copies, waits for them, and re-layouts: none -> 3.05 us  [element_energy(): nodes[:, :, dy:dy + count_y, dz:dz + count_z]]
    another operation x1 -> x0, other arithmetic: 2.82 us -> none  [element_energy(): jnp.stack([nodes[:, :, dy:dy + count_y, dz:dz + count_z] for dy, dz in ((...]
where the time goes in v13:
time: 108 us; the launch traced here: 107 us
  Pallas kernels  69 us (64%)
  local copies, waits for them, and re-layouts  19.3 us (18%)
  other arithmetic  18 us (17%)
    pallas_call x2, Pallas kernels, with_plane_halo(): pl.pallas_call(kernel, out_shape=shapes, in_specs=[vmem] * len(pieces), o...  27.4 us
    pallas_call x1, Pallas kernels, element_energy(): pl.pallas_call(kernel, out_shape=jax.ShapeDtypeStruct((count_x, count_y,...  15.5 us
    pallas_call x2, Pallas kernels, exchange(): pl.pallas_call(kernel, out_shape=(slab, slab), in_specs=[vmem, vmem], out...  13.9 us
    pallas_call x1, Pallas kernels, gather_peers(): pl.pallas_call(kernel, out_shape=jax.ShapeDtypeStruct(stacked, shard.dtyp...  12.2 us
    add x3, other arithmetic, average_rows(): return own_rows * factor + rim_part * 0.5  4.87 us
    add x3, other arithmetic, smooth(): summed = term_value if summed is None else summed + term_value  3.36 us
    another operation x4, other arithmetic, local(): smoothed = filter_field(jnp.stack([density * sens, density]), sides)  3.18 us
    slice x1, local copies, waits for them, and re-layouts, element_energy(): nodes[:, :, dy:dy + count_y, dz:dz + count_z]  3.05 us

profile of v13, /device:TPU:29, one launch (start us, length us, event | category | flops | bytes accessed | tf_op | source)
XLA Modules:
  0.0 107.3 jit_solution(8212958502169753615)
XLA Ops:
  0.6 12.2 %shard_map.77 = f32[16,3,512]{2,1,0:T(4,128)} custom-call(f32[3,512]{1,0:T(4,128)} %shard.1), custom_call_target="tpu_custom_call" | custom-call | tf_op jit(solution)/shard_map/pallas_call | solution.py:157
  12.8 0.8 iota_compare_fusion
  13.6 1.1 %select_reduce_fusion = f32[3,8]{1,0:T(4,128)S(1)} fusion(f32[3,8192]{1,0:T(4,128)} %bitcast.42, pred[8,8192]{1,0:T(8,128)(4,1)S(1)} %iota_compare_fusion), kind=kLoop, calls=%fused_computation.71 | loop fusion | flops 393192 | bytes 163936 | tf_op jit(solution)/shard_map/reduce_sum | solution.py:447
  15.2 1.3 %copy.59 = f32[3,17,45,1]{3,2,1,0:T(8,128)S(1)} copy(f32[3,17,45,1]{2,3,1,0:T(1,128)} %param.7) | data formatting | bytes 18360 | tf_op args[1]
  16.5 0.9 fusion.1
  18.1 0.9 fusion.58
  20.5 12.3 %shard_map.78 = (f32[3,1,1,129]{3,2,1,0:T(1,128)}, f32[3,1,45,129]{3,2,1,0:T(8,128)}, f32[3,1,1,129]{3,2,1,0:T(1,128)}, f32[51,129]{1,0:T(8,128)}, f32[51,129]{1...) custom-call(f32[3,1,1,129]{3,2,1,0:T(1,128)} %get-tuple-element.73.refs_0_, ...), custom_call_target="tpu_custom_call" | custom-call | tf_op jit(solution)/shard_map/pallas_call | solution.py:282
  32.8 0.9 maximum_bitcast_fusion
  33.8 0.9 maximum_bitcast_fusion.1
  34.7 0.9 transpose_reshape.8
  35.6 0.9 transpose_reshape.9
  36.5 2.7 %fusion.2 = f32[3,17,47,129]{3,2,1,0:T(8,128)S(1)} fusion(f32[3,17,1,129]{3,2,1,0:T(1,128)S(1)} %transpose_reshape.9, f32[3,17,45,129]{3,2,1,0:T(8,128)} %copy-done, f32[3,17,1,129]{3,2,1,0:T(1,128)S(1)} %transpose_reshape.8, f32[3,47,129]{2,1,0:T(8,128)S(1)} %maximum_bitcast_fusion.1, f32[3,47,129]{2,1,0:T(8,128)S(1)} %maximum_bitcast_fusion, ...), kind=kLoop, calls=%fused_computation.5 | loop fusion | flops 2473704 | bytes 2619318 | tf_op jit(solution)/shard_map/add | solution.py:349
  39.4 0.8 fusion
  40.3 0.7 slice_reduce_fusion
  42.2 6.8 %shard_map.79 = (f32[51,45]{1,0:T(8,128)}, f32[51,45]{1,0:T(8,128)}) custom-call(f32[51,45]{1,0:T(8,128)} %reshape_transpose.14.low, f32[51,45]{1,0:T(8,128)} %reshape_transpose.15.high), custom_call_target="tpu_custom_call" | custom-call | tf_op jit(solution)/shard_map/pallas_call | solution.py:90
  49.0 0.8 broadcast_in_dim.204
  49.8 0.8 broadcast_in_dim.207
  50.5 1.3 %multiply_add_fusion = f32[3,17,45,129]{3,2,1,0:T(8,128)S(1)} fusion(f32[3,17,45]{2,1,0:T(8,128)S(1)} %broadcast_in_dim.207, f32[3,17,45]{2,1,0:T(8,128)S(1)} %broadcast_in_dim.204, f32[129]{0:T(256)S(1)} %and_select_fusion.16, pred[129]{0:T(512)(128)(4,1)S(1)} %get-tuple-element.108, pred[129]{0:T(512)(128)(4,1)S(1)} %get-tuple-element.109, ...), kind=kLoop, calls=%fused_computation.6 | loop fusion | flops 3552660 | bytes 2440476 | tf_op jit(solution)/shard_map/add | solution.py:349
  51.9 3.1 %fusion.55 = (f32[3,17,44,128]{3,2,1,0:T(8,128)}, f32[3,17,44,128]{3,2,1,0:T(8,128)}, f32[3,17,44,128]{3,2,1,0:T(8,128)}, f32[3,17,44,128]{3,2,1,0:T(8,128)}) fusion(f32[3,17,45,129]{3,2,1,0:T(8,128)S(1)} %multiply_add_fusion), kind=kLoop, calls=%fused_computation.169 | loop fusion | bytes 9191424 | tf_op jit(solution)/shard_map/slice | solution.py:388
  54.9 15.5 %shard_map.80 = f32[16,44,128]{2,1,0:T(8,128)} custom-call(f32[24,24]{1,0:T(8,128)} %stiffness.1, f32[3,17,44,128]{3,2,1,0:T(8,128)} %get-tuple-element.67.base, f32[3,17,44,128]{3,2,1,0:T(8,128)} %get-tuple-element.66.up_y, f32[3,17,44,128]{3,2,1,0:T(8,128)} %get-tuple-element.65.up_z, f32[3,17,44,128]{3,2,1,0:T(8,128)} %get-tuple-element.64.up_yz), custom_call_target="tpu_custom_call" | custom-call | tf_op jit(solution)/shard_map/pallas_call | solution.py:394
  70.4 1.1 %fusion.30 = (f32[1,16,44,128]{3,2,1,0:T(8,128)S(1)}, f32[1,16,44,128]{3,2,1,0:T(8,128)S(1)}) fusion(f32[16,44,128]{2,1,0:T(8,128)} %shard_map.80, f32[16,44,128]{2,0,1:T(8,128)S(1)} %copy-done.1), kind=kLoop, calls=%fused_computation.78 | loop fusion | flops 360448 | bytes 1441792 | tf_op jit(solution)/shard_map/stack | solution.py:464
  72.3 0.7 fusion.31
  73.6 15.1 %shard_map.81 = (f32[2,3,3,128]{3,2,1,0:T(4,128)}, f32[2,3,44,128]{3,2,1,0:T(8,128)}, f32[2,3,3,128]{3,2,1,0:T(4,128)}, f32[2,16,3,128]{3,2,1,0:T(4,128)}, f32[2...) custom-call(f32[2,3,3,128]{3,2,1,0:T(4,128)} %get-tuple-element.85.refs_0, ...), custom_call_target="tpu_custom_call" | custom-call | tf_op jit(solution)/shard_map/pallas_call | solution.py:282
  88.8 1.4 %maximum_maximum_fusion = (f32[2,19,50,128]{3,2,1,0:T(8,128)S(1)}, f32[2,19,50,128]{3,2,1,0:T(8,128)S(1)}) fusion(f32[2,16,3,128]{3,2,1,0:T(4,128)} %get-tuple-element.36, f32[1,16,44,128]{3,2,1,0:T(8,128)S(1)} %get-tuple-element.91, f32[1,16,44,128]{3,2,1,0:T(8,128)S(1)} %get-tuple-element.90, f32[2,16,3,128]{3,2,1,0:T(4,128)} %get-tuple-element.35, ...), kind=kLoop, calls=%fused_computation.29 | loop fusion | flops 2918400 | bytes 3072000 | tf_op jit(solution)/shard_map/concatenate | solution.py:296
  91.5 1.0 copy.63
  92.5 1.0 copy.62
  93.5 7.1 %shard_map.82 = (f32[96,44]{1,0:T(8,128)}, f32[96,44]{1,0:T(8,128)}) custom-call(f32[96,44]{1,0:T(8,128)} %bitcast.44, f32[96,44]{1,0:T(8,128)} %bitcast.43), custom_call_target="tpu_custom_call" | custom-call | tf_op jit(solution)/shard_map/pallas_call | solution.py:90
  100.6 1.2 %copy.64 = f32[3,2,16,44]{0,3,2,1:T(8,128)S(1)} copy(f32[3,2,16,44]{3,2,1,0:T(8,128)} %bitcast.46) | data formatting | bytes 33792 | tf_op jit(solution)/shard_map/reshape | solution.py:313
  101.8 1.2 %copy.65 = f32[3,2,16,44]{0,3,2,1:T(8,128)S(1)} copy(f32[3,2,16,44]{3,2,1,0:T(8,128)} %bitcast.45) | data formatting | bytes 33792 | tf_op jit(solution)/shard_map/reshape | solution.py:314
  103.0 2.3 %fusion.11 = f32[2,16,44,128]{3,2,1,0:T(8,128)S(1)} fusion(f32[2,16,44,128]{3,2,1,0:T(8,128)S(1)} %slice_add_fusion.1, f32[2,16,44,3]{3,2,1,0:T(8,128)S(1)} %bitcast.37, f32[2,16,44,3]{3,2,1,0:T(8,128)S(1)} %bitcast.36), kind=kLoop, calls=%fused_computation.45 | loop fusion | flops 3063808 | bytes 1475584 | tf_op jit(solution)/shard_map/add | solution.py:409
  105.6 0.8 copy.67
  106.5 0.8 copy.68
  (41 shorter events, 7.0 us)
Async XLA Ops:
  0.6 15.9 %copy-start.2 = (f32[3,17,45,128]{3,2,1,0:T(8,128)S(1)}, f32[3,17,45,128]{3,2,1,0:T(8,128)}, u32[]{:S(2)}) copy-start(f32[3,17,45,128]{3,2,1,0:T(8,128)} %param.6) | copy-start | bytes 3525124
  17.4 1.6 %copy-start = (f32[3,17,45,129]{3,2,1,0:T(8,128)}, f32[3,17,45,129]{3,2,1,0:T(8,128)S(1)}, u32[]{:S(2)}) copy-start(f32[3,17,45,129]{3,2,1,0:T(8,128)S(1)} %fusion.1) | copy-start | bytes 3552664
  54.9 15.5 %copy-start.1 = (f32[16,44,128]{2,0,1:T(8,128)S(1)}, f32[16,44,128]{2,0,1:T(8,128)}, u32[]{:S(2)}) copy-start(f32[16,44,128]{2,0,1:T(8,128)} %param.10) | copy-start | bytes 1081348
  88.7 1.4 %copy-start.3 = (f32[2,16,3,128]{3,2,1,0:T(4,128)S(1)}, f32[2,16,3,128]{3,2,1,0:T(4,128)}, u32[]{:S(2)}) copy-start(f32[2,16,3,128]{3,2,1,0:T(4,128)} %get-tuple-element.35) | copy-start | bytes 147460
  88.8 1.4 %copy-start.4 = (f32[2,16,3,128]{3,2,1,0:T(4,128)S(1)}, f32[2,16,3,128]{3,2,1,0:T(4,128)}, u32[]{:S(2)}) copy-start(f32[2,16,3,128]{3,2,1,0:T(4,128)} %get-tuple-element.36) | copy-start | bytes 147460

commit v14 on v13

--- a/solution.py
+++ b/solution.py
@@ -349,8 +349,7 @@
     return own_rows * factor + rim_part * 0.5
 
 
-def energy_kernel(stiffness, base, up_y, up_z, up_yz, out, weights, *, count_x, chunks):
-    sources = (base, up_z, up_y, up_yz)
+def energy_kernel(stiffness, nodes, out, weights, *, count_x, chunks):
     for a in range(24):
         weights[a * 24 + a] = stiffness[a, a]
         for b in range(a + 1, 24):
@@ -362,8 +361,9 @@
             for component in range(3):
                 for corner in range(8):
                     shift_x = corner // 4
-                    source = sources[corner % 4]
-                    vectors.append(source[component, i + shift_x, pl.ds(first, 8), :])
+                    shift_y = corner // 2 % 2
+                    shift_z = corner % 2
+                    vectors.append(nodes[component, i + shift_x, pl.ds(first + shift_y, 8), pl.ds(shift_z, 128)])
             total = None
             for a in range(24):
                 inner = weights[a * 24 + a] * vectors[a]
@@ -385,7 +385,6 @@
     count_x = nodes.shape[1] - 1
     count_y = nodes.shape[2] - 1
     count_z = nodes.shape[3] - 1
-    shifted = [nodes[:, :, dy : dy + count_y, dz : dz + count_z] for dy, dz in ((0, 0), (1, 0), (0, 1), (1, 1))]
     chunks = tuple(range(0, count_y - 7, 8))
     if count_y % 8:
         chunks = chunks + (count_y - 8,)
@@ -394,10 +393,10 @@
     energy = pl.pallas_call(
         kernel,
         out_shape=jax.ShapeDtypeStruct((count_x, count_y, count_z), jnp.float32),
-        in_specs=[pl.BlockSpec(memory_space=pltpu.SMEM)] + [vmem] * 4,
+        in_specs=[pl.BlockSpec(memory_space=pltpu.SMEM), vmem],
         out_specs=vmem,
         scratch_shapes=[pltpu.SMEM((24 * 24,), jnp.float32)],
-    )(stiffness, *shifted)
+    )(stiffness, nodes)
     return energy
 
 

time: 108 us -> 195 us (1.81)
  Pallas kernels: 69 us -> 157 us
  local copies, waits for them, and re-layouts: 19.3 us -> 16.3 us
    pallas_call x1, Pallas kernels: 15.5 us -> 104 us  [element_energy(): pl.pallas_call(kernel, out_shape=jax.ShapeDtypeStruct((count_x, count_y,...]
    slice x1 -> x0, local copies, waits for them, and re-layouts: 3.05 us -> none  [element_energy(): nodes[:, :, dy:dy + count_y, dz:dz + count_z]]
where the time goes in v14:
time: 195 us; the launch traced here: 194 us
  Pallas kernels  157 us (81%)
  other arithmetic  19.3 us (10%)
  local copies, waits for them, and re-layouts  16.3 us (8%)
    pallas_call x1, Pallas kernels, element_energy(): pl.pallas_call(kernel, out_shape=jax.ShapeDtypeStruct((count_x, count_y,...  104 us
    pallas_call x2, Pallas kernels, with_plane_halo(): pl.pallas_call(kernel, out_shape=shapes, in_specs=[vmem] * len(pieces), o...  27.4 us
    pallas_call x2, Pallas kernels, exchange(): pl.pallas_call(kernel, out_shape=(slab, slab), in_specs=[vmem, vmem], out...  13.9 us
    pallas_call x1, Pallas kernels, gather_peers(): pl.pallas_call(kernel, out_shape=jax.ShapeDtypeStruct(stacked, shard.dtyp...  12.2 us
    add x3, other arithmetic, average_rows(): return own_rows * factor + rim_part * 0.5  6.09 us

profile of v14, /device:TPU:29, one launch (start us, length us, event | category | flops | bytes accessed | tf_op | source)
XLA Modules:
  0.0 193.9 jit_solution(9784140140705102824)
XLA Ops:
  0.6 12.2 %shard_map.77 = f32[16,3,512]{2,1,0:T(4,128)} custom-call(f32[3,512]{1,0:T(4,128)} %shard.1), custom_call_target="tpu_custom_call" | custom-call | tf_op jit(solution)/shard_map/pallas_call | solution.py:157
  12.8 0.8 iota_compare_fusion
  13.6 1.1 select_reduce_fusion
  15.2 1.3 copy.59
  16.5 0.9 fusion.1
  18.1 0.9 fusion.57
  20.5 12.3 %shard_map.78 = (f32[3,1,1,129]{3,2,1,0:T(1,128)}, f32[3,1,45,129]{3,2,1,0:T(8,128)}, f32[3,1,1,129]{3,2,1,0:T(1,128)}, f32[51,129]{1,0:T(8,128)}, f32[51,129]{1...) custom-call(f32[3,1,1,129]{3,2,1,0:T(1,128)} %get-tuple-element.69.refs_0_, ...), custom_call_target="tpu_custom_call" | custom-call | tf_op jit(solution)/shard_map/pallas_call | solution.py:282
  32.8 0.9 maximum_bitcast_fusion
  33.8 0.9 maximum_bitcast_fusion.1
  34.7 0.9 transpose_reshape.8
  35.6 0.9 transpose_reshape.9
  36.5 2.7 %fusion.2 = f32[3,17,47,129]{3,2,1,0:T(8,128)S(1)} fusion(f32[3,17,1,129]{3,2,1,0:T(1,128)S(1)} %transpose_reshape.9, f32[3,17,45,129]{3,2,1,0:T(8,128)} %copy-done, f32[3,17,1,129]{3,2,1,0:T(1,128)S(1)} %transpose_reshape.8, f32[3,47,129]{2,1,0:T(8,128)S(1)} %maximum_bitcast_fusion.1, f32[3,47,129]{2,1,0:T(8,128)S(1)} %maximum_bitcast_fusion, ...), kind=kLoop, calls=%fused_computation.5 | loop fusion | flops 2473704 | bytes 2619318 | tf_op jit(solution)/shard_map/add | solution.py:349
  39.4 0.8 fusion
  40.3 0.7 slice_reduce_fusion
  42.2 6.8 %shard_map.79 = (f32[51,45]{1,0:T(8,128)}, f32[51,45]{1,0:T(8,128)}) custom-call(f32[51,45]{1,0:T(8,128)} %reshape_transpose.14.low, f32[51,45]{1,0:T(8,128)} %reshape_transpose.15.high), custom_call_target="tpu_custom_call" | custom-call | tf_op jit(solution)/shard_map/pallas_call | solution.py:90
  49.0 0.8 broadcast_in_dim.204
  49.8 0.8 broadcast_in_dim.207
  50.5 2.5 %multiply_add_fusion.nodes = f32[3,17,45,129]{3,2,1,0:T(8,128)} fusion(f32[3,17,45]{2,1,0:T(8,128)S(1)} %broadcast_in_dim.207, f32[3,17,45]{2,1,0:T(8,128)S(1)} %broadcast_in_dim.204, f32[129]{0:T(256)S(1)} %and_select_fusion.16, pred[129]{0:T(512)(128)(4,1)S(1)} %get-tuple-element.104, pred[129]{0:T(512)(128)(4,1)S(1)} %get-tuple-element.105, ...), kind=kLoop, calls=%fused_computation.6 | loop fusion | flops 3552660 | bytes 2440476 | tf_op jit(solution)/shard_map/add | solution.py:349
  53.1 104.0 %shard_map.80 = f32[16,44,128]{2,1,0:T(8,128)} custom-call(f32[24,24]{1,0:T(8,128)} %stiffness.1, f32[3,17,45,129]{3,2,1,0:T(8,128)} %multiply_add_fusion.nodes), custom_call_target="tpu_custom_call" | custom-call | tf_op jit(solution)/shard_map/pallas_call | solution.py:393
  157.0 1.1 fusion.30
  158.2 0.7 fusion.34
  158.9 0.7 fusion.31
  160.2 15.1 %shard_map.81 = (f32[2,3,3,128]{3,2,1,0:T(4,128)}, f32[2,3,44,128]{3,2,1,0:T(8,128)}, f32[2,3,3,128]{3,2,1,0:T(4,128)}, f32[2,16,3,128]{3,2,1,0:T(4,128)}, f32[2...) custom-call(f32[2,3,3,128]{3,2,1,0:T(4,128)} %get-tuple-element.81.refs_0, ...), custom_call_target="tpu_custom_call" | custom-call | tf_op jit(solution)/shard_map/pallas_call | solution.py:282
  175.4 1.4 maximum_maximum_fusion
  178.1 1.0 copy.63
  179.1 1.0 copy.62
  180.1 7.1 %shard_map.82 = (f32[96,44]{1,0:T(8,128)}, f32[96,44]{1,0:T(8,128)}) custom-call(f32[96,44]{1,0:T(8,128)} %bitcast.44, f32[96,44]{1,0:T(8,128)} %bitcast.43), custom_call_target="tpu_custom_call" | custom-call | tf_op jit(solution)/shard_map/pallas_call | solution.py:90
  187.2 1.2 copy.64
  188.4 1.2 copy.65
  189.6 2.3 %fusion.11 = f32[2,16,44,128]{3,2,1,0:T(8,128)S(1)} fusion(f32[2,16,44,128]{3,2,1,0:T(8,128)S(1)} %slice_add_fusion.1, f32[2,16,44,3]{3,2,1,0:T(8,128)S(1)} %bitcast.37, f32[2,16,44,3]{3,2,1,0:T(8,128)S(1)} %bitcast.36), kind=kLoop, calls=%fused_computation.45 | loop fusion | flops 3063808 | bytes 1475584 | tf_op jit(solution)/shard_map/add | solution.py:408
  192.2 0.8 copy.67
  193.1 0.8 copy.68
  (40 shorter events, 6.3 us)
Async XLA Ops:
  0.6 15.9 %copy-start.2 = (f32[3,17,45,128]{3,2,1,0:T(8,128)S(1)}, f32[3,17,45,128]{3,2,1,0:T(8,128)}, u32[]{:S(2)}) copy-start(f32[3,17,45,128]{3,2,1,0:T(8,128)} %param.6) | copy-start | bytes 3525124
  17.4 1.6 copy-start
  53.1 104.0 %copy-start.1 = (f32[16,44,128]{2,0,1:T(8,128)S(1)}, f32[16,44,128]{2,0,1:T(8,128)}, u32[]{:S(2)}) copy-start(f32[16,44,128]{2,0,1:T(8,128)} %param.10) | copy-start | bytes 1081348
  175.3 1.4 copy-start.3
  175.4 1.4 copy-start.4

commit v15 on v13

--- a/solution.py
+++ b/solution.py
@@ -241,7 +241,8 @@
 
 
 def as_rows(piece, thin):
-    tiled = math.prod(piece.shape[:-2]) * -(-piece.shape[-2] // 8) * 8 * -(-piece.shape[-1] // 128) * 128
+    sublanes = 1 if piece.shape[-2] == 1 else -(-piece.shape[-2] // 8) * 8
+    tiled = math.prod(piece.shape[:-2]) * sublanes * -(-piece.shape[-1] // 128) * 128
     if tiled <= 3 * piece.size or tiled <= 65536:
         return piece, None
     moved = jnp.moveaxis(piece, thin, tuple(range(len(thin))))

time: 108 us -> 105 us (0.972)
  local copies, waits for them, and re-layouts: 19.3 us -> 16.8 us
    another operation x4 -> x0, local copies, waits for them, and re-layouts: 3.02 us -> none  [the longest x2 1.75 us: from_rows(): return jnp.moveaxis(piece.reshape(moved), tuple(range(len(thin))), thin)]
where the time goes in v15:
time: 105 us
  Pallas kernels  68.9 us (66%)
  other arithmetic  18.1 us (17%)
  local copies, waits for them, and re-layouts  16.8 us (16%)
    pallas_call x2, Pallas kernels, with_plane_halo(): pl.pallas_call(kernel, out_shape=shapes, in_specs=[vmem] * len(pieces), o...  27.3 us
    pallas_call x1, Pallas kernels, element_energy(): pl.pallas_call(kernel, out_shape=jax.ShapeDtypeStruct((count_x, count_y,...  15.5 us
    pallas_call x2, Pallas kernels, exchange(): pl.pallas_call(kernel, out_shape=(slab, slab), in_specs=[vmem, vmem], out...  13.9 us
    pallas_call x1, Pallas kernels, gather_peers(): pl.pallas_call(kernel, out_shape=jax.ShapeDtypeStruct(stacked, shard.dtyp...  12.2 us
    add x3, other arithmetic, average_rows(): return own_rows * factor + rim_part * 0.5  4.89 us
    add x3, other arithmetic, smooth(): summed = term_value if summed is None else summed + term_value  3.36 us
    another operation x4, other arithmetic, local(): smoothed = filter_field(jnp.stack([density * sens, density]), sides)  3.18 us
    slice x1, local copies, waits for them, and re-layouts, element_energy(): nodes[:, :, dy:dy + count_y, dz:dz + count_z]  3.05 us

profile of v15, /device:TPU:29, one launch (start us, length us, event | category | flops | bytes accessed | tf_op | source)
XLA Modules:
  0.0 104.6 jit_solution(15547192863566674595)
XLA Ops:
  0.6 12.2 %shard_map.77 = f32[16,3,512]{2,1,0:T(4,128)} custom-call(f32[3,512]{1,0:T(4,128)} %shard.1), custom_call_target="tpu_custom_call" | custom-call | tf_op jit(solution)/shard_map/pallas_call | solution.py:157
  12.8 0.8 iota_compare_fusion
  13.6 1.1 %select_reduce_fusion = f32[3,8]{1,0:T(4,128)S(1)} fusion(f32[3,8192]{1,0:T(4,128)} %bitcast.42, pred[8,8192]{1,0:T(8,128)(4,1)S(1)} %iota_compare_fusion), kind=kLoop, calls=%fused_computation.71 | loop fusion | flops 393192 | bytes 163936 | tf_op jit(solution)/shard_map/reduce_sum | solution.py:448
  15.2 1.3 %copy.59 = f32[3,17,45,1]{3,2,1,0:T(8,128)S(1)} copy(f32[3,17,45,1]{2,3,1,0:T(1,128)} %param.7) | data formatting | bytes 18360 | tf_op args[1]
  16.5 0.9 fusion.1
  18.1 0.9 fusion.58
  19.0 0.7 fusion.59
  19.7 12.3 %shard_map.78 = (f32[3,1,1,129]{3,2,1,0:T(1,128)}, f32[3,1,45,129]{3,2,1,0:T(8,128)}, f32[3,1,1,129]{3,2,1,0:T(1,128)}, f32[3,17,1,129]{3,2,1,0:T(1,128)}, f32[3...) custom-call(f32[3,1,1,129]{3,2,1,0:T(1,128)} %get-tuple-element.71.refs_0, ...), custom_call_target="tpu_custom_call" | custom-call | tf_op jit(solution)/shard_map/pallas_call | solution.py:283
  32.0 0.9 maximum_bitcast_fusion
  33.0 0.9 maximum_bitcast_fusion.1
  34.0 2.8 %fusion.2 = f32[3,17,47,129]{3,2,1,0:T(8,128)S(1)} fusion(f32[3,17,1,129]{3,2,1,0:T(1,128)} %get-tuple-element.23, f32[3,17,45,129]{3,2,1,0:T(8,128)} %copy-done, f32[3,17,1,129]{3,2,1,0:T(1,128)} %get-tuple-element.22, f32[3,47,129]{2,1,0:T(8,128)S(1)} %maximum_bitcast_fusion.1, f32[3,47,129]{2,1,0:T(8,128)S(1)} %maximum_bitcast_fusion, ...), kind=kLoop, calls=%fused_computation.5 | loop fusion | flops 2473704 | bytes 2619318 | tf_op jit(solution)/shard_map/add | solution.py:350
  36.9 0.8 fusion
  37.7 0.7 slice_reduce_fusion
  39.7 6.8 %shard_map.79 = (f32[51,45]{1,0:T(8,128)}, f32[51,45]{1,0:T(8,128)}) custom-call(f32[51,45]{1,0:T(8,128)} %reshape_transpose.6.low, f32[51,45]{1,0:T(8,128)} %reshape_transpose.7.high), custom_call_target="tpu_custom_call" | custom-call | tf_op jit(solution)/shard_map/pallas_call | solution.py:90
  46.5 0.8 broadcast_in_dim.204
  47.2 0.8 broadcast_in_dim.207
  48.0 1.3 %multiply_add_fusion = f32[3,17,45,129]{3,2,1,0:T(8,128)S(1)} fusion(f32[3,17,45]{2,1,0:T(8,128)S(1)} %broadcast_in_dim.207, f32[3,17,45]{2,1,0:T(8,128)S(1)} %broadcast_in_dim.204, f32[129]{0:T(256)S(1)} %and_select_fusion.16, pred[129]{0:T(512)(128)(4,1)S(1)} %get-tuple-element.108, pred[129]{0:T(512)(128)(4,1)S(1)} %get-tuple-element.109, ...), kind=kLoop, calls=%fused_computation.6 | loop fusion | flops 3552660 | bytes 2440476 | tf_op jit(solution)/shard_map/add | solution.py:350
  49.3 3.1 %fusion.55 = (f32[3,17,44,128]{3,2,1,0:T(8,128)}, f32[3,17,44,128]{3,2,1,0:T(8,128)}, f32[3,17,44,128]{3,2,1,0:T(8,128)}, f32[3,17,44,128]{3,2,1,0:T(8,128)}) fusion(f32[3,17,45,129]{3,2,1,0:T(8,128)S(1)} %multiply_add_fusion), kind=kLoop, calls=%fused_computation.167 | loop fusion | bytes 9191424 | tf_op jit(solution)/shard_map/slice | solution.py:389
  52.4 15.5 %shard_map.80 = f32[16,44,128]{2,1,0:T(8,128)} custom-call(f32[24,24]{1,0:T(8,128)} %stiffness.1, f32[3,17,44,128]{3,2,1,0:T(8,128)} %get-tuple-element.65.base, f32[3,17,44,128]{3,2,1,0:T(8,128)} %get-tuple-element.64.up_y, f32[3,17,44,128]{3,2,1,0:T(8,128)} %get-tuple-element.63.up_z, f32[3,17,44,128]{3,2,1,0:T(8,128)} %get-tuple-element.62.up_yz), custom_call_target="tpu_custom_call" | custom-call | tf_op jit(solution)/shard_map/pallas_call | solution.py:395
  67.9 1.1 %fusion.30 = (f32[1,16,44,128]{3,2,1,0:T(8,128)S(1)}, f32[1,16,44,128]{3,2,1,0:T(8,128)S(1)}) fusion(f32[16,44,128]{2,1,0:T(8,128)} %shard_map.80, f32[16,44,128]{2,0,1:T(8,128)S(1)} %copy-done.1), kind=kLoop, calls=%fused_computation.78 | loop fusion | flops 360448 | bytes 1441792 | tf_op jit(solution)/shard_map/stack | solution.py:465
  69.0 0.7 fusion.34
  69.7 0.7 fusion.31
  71.1 15.0 %shard_map.81 = (f32[2,3,3,128]{3,2,1,0:T(4,128)}, f32[2,3,44,128]{3,2,1,0:T(8,128)}, f32[2,3,3,128]{3,2,1,0:T(4,128)}, f32[2,16,3,128]{3,2,1,0:T(4,128)}, f32[2...) custom-call(f32[2,3,3,128]{3,2,1,0:T(4,128)} %get-tuple-element.85.refs_0, ...), custom_call_target="tpu_custom_call" | custom-call | tf_op jit(solution)/shard_map/pallas_call | solution.py:283
  86.1 1.4 %maximum_maximum_fusion = (f32[2,19,50,128]{3,2,1,0:T(8,128)S(1)}, f32[2,19,50,128]{3,2,1,0:T(8,128)S(1)}) fusion(f32[2,16,3,128]{3,2,1,0:T(4,128)} %get-tuple-element.36, f32[1,16,44,128]{3,2,1,0:T(8,128)S(1)} %get-tuple-element.91, f32[1,16,44,128]{3,2,1,0:T(8,128)S(1)} %get-tuple-element.90, f32[2,16,3,128]{3,2,1,0:T(4,128)} %get-tuple-element.35, ...), kind=kLoop, calls=%fused_computation.29 | loop fusion | flops 2918400 | bytes 3072000 | tf_op jit(solution)/shard_map/concatenate | solution.py:297
  88.8 1.0 copy.63
  89.8 1.0 copy.62
  90.8 7.1 %shard_map.82 = (f32[96,44]{1,0:T(8,128)}, f32[96,44]{1,0:T(8,128)}) custom-call(f32[96,44]{1,0:T(8,128)} %bitcast.44, f32[96,44]{1,0:T(8,128)} %bitcast.43), custom_call_target="tpu_custom_call" | custom-call | tf_op jit(solution)/shard_map/pallas_call | solution.py:90
  97.9 1.2 %copy.64 = f32[3,2,16,44]{0,3,2,1:T(8,128)S(1)} copy(f32[3,2,16,44]{3,2,1,0:T(8,128)} %bitcast.46) | data formatting | bytes 33792 | tf_op jit(solution)/shard_map/reshape | solution.py:314
  99.1 1.2 %copy.65 = f32[3,2,16,44]{0,3,2,1:T(8,128)S(1)} copy(f32[3,2,16,44]{3,2,1,0:T(8,128)} %bitcast.45) | data formatting | bytes 33792 | tf_op jit(solution)/shard_map/reshape | solution.py:315
  100.3 2.3 %fusion.11 = f32[2,16,44,128]{3,2,1,0:T(8,128)S(1)} fusion(f32[2,16,44,128]{3,2,1,0:T(8,128)S(1)} %slice_add_fusion.1, f32[2,16,44,3]{3,2,1,0:T(8,128)S(1)} %bitcast.37, f32[2,16,44,3]{3,2,1,0:T(8,128)S(1)} %bitcast.36), kind=kLoop, calls=%fused_computation.45 | loop fusion | flops 3063808 | bytes 1475584 | tf_op jit(solution)/shard_map/add | solution.py:410
  102.9 0.8 copy.67
  103.8 0.8 copy.68
  (37 shorter events, 4.8 us)
Async XLA Ops:
  0.6 15.9 %copy-start.2 = (f32[3,17,45,128]{3,2,1,0:T(8,128)S(1)}, f32[3,17,45,128]{3,2,1,0:T(8,128)}, u32[]{:S(2)}) copy-start(f32[3,17,45,128]{3,2,1,0:T(8,128)} %param.6) | copy-start | bytes 3525124
  17.4 1.6 %copy-start = (f32[3,17,45,129]{3,2,1,0:T(8,128)}, f32[3,17,45,129]{3,2,1,0:T(8,128)S(1)}, u32[]{:S(2)}) copy-start(f32[3,17,45,129]{3,2,1,0:T(8,128)S(1)} %fusion.1) | copy-start | bytes 3552664
  52.4 15.5 %copy-start.1 = (f32[16,44,128]{2,0,1:T(8,128)S(1)}, f32[16,44,128]{2,0,1:T(8,128)}, u32[]{:S(2)}) copy-start(f32[16,44,128]{2,0,1:T(8,128)} %param.10) | copy-start | bytes 1081348
  86.0 1.4 %copy-start.3 = (f32[2,16,3,128]{3,2,1,0:T(4,128)S(1)}, f32[2,16,3,128]{3,2,1,0:T(4,128)}, u32[]{:S(2)}) copy-start(f32[2,16,3,128]{3,2,1,0:T(4,128)} %get-tuple-element.35) | copy-start | bytes 147460
  86.1 1.4 %copy-start.4 = (f32[2,16,3,128]{3,2,1,0:T(4,128)S(1)}, f32[2,16,3,128]{3,2,1,0:T(4,128)}, u32[]{:S(2)}) copy-start(f32[2,16,3,128]{3,2,1,0:T(4,128)} %get-tuple-element.36) | copy-start | bytes 147460

commit v16 on v15

--- a/solution.py
+++ b/solution.py
@@ -443,9 +443,8 @@
     sides = (("gx", 1), ("gy", 2), ("gz", 3))
     wanted = corner_dofs.reshape(8)
     gathered = gather_peers(coarse_solution, "gz")
-    columns = gathered.transpose(1, 0, 2).reshape(coarse_solution.shape[0], -1)
-    matches = wanted[:, None] == jnp.arange(columns.shape[1], dtype=jnp.int32)[None, :]
-    corner_vals = jnp.sum(jnp.where(matches[None], columns[:, None, :], 0.0), axis=2)
+    width = coarse_solution.shape[1]
+    corner_vals = gathered[wanted // width, :, wanted % width].T
     depth = local_solution.shape[3]
     full = jnp.concatenate([local_solution, top_nodes], axis=3)
     nodes = recover(full, corner_vals, jnp.arange(depth + 1, dtype=jnp.float32) / depth)

time: 105 us -> 107 us (1.019)
  local copies, waits for them, and re-layouts: 16.8 us -> 20.5 us
  other arithmetic: 18.1 us -> 16.2 us
    pallas_call x0 -> x1, local copies, waits for them, and re-layouts: none -> 3.54 us  [gather_peers(): pl.pallas_call(kernel, out_shape=jax.ShapeDtypeStruct(stacked, shard.dtyp...]
    gather x0 -> x1, local copies, waits for them, and re-layouts: none -> 1.26 us  [local(): corner_vals = gathered[wanted // width, :, wanted % width].T]
    reduce_sum x1 -> x0, other arithmetic: 1.11 us -> none  [local(): jnp.sum(jnp.where(matches[None], columns[:, None, :], 0.0), axis=2)]
    unnamed x15 -> x19, local copies, waits for them, and re-layouts: 3.03 us -> 2.31 us
where the time goes in v16:
time: 107 us; the launch traced here: 106 us
  Pallas kernels  68.8 us (64%)
  local copies, waits for them, and re-layouts  20.5 us (19%)
  other arithmetic  16.2 us (15%)
    pallas_call x2, Pallas kernels, with_plane_halo(): pl.pallas_call(kernel, out_shape=shapes, in_specs=[vmem] * len(pieces), o...  27.2 us
    pallas_call x1, Pallas kernels, element_energy(): pl.pallas_call(kernel, out_shape=jax.ShapeDtypeStruct((count_x, count_y,...  15.5 us
    pallas_call x2, Pallas kernels, exchange(): pl.pallas_call(kernel, out_shape=(slab, slab), in_specs=[vmem, vmem], out...  13.9 us
    pallas_call x1, Pallas kernels, gather_peers(): pl.pallas_call(kernel, out_shape=jax.ShapeDtypeStruct(stacked, shard.dtyp...  12.1 us
    add x3, other arithmetic, average_rows(): return own_rows * factor + rim_part * 0.5  4.89 us
    pallas_call x1, local copies, waits for them, and re-layouts, gather_peers(): pl.pallas_call(kernel, out_shape=jax.ShapeDtypeStruct(stacked, shard.dtyp...  3.54 us
    add x3, other arithmetic, smooth(): summed = term_value if summed is None else summed + term_value  3.36 us
    another operation x4, other arithmetic, local(): smoothed = filter_field(jnp.stack([density * sens, density]), sides)  3.16 us

profile of v16, /device:TPU:29, one launch (start us, length us, event | category | flops | bytes accessed | tf_op | source)
XLA Modules:
  0.0 106.4 jit_solution(16556416979784348724)
XLA Ops:
  0.7 12.1 %shard_map.77 = f32[16,3,512]{2,1,0:T(4,128)} custom-call(f32[3,512]{1,0:T(4,128)} %shard.1), custom_call_target="tpu_custom_call" | custom-call | tf_op jit(solution)/shard_map/pallas_call | solution.py:157
  12.8 3.5 %copy.38 = f32[16,3,512]{1,2,0:T(8,128)} copy(f32[16,3,512]{2,1,0:T(4,128)} %shard_map.77) | data formatting | bytes 196608 | tf_op jit(solution)/shard_map/pallas_call | solution.py:157
  16.3 1.3 %gather_fusion = f32[8,3]{1,0:T(8,128)S(1)} fusion(f32[16,3,512]{1,2,0:T(8,128)} %copy.38, s32[8]{0:T(128)S(1)} %fusion.60), kind=kCustom, calls=%fused_computation | custom fusion | bytes 256 | tf_op jit(solution)/shard_map/gather | solution.py:447
  18.4 0.9 fusion.1
  19.3 0.7 fusion.63
  20.0 0.9 fusion.64
  20.9 0.7 fusion.65
  21.6 12.3 %shard_map.78 = (f32[3,1,1,129]{3,2,1,0:T(1,128)}, f32[3,1,45,129]{3,2,1,0:T(8,128)}, f32[3,1,1,129]{3,2,1,0:T(1,128)}, f32[3,17,1,129]{3,2,1,0:T(1,128)}, f32[3...) custom-call(f32[3,1,1,129]{3,2,1,0:T(1,128)} %get-tuple-element.59.refs_0, ...), custom_call_target="tpu_custom_call" | custom-call | tf_op jit(solution)/shard_map/pallas_call | solution.py:283
  33.9 0.9 maximum_bitcast_fusion
  34.8 0.9 maximum_bitcast_fusion.1
  35.8 2.8 %fusion.2 = f32[3,17,47,129]{3,2,1,0:T(8,128)S(1)} fusion(f32[3,17,1,129]{3,2,1,0:T(1,128)} %get-tuple-element.23, f32[3,17,45,129]{3,2,1,0:T(8,128)} %copy-done, f32[3,17,1,129]{3,2,1,0:T(1,128)} %get-tuple-element.22, f32[3,47,129]{2,1,0:T(8,128)S(1)} %maximum_bitcast_fusion.1, f32[3,47,129]{2,1,0:T(8,128)S(1)} %maximum_bitcast_fusion, ...), kind=kLoop, calls=%fused_computation.6 | loop fusion | flops 2473704 | bytes 2619318 | tf_op jit(solution)/shard_map/add | solution.py:350
  38.8 0.8 fusion
  39.6 0.7 slice_reduce_fusion
  41.5 6.8 %shard_map.79 = (f32[51,45]{1,0:T(8,128)}, f32[51,45]{1,0:T(8,128)}) custom-call(f32[51,45]{1,0:T(8,128)} %reshape_transpose.6.low, f32[51,45]{1,0:T(8,128)} %reshape_transpose.7.high), custom_call_target="tpu_custom_call" | custom-call | tf_op jit(solution)/shard_map/pallas_call | solution.py:90
  48.3 0.8 broadcast_in_dim.178
  49.1 0.8 broadcast_in_dim.181
  49.9 1.3 %multiply_add_fusion = f32[3,17,45,129]{3,2,1,0:T(8,128)S(1)} fusion(f32[3,17,45]{2,1,0:T(8,128)S(1)} %broadcast_in_dim.181, f32[3,17,45]{2,1,0:T(8,128)S(1)} %broadcast_in_dim.178, f32[129]{0:T(256)S(1)} %and_select_fusion.16, pred[129]{0:T(512)(128)(4,1)S(1)} %get-tuple-element.104, pred[129]{0:T(512)(128)(4,1)S(1)} %get-tuple-element.105, ...), kind=kLoop, calls=%fused_computation.7 | loop fusion | flops 3552660 | bytes 2440476 | tf_op jit(solution)/shard_map/add | solution.py:350
  51.2 3.0 %fusion.61 = (f32[3,17,44,128]{3,2,1,0:T(8,128)}, f32[3,17,44,128]{3,2,1,0:T(8,128)}, f32[3,17,44,128]{3,2,1,0:T(8,128)}, f32[3,17,44,128]{3,2,1,0:T(8,128)}) fusion(f32[3,17,45,129]{3,2,1,0:T(8,128)S(1)} %multiply_add_fusion), kind=kLoop, calls=%fused_computation.180 | loop fusion | bytes 9191424 | tf_op jit(solution)/shard_map/slice | solution.py:389
  54.2 15.5 %shard_map.80 = f32[16,44,128]{2,1,0:T(8,128)} custom-call(f32[24,24]{1,0:T(8,128)} %stiffness.1, f32[3,17,44,128]{3,2,1,0:T(8,128)} %get-tuple-element.53.base, f32[3,17,44,128]{3,2,1,0:T(8,128)} %get-tuple-element.52.up_y, f32[3,17,44,128]{3,2,1,0:T(8,128)} %get-tuple-element.51.up_z, f32[3,17,44,128]{3,2,1,0:T(8,128)} %get-tuple-element.50.up_yz), custom_call_target="tpu_custom_call" | custom-call | tf_op jit(solution)/shard_map/pallas_call | solution.py:395
  69.7 1.1 %fusion.30 = (f32[1,16,44,128]{3,2,1,0:T(8,128)S(1)}, f32[1,16,44,128]{3,2,1,0:T(8,128)S(1)}) fusion(f32[16,44,128]{2,1,0:T(8,128)} %shard_map.80, f32[16,44,128]{2,0,1:T(8,128)S(1)} %copy-done.1), kind=kLoop, calls=%fused_computation.78 | loop fusion | flops 360448 | bytes 1441792 | tf_op jit(solution)/shard_map/stack | solution.py:464
  70.9 0.7 fusion.34
  71.5 0.7 fusion.31
  72.9 14.9 %shard_map.81 = (f32[2,3,3,128]{3,2,1,0:T(4,128)}, f32[2,3,44,128]{3,2,1,0:T(8,128)}, f32[2,3,3,128]{3,2,1,0:T(4,128)}, f32[2,16,3,128]{3,2,1,0:T(4,128)}, f32[2...) custom-call(f32[2,3,3,128]{3,2,1,0:T(4,128)} %get-tuple-element.73.refs_0, ...), custom_call_target="tpu_custom_call" | custom-call | tf_op jit(solution)/shard_map/pallas_call | solution.py:283
  87.9 1.4 %maximum_maximum_fusion = (f32[2,19,50,128]{3,2,1,0:T(8,128)S(1)}, f32[2,19,50,128]{3,2,1,0:T(8,128)S(1)}) fusion(f32[2,16,3,128]{3,2,1,0:T(4,128)} %get-tuple-element.36, f32[1,16,44,128]{3,2,1,0:T(8,128)S(1)} %get-tuple-element.79, f32[1,16,44,128]{3,2,1,0:T(8,128)S(1)} %get-tuple-element.78, f32[2,16,3,128]{3,2,1,0:T(4,128)} %get-tuple-element.35, ...), kind=kLoop, calls=%fused_computation.30 | loop fusion | flops 2918400 | bytes 3072000 | tf_op jit(solution)/shard_map/concatenate | solution.py:297
  90.7 1.0 copy.41
  91.6 1.0 copy.42
  92.6 7.1 %shard_map.82 = (f32[96,44]{1,0:T(8,128)}, f32[96,44]{1,0:T(8,128)}) custom-call(f32[96,44]{1,0:T(8,128)} %bitcast.72, f32[96,44]{1,0:T(8,128)} %bitcast.73), custom_call_target="tpu_custom_call" | custom-call | tf_op jit(solution)/shard_map/pallas_call | solution.py:90
  99.7 1.2 %copy.43 = f32[3,2,16,44]{0,3,2,1:T(8,128)S(1)} copy(f32[3,2,16,44]{3,2,1,0:T(8,128)} %bitcast.75) | data formatting | bytes 33792 | tf_op jit(solution)/shard_map/reshape | solution.py:314
  100.9 1.2 %copy.44 = f32[3,2,16,44]{0,3,2,1:T(8,128)S(1)} copy(f32[3,2,16,44]{3,2,1,0:T(8,128)} %bitcast.74) | data formatting | bytes 33792 | tf_op jit(solution)/shard_map/reshape | solution.py:315
  102.1 2.3 %fusion.11 = f32[2,16,44,128]{3,2,1,0:T(8,128)S(1)} fusion(f32[2,16,44,128]{3,2,1,0:T(8,128)S(1)} %slice_add_fusion.1, f32[2,16,44,3]{3,2,1,0:T(8,128)S(1)} %bitcast.67, f32[2,16,44,3]{3,2,1,0:T(8,128)S(1)} %bitcast.66), kind=kLoop, calls=%fused_computation.46 | loop fusion | flops 3063808 | bytes 1475584 | tf_op jit(solution)/shard_map/add | solution.py:410
  104.7 0.8 copy.46
  105.6 0.8 copy.47
  (42 shorter events, 4.4 us)
Async XLA Ops:
  0.6 15.7 %copy-start.6 = (s32[1,1,1,8]{3,2,1,0:T(1,128)S(1)}, s32[1,1,1,8]{3,2,1,0:T(1,128)}, u32[]{:S(2)}) copy-start(s32[1,1,1,8]{3,2,1,0:T(1,128)} %param.9) | copy-start | bytes 100
  0.6 17.2 %copy-start.5 = (f32[3,17,45,1]{2,3,1,0:T(1,128)S(1)}, f32[3,17,45,1]{2,3,1,0:T(1,128)}, u32[]{:S(2)}) copy-start(f32[3,17,45,1]{2,3,1,0:T(1,128)} %param.7) | copy-start | bytes 27544
  12.8 5.6 %copy-start.2 = (f32[3,17,45,128]{3,2,1,0:T(8,128)S(1)}, f32[3,17,45,128]{3,2,1,0:T(8,128)}, u32[]{:S(2)}) copy-start(f32[3,17,45,128]{3,2,1,0:T(8,128)} %param.6) | copy-start | bytes 3525124
  19.3 1.6 %copy-start = (f32[3,17,45,129]{3,2,1,0:T(8,128)}, f32[3,17,45,129]{3,2,1,0:T(8,128)S(1)}, u32[]{:S(2)}) copy-start(f32[3,17,45,129]{3,2,1,0:T(8,128)S(1)} %fusion.1) | copy-start | bytes 3552664
  54.2 15.5 %copy-start.1 = (f32[16,44,128]{2,0,1:T(8,128)S(1)}, f32[16,44,128]{2,0,1:T(8,128)}, u32[]{:S(2)}) copy-start(f32[16,44,128]{2,0,1:T(8,128)} %param.10) | copy-start | bytes 1081348
  87.8 1.4 %copy-start.3 = (f32[2,16,3,128]{3,2,1,0:T(4,128)S(1)}, f32[2,16,3,128]{3,2,1,0:T(4,128)}, u32[]{:S(2)}) copy-start(f32[2,16,3,128]{3,2,1,0:T(4,128)} %get-tuple-element.35) | copy-start | bytes 147460
  87.9 1.4 %copy-start.4 = (f32[2,16,3,128]{3,2,1,0:T(4,128)S(1)}, f32[2,16,3,128]{3,2,1,0:T(4,128)}, u32[]{:S(2)}) copy-start(f32[2,16,3,128]{3,2,1,0:T(4,128)} %get-tuple-element.36) | copy-start | bytes 147460

commit v17 on v15

--- a/solution.py
+++ b/solution.py
@@ -1,4 +1,5 @@
 import functools
+import itertools
 import math
 
 import jax
@@ -255,8 +256,9 @@
     return jnp.moveaxis(piece.reshape(moved), tuple(range(len(thin))), thin)
 
 
-def with_plane_halo(shard, axes, dims, width):
-    offsets = [(ox, oy) for ox in (-1, 0, 1) for oy in (-1, 0, 1) if (ox, oy) != (0, 0)]
+def with_box_halo(shard, axes, dims, width):
+    steps = (-1, 0, 1)
+    offsets = [offset for offset in itertools.product(steps, repeat=len(axes)) if any(offset)]
     pieces = []
     layouts = []
     for offset in offsets:
@@ -273,7 +275,7 @@
         piece, moved = as_rows(piece, thin)
         pieces.append(piece)
         layouts.append((moved, thin))
-    key = ("plane",) + tuple(piece.shape for piece in pieces)
+    key = ("box",) + tuple(piece.shape for piece in pieces)
     if key not in HALO_IDS:
         HALO_IDS[key] = len(HALO_IDS)
     sizes = tuple(lax.axis_size(axis) for axis in axes)
@@ -290,11 +292,15 @@
         compiler_params=pltpu.CompilerParams(collective_id=HALO_IDS[key], has_side_effects=True),
     )(*pieces)
     got = {offset: from_rows(piece, *layout) for offset, piece, layout in zip(offsets, received, layouts)}
-    got[(0, 0)] = shard
-    rows = []
-    for ox in (-1, 0, 1):
-        rows.append(jnp.concatenate([got[(ox, oy)] for oy in (-1, 0, 1)], axis=dims[1]))
-    return jnp.concatenate(rows, axis=dims[0])
+    got[(0,) * len(axes)] = shard
+
+    def assemble(prefix):
+        level = len(prefix)
+        if level == len(axes):
+            return got[prefix]
+        return jnp.concatenate([assemble(prefix + (step,)) for step in steps], axis=dims[level])
+
+    return assemble(())
 
 
 def with_halo(shard, sides, width):
@@ -422,12 +428,13 @@
 
 
 def filter_field(field, sides):
-    (axis_x, dim_x), (axis_y, dim_y), (axis_z, dim_z) = sides
-    count_x, count_y = field.shape[dim_x], field.shape[dim_y]
-    padded = with_plane_halo(field, (axis_x, axis_y), (dim_x, dim_y), RADIUS)
-    field = smooth(smooth(padded, dim_x, count_x), dim_y, count_y)
-    padded = with_halo(field, ((axis_z, dim_z),), RADIUS)
-    return smooth(padded, dim_z, field.shape[dim_z])
+    axes = tuple(axis for axis, _ in sides)
+    dims = tuple(dim for _, dim in sides)
+    counts = [field.shape[dim] for dim in dims]
+    padded = with_box_halo(field, axes, dims, RADIUS)
+    for dim, count in zip(dims, counts):
+        padded = smooth(padded, dim, count)
+    return padded
 
 
 def local(local_solution, top_nodes, coarse_solution, corner_dofs, density, element_stiffness):
@@ -455,10 +462,9 @@
     upper_y = index_y < lax.axis_size("gy") - 1
     lower_z = index_z > 0
     upper_z = index_z < lax.axis_size("gz") - 1
-    extended = with_plane_halo(nodes, ("gx", "gy"), (1, 2), 1)
+    extended = with_box_halo(nodes, ("gx", "gy", "gz"), (1, 2, 3), 1)
     extended = average_rows(extended, 1, lower_x, upper_x)
-    averaged = average_rows(extended, 2, lower_y, upper_y)
-    extended = with_halo(averaged, (("gz", 3),), 1)
+    extended = average_rows(extended, 2, lower_y, upper_y)
     averaged = average_rows(extended, 3, lower_z, upper_z)
     energy = element_energy(averaged, element_stiffness)
     sens = penal_scale * density * density * energy

time: 105 us -> 136 us (1.30)
  other arithmetic: 18.1 us -> 33.3 us
  local copies, waits for them, and re-layouts: 16.8 us -> 24.5 us
  Pallas kernels: 68.9 us -> 76.1 us
    pallas_call x4 -> x2, Pallas kernels: 41.2 us -> 48.5 us  [with_box_halo(): pl.pallas_call(kernel, out_shape=shapes, in_specs=[vmem] * len(pieces), o...]
    concatenate x1 -> x2, other arithmetic: 1.42 us -> 7.59 us  [assemble(): jnp.concatenate([assemble(prefix + (step,)) for step in steps], axis=dims...]
    another operation x2 -> x4, local copies, waits for them, and re-layouts: 1.23 us -> 5.24 us  [the longest x2 4.03 us: from_rows(): return jnp.moveaxis(piece.reshape(moved), tuple(range(len(thin))), thin)]
    add x3, other arithmetic: 4.89 us -> 8.27 us  [average_rows(): return own_rows * factor + rim_part * 0.5]
    unnamed x15 -> x53, local copies, waits for them, and re-layouts: 3.03 us -> 5.63 us
    another operation x4 -> x7, other arithmetic: 3.18 us -> 5.55 us  [local(): smoothed = filter_field(jnp.stack([density * sens, density]), sides)]
    slice x4 -> x7, local copies, waits for them, and re-layouts: 2.99 us -> 4.88 us  [with_box_halo(): piece = lax.slice_in_dim(piece, length - width, length, axis=dim)]
    broadcast_in_dim x2 -> x0, local copies, waits for them, and re-layouts: 1.5 us -> none  [the longest x1 0.75 us: average_rows(): jnp.where(is_low, rim_low, 0.0) + jnp.where(is_high, rim_high, 0.0)]
where the time goes in v17:
time: 136 us; the launch traced here: 135 us
  Pallas kernels  76.1 us (56%)
  other arithmetic  33.3 us (24%)
  local copies, waits for them, and re-layouts  24.5 us (18%)
    pallas_call x2, Pallas kernels, with_box_halo(): pl.pallas_call(kernel, out_shape=shapes, in_specs=[vmem] * len(pieces), o...  48.5 us
    pallas_call x1, Pallas kernels, element_energy(): pl.pallas_call(kernel, out_shape=jax.ShapeDtypeStruct((count_x, count_y,...  15.5 us
    pallas_call x1, Pallas kernels, gather_peers(): pl.pallas_call(kernel, out_shape=jax.ShapeDtypeStruct(stacked, shard.dtyp...  12.1 us
    add x3, other arithmetic, average_rows(): return own_rows * factor + rim_part * 0.5  8.27 us
    concatenate x2, other arithmetic, assemble(): jnp.concatenate([assemble(prefix + (step,)) for step in steps], axis=dims...  7.59 us
    unnamed x53, local copies, waits for them, and re-layouts  5.63 us
    another operation x7, other arithmetic, local(): smoothed = filter_field(jnp.stack([density * sens, density]), sides)  5.55 us
    slice x7, local copies, waits for them, and re-layouts, with_box_halo(): piece = lax.slice_in_dim(piece, length - width, length, axis=dim)  4.88 us

profile of v17, /device:TPU:29, one launch (start us, length us, event | category | flops | bytes accessed | tf_op | source)
XLA Modules:
  0.0 135.2 jit_solution(1479890941461902326)
XLA Ops:
  0.6 12.1 %shard_map.77 = f32[16,3,512]{2,1,0:T(4,128)} custom-call(f32[3,512]{1,0:T(4,128)} %shard.1), custom_call_target="tpu_custom_call" | custom-call | tf_op jit(solution)/shard_map/pallas_call | solution.py:158
  12.8 0.8 iota_compare_fusion
  13.5 1.1 select_reduce_fusion
  15.1 2.4 %copy.61 = f32[3,17,45,1]{3,2,1,0:T(8,128)} copy(f32[3,17,45,1]{2,3,1,0:T(1,128)} %param.7) | data formatting | bytes 18360 | tf_op args[1]
  17.5 2.1 %fusion.2 = f32[3,17,45,129]{3,2,1,0:T(8,128)S(1)} fusion(f32[3,17,45,1]{3,2,1,0:T(8,128)} %copy.61, f32[3,17,45,128]{3,2,1,0:T(8,128)} %param.6, f32[129]{0:T(256)S(1)} %get-tuple-element.198, f32[3,17,45]{2,1,0:T(8,128)S(1)} %get-tuple-element.189, f32[129]{0:T(256)S(1)} %get-tuple-element.199, f32[3,17,45]{2,1,0:T(8,128)S(1)} %get-tuple-element.188), kind=kLoop, calls=%fused_computation.49 | loop fusion | flops 1480275 | bytes 2387832 | tf_op jit(solution)/shard_map/add | solution.py:341
  25.7 20.4 %shard_map.78 = (f32[3,1,1,1]{3,2,1,0:T(1,128)}, f32[3,1,1,129]{3,2,1,0:T(1,128)}, f32[3,1,1,1]{3,2,1,0:T(1,128)}, f32[3,1,45,1]{3,2,1,0:T(8,128)}, f32[3,1,45,1...) custom-call(f32[3,1,1,1]{3,2,1,0:T(1,128)} %get-tuple-element.141.re, ...), custom_call_target="tpu_custom_call" | custom-call | tf_op jit(solution)/shard_map/pallas_call | solution.py:285
  46.2 1.2 maximum_bitcast_fusion
  47.5 1.2 maximum_bitcast_fusion.1
  48.6 2.4 %transpose_reshape.8 = f32[3,17,45,1]{3,2,1,0:T(8,128)} reshape(f32[51,45]{1,0:T(8,128)} %get-tuple-element.57) | data formatting | bytes 18360 | tf_op jit(solution)/shard_map/transpose;reshape | solution.py:256
  51.0 1.6 %transpose_reshape.9 = f32[3,17,45,1]{3,2,1,0:T(8,128)} reshape(f32[51,45]{1,0:T(8,128)S(1)} %copy-done.13) | data formatting | bytes 18360 | tf_op jit(solution)/shard_map/transpose;reshape | solution.py:256
  52.7 4.2 %fusion.3 = f32[3,17,47,131]{3,2,1,0:T(8,128)S(1)} fusion(f32[3,17,1,1]{3,2,1,0:T(1,128)S(1)} %copy-done.17, f32[3,17,1,129]{3,2,1,0:T(1,128)S(1)} %copy-done.12, f32[3,17,1,1]{3,2,1,0:T(1,128)S(1)} %copy-done.16, f32[3,17,45,1]{3,2,1,0:T(8,128)} %transpose_reshape.9, f32[3,17,45,129]{3,2,1,0:T(8,128)S(1)} %fusion.2, f32[3,17,45,1]{3,2,1,0:T(8,128)} %transpose_reshape.8, ...), kind=kLoop, calls=%fused_computation.51 | loop fusion | flops 4396098 | bytes 2659926 | tf_op jit(solution)/shard_map/add | solution.py:356
  57.0 1.5 %copy-done = f32[3,17,47,131]{3,2,1,0:T(8,128)} copy-done((f32[3,17,47,131]{3,2,1,0:T(8,128)}, f32[3,17,47,131]{3,2,1,0:T(8,128)S(1)}, u32[]{:S(2)}) %copy-start) | copy-done | bytes 1256052
  58.6 2.5 %fusion.1 = f32[3,17,45,131]{3,2,1,0:T(8,128)S(1)} fusion(f32[3,17,47,131]{3,2,1,0:T(8,128)} %copy-done, f32[3,17,131]{2,1,0:T(8,128)S(1)} %bitcast.43, f32[3,17,131]{2,1,0:T(8,128)S(1)} %bitcast.44, f32[45]{0:T(128)S(1)} %and_select_fusion.18, pred[45]{0:T(512)(128)(4,1)S(1)} %get-tuple-element.202, pred[45]{0:T(512)(128)(4,1)S(1)} %get-tuple-element.203), kind=kLoop, calls=%fused_computation.47 | loop fusion | flops 1803870 | bytes 2458878 | tf_op jit(solution)/shard_map/add | solution.py:356
  61.1 1.1 slice_reduce_fusion.1
  62.2 1.5 %fusion = f32[3,17,45,129]{3,2,1,0:T(8,128)S(1)} fusion(f32[3,17,45,131]{3,2,1,0:T(8,128)S(1)} %fusion.1, f32[3,17,45]{2,1,0:T(8,128)S(1)} %get-tuple-element.117, f32[3,17,45]{2,1,0:T(8,128)S(1)} %get-tuple-element.116, f32[129]{0:T(256)S(1)} %and_select_fusion.16, pred[129]{0:T(512)(128)(4,1)S(1)} %get-tuple-element.204, ...), kind=kLoop, calls=%fused_computation.45 | loop fusion | flops 1776330 | bytes 2387574 | tf_op jit(solution)/shard_map/add | solution.py:356
  63.7 3.0 %fusion.65 = (f32[3,17,44,128]{3,2,1,0:T(8,128)}, f32[3,17,44,128]{3,2,1,0:T(8,128)}, f32[3,17,44,128]{3,2,1,0:T(8,128)}, f32[3,17,44,128]{3,2,1,0:T(8,128)}) fusion(f32[3,17,45,129]{3,2,1,0:T(8,128)S(1)} %fusion), kind=kLoop, calls=%fused_computation.207 | loop fusion | bytes 9191424 | tf_op jit(solution)/shard_map/slice | solution.py:395
  66.8 15.5 %shard_map.79 = f32[16,44,128]{2,1,0:T(8,128)} custom-call(f32[24,24]{1,0:T(8,128)} %stiffness.1, f32[3,17,44,128]{3,2,1,0:T(8,128)} %get-tuple-element.131.base, f32[3,17,44,128]{3,2,1,0:T(8,128)} %get-tuple-element.130.up_y, f32[3,17,44,128]{3,2,1,0:T(8,128)} %get-tuple-element.129.up_z, f32[3,17,44,128]{3,2,1,0:T(8,128)} %get-tuple-element.128.up_yz), custom_call_target="tpu_custom_call" | custom-call | tf_op jit(solution)/shard_map/pallas_call | solution.py:401
  82.3 1.1 fusion.26
  83.7 1.0 copy.67
  84.7 1.0 copy.66
  86.3 0.8 fusion.38
  87.8 0.9 fusion.32
  90.0 28.0 %shard_map.80 = (f32[2,3,3,3]{3,2,1,0:T(4,128)}, f32[2,3,3,128]{3,2,1,0:T(4,128)}, f32[2,3,3,3]{3,2,1,0:T(4,128)}, f32[2,3,44,3]{3,2,1,0:T(8,128)}, f32[2,3,44,1...) custom-call(f32[2,3,3,3]{3,2,1,0:T(4,128)} %get-tuple-element.167.re, ...), custom_call_target="tpu_custom_call" | custom-call | tf_op jit(solution)/shard_map/pallas_call | solution.py:285
  118.1 1.2 copy.68
  119.3 1.2 copy.69
  120.6 4.1 %maximum_maximum_fusion = f32[2,19,50,134]{3,2,1,0:T(8,128)S(1)} fusion(f32[2,16,3,3]{3,2,1,0:T(4,128)} %get-tuple-element.96, f32[2,16,3,128]{3,2,1,0:T(4,128)} %get-tuple-element.95, f32[2,16,3,3]{3,2,1,0:T(4,128)} %get-tuple-element.94, f32[2,16,44,3]{3,2,1,0:T(8,128)S(1)} %bitcast.39, f32[1,16,44,128]{3,2,1,0:T(8,128)S(1)} %get-tuple-element.187, ...), kind=kLoop, calls=%fused_computation.52 | loop fusion | flops 4582800 | bytes 2036800 | tf_op jit(solution)/shard_map/concatenate | solution.py:301
  124.9 3.5 %maximum_maximum_fusion.1 = f32[2,19,50,134]{3,2,1,0:T(8,128)S(1)} fusion(f32[2,3,3,3]{3,2,1,0:T(4,128)S(1)} %copy-done.23, f32[2,3,3,128]{3,2,1,0:T(4,128)S(1)} %copy-done.22, f32[2,3,3,3]{3,2,1,0:T(4,128)S(1)} %copy-done.21, f32[2,3,44,3]{3,2,1,0:T(8,128)S(1)} %copy-done.10, f32[2,3,44,128]{3,2,1,0:T(8,128)S(1)} %copy-done.9, ...), kind=kLoop, calls=%fused_computation.53 | loop fusion | flops 4582800 | bytes 2036800 | tf_op jit(solution)/shard_map/concatenate | solution.py:301
  128.4 2.3 %slice_add_fusion = f32[2,16,50,134]{3,2,1,0:T(8,128)S(1)} fusion(f32[2,19,50,134]{3,2,1,0:T(8,128)S(1)} %maximum_maximum_fusion.1, f32[2,19,50,134]{3,2,1,0:T(8,128)S(1)} %maximum_maximum_fusion, f32[2,16,3,3]{3,2,1,0:T(4,128)S(1)} %copy-done.7, f32[2,16,3,128]{3,2,1,0:T(4,128)S(1)} %copy-done.6, f32[2,16,3,3]{3,2,1,0:T(4,128)S(1)} %copy-done.5, ...), kind=kLoop, calls=%fused_computation.54 | loop fusion | flops 4288000 | bytes 6860800 | tf_op jit(solution)/shard_map/add | solution.py:416
  130.7 1.2 slice_add_fusion.1
  131.9 1.3 slice_add_fusion.2
  133.5 0.8 copy.71
  134.3 0.8 copy.72
  (81 shorter events, 10.1 us)
Async XLA Ops:
  46.2 4.8 %copy-start.13 = (f32[51,45]{1,0:T(8,128)S(1)}, f32[51,45]{1,0:T(8,128)}, u32[]{:S(2)}) copy-start(f32[51,45]{1,0:T(8,128)} %get-tuple-element.58) | copy-start | bytes 27544
  46.2 6.5 %copy-start.11 = (f32[3,17,1,129]{3,2,1,0:T(1,128)S(1)}, f32[3,17,1,129]{3,2,1,0:T(1,128)}, u32[]{:S(2)}) copy-start(f32[3,17,1,129]{3,2,1,0:T(1,128)} %get-tuple-element.55) | copy-start | bytes 78952
  46.2 6.5 %copy-start.12 = (f32[3,17,1,129]{3,2,1,0:T(1,128)S(1)}, f32[3,17,1,129]{3,2,1,0:T(1,128)}, u32[]{:S(2)}) copy-start(f32[3,17,1,129]{3,2,1,0:T(1,128)} %get-tuple-element.60) | copy-start | bytes 78952
  46.2 6.5 %copy-start.14 = (f32[3,17,1,1]{3,2,1,0:T(1,128)S(1)}, f32[3,17,1,1]{3,2,1,0:T(1,128)}, u32[]{:S(2)}) copy-start(f32[3,17,1,1]{3,2,1,0:T(1,128)} %get-tuple-element.54) | copy-start | bytes 616
  46.2 6.5 %copy-start.15 = (f32[3,17,1,1]{3,2,1,0:T(1,128)S(1)}, f32[3,17,1,1]{3,2,1,0:T(1,128)}, u32[]{:S(2)}) copy-start(f32[3,17,1,1]{3,2,1,0:T(1,128)} %get-tuple-element.56) | copy-start | bytes 616
  46.2 6.5 %copy-start.16 = (f32[3,17,1,1]{3,2,1,0:T(1,128)S(1)}, f32[3,17,1,1]{3,2,1,0:T(1,128)}, u32[]{:S(2)}) copy-start(f32[3,17,1,1]{3,2,1,0:T(1,128)} %get-tuple-element.59) | copy-start | bytes 616
  46.2 6.5 %copy-start.17 = (f32[3,17,1,1]{3,2,1,0:T(1,128)S(1)}, f32[3,17,1,1]{3,2,1,0:T(1,128)}, u32[]{:S(2)}) copy-start(f32[3,17,1,1]{3,2,1,0:T(1,128)} %get-tuple-element.61) | copy-start | bytes 616
  57.0 1.5 %copy-start = (f32[3,17,47,131]{3,2,1,0:T(8,128)}, f32[3,17,47,131]{3,2,1,0:T(8,128)S(1)}, u32[]{:S(2)}) copy-start(f32[3,17,47,131]{3,2,1,0:T(8,128)S(1)} %fusion.3) | copy-start | bytes 3768088
  66.8 15.5 %copy-start.1 = (f32[16,44,128]{2,0,1:T(8,128)S(1)}, f32[16,44,128]{2,0,1:T(8,128)}, u32[]{:S(2)}) copy-start(f32[16,44,128]{2,0,1:T(8,128)} %param.10) | copy-start | bytes 1081348
  120.5 4.2 %copy-start.2 = (f32[2,16,3,3]{3,2,1,0:T(4,128)S(1)}, f32[2,16,3,3]{3,2,1,0:T(4,128)}, u32[]{:S(2)}) copy-start(f32[2,16,3,3]{3,2,1,0:T(4,128)} %get-tuple-element.89) | copy-start | bytes 3460
  120.5 4.2 %copy-start.3 = (f32[2,16,3,128]{3,2,1,0:T(4,128)S(1)}, f32[2,16,3,128]{3,2,1,0:T(4,128)}, u32[]{:S(2)}) copy-start(f32[2,16,3,128]{3,2,1,0:T(4,128)} %get-tuple-element.90) | copy-start | bytes 147460
  120.5 4.2 %copy-start.4 = (f32[2,16,3,3]{3,2,1,0:T(4,128)S(1)}, f32[2,16,3,3]{3,2,1,0:T(4,128)}, u32[]{:S(2)}) copy-start(f32[2,16,3,3]{3,2,1,0:T(4,128)} %get-tuple-element.91) | copy-start | bytes 3460
  120.5 4.2 %copy-start.5 = (f32[2,16,3,3]{3,2,1,0:T(4,128)S(1)}, f32[2,16,3,3]{3,2,1,0:T(4,128)}, u32[]{:S(2)}) copy-start(f32[2,16,3,3]{3,2,1,0:T(4,128)} %get-tuple-element.94) | copy-start | bytes 3460
  120.5 4.2 %copy-start.6 = (f32[2,16,3,128]{3,2,1,0:T(4,128)S(1)}, f32[2,16,3,128]{3,2,1,0:T(4,128)}, u32[]{:S(2)}) copy-start(f32[2,16,3,128]{3,2,1,0:T(4,128)} %get-tuple-element.95) | copy-start | bytes 147460
  120.5 4.2 %copy-start.7 = (f32[2,16,3,3]{3,2,1,0:T(4,128)S(1)}, f32[2,16,3,3]{3,2,1,0:T(4,128)}, u32[]{:S(2)}) copy-start(f32[2,16,3,3]{3,2,1,0:T(4,128)} %get-tuple-element.96) | copy-start | bytes 3460
  120.6 4.2 %copy-start.8 = (f32[2,3,44,3]{3,2,1,0:T(8,128)S(1)}, f32[2,3,44,3]{3,2,1,0:T(8,128)}, u32[]{:S(2)}) copy-start(f32[2,3,44,3]{3,2,1,0:T(8,128)} %get-tuple-element.100) | copy-start | bytes 9508
  120.6 4.2 %copy-start.9 = (f32[2,3,44,128]{3,2,1,0:T(8,128)S(1)}, f32[2,3,44,128]{3,2,1,0:T(8,128)}, u32[]{:S(2)}) copy-start(f32[2,3,44,128]{3,2,1,0:T(8,128)} %get-tuple-element.101) | copy-start | bytes 405508
  120.6 4.2 %copy-start.10 = (f32[2,3,44,3]{3,2,1,0:T(8,128)S(1)}, f32[2,3,44,3]{3,2,1,0:T(8,128)}, u32[]{:S(2)}) copy-start(f32[2,3,44,3]{3,2,1,0:T(8,128)} %get-tuple-element.102) | copy-start | bytes 9508
  120.6 4.2 %copy-start.18 = (f32[2,3,3,3]{3,2,1,0:T(4,128)S(1)}, f32[2,3,3,3]{3,2,1,0:T(4,128)}, u32[]{:S(2)}) copy-start(f32[2,3,3,3]{3,2,1,0:T(4,128)} %get-tuple-element.97) | copy-start | bytes 652
  120.6 4.2 %copy-start.19 = (f32[2,3,3,128]{3,2,1,0:T(4,128)S(1)}, f32[2,3,3,128]{3,2,1,0:T(4,128)}, u32[]{:S(2)}) copy-start(f32[2,3,3,128]{3,2,1,0:T(4,128)} %get-tuple-element.98) | copy-start | bytes 27652
  120.6 4.2 %copy-start.20 = (f32[2,3,3,3]{3,2,1,0:T(4,128)S(1)}, f32[2,3,3,3]{3,2,1,0:T(4,128)}, u32[]{:S(2)}) copy-start(f32[2,3,3,3]{3,2,1,0:T(4,128)} %get-tuple-element.99) | copy-start | bytes 652
  120.6 4.2 %copy-start.21 = (f32[2,3,3,3]{3,2,1,0:T(4,128)S(1)}, f32[2,3,3,3]{3,2,1,0:T(4,128)}, u32[]{:S(2)}) copy-start(f32[2,3,3,3]{3,2,1,0:T(4,128)} %get-tuple-element.103) | copy-start | bytes 652
  120.6 4.2 %copy-start.22 = (f32[2,3,3,128]{3,2,1,0:T(4,128)S(1)}, f32[2,3,3,128]{3,2,1,0:T(4,128)}, u32[]{:S(2)}) copy-start(f32[2,3,3,128]{3,2,1,0:T(4,128)} %get-tuple-element.104) | copy-start | bytes 27652
  120.6 4.2 %copy-start.23 = (f32[2,3,3,3]{3,2,1,0:T(4,128)S(1)}, f32[2,3,3,3]{3,2,1,0:T(4,128)}, u32[]{:S(2)}) copy-start(f32[2,3,3,3]{3,2,1,0:T(4,128)} %get-tuple-element.105) | copy-start | bytes 652

commit v18 on v15

--- a/solution.py
+++ b/solution.py
@@ -350,36 +350,46 @@
     return own_rows * factor + rim_part * 0.5
 
 
-def energy_kernel(stiffness, base, up_y, up_z, up_yz, out, weights, *, count_x, chunks):
+def quadratic(weights, vectors):
+    total = None
+    for a in range(24):
+        inner = weights[a * 24 + a] * vectors[a]
+        for b in range(a + 1, 24):
+            inner = inner + weights[a * 24 + b] * vectors[b]
+        term = vectors[a] * inner
+        total = term if total is None else total + term
+    return total
+
+
+def energy_kernel(stiffness, base, up_y, up_z, up_yz, out, weights, *, count_x, count_y):
     sources = (base, up_z, up_y, up_yz)
     for a in range(24):
         weights[a * 24 + a] = stiffness[a, a]
         for b in range(a + 1, 24):
             weights[a * 24 + b] = stiffness[a, b] + stiffness[b, a]
-
-    def row(i, carry):
-        for first in chunks:
-            vectors = []
-            for component in range(3):
-                for corner in range(8):
-                    shift_x = corner // 4
-                    source = sources[corner % 4]
-                    vectors.append(source[component, i + shift_x, pl.ds(first, 8), :])
-            total = None
-            for a in range(24):
-                inner = weights[a * 24 + a] * vectors[a]
-                for b in range(a + 1, 24):
-                    inner = inner + weights[a * 24 + b] * vectors[b]
-                term = vectors[a] * inner
-                total = term if total is None else total + term
-            if first % 8 == 0:
-                out[i, pl.ds(first, 8), :] = total
-            else:
-                keep = 8 - first % 8
-                out[i, pl.ds(first + 8 - keep, keep), :] = total[8 - keep :]
+    tail = count_y % 8
+    full = count_y - tail
+
+    def load(i, first, rows):
+        vectors = []
+        for component in range(3):
+            for corner in range(8):
+                source = sources[corner % 4]
+                vectors.append(source[component, i + corner // 4, pl.ds(first, rows), :])
+        return vectors
+
+    def pair(step, carry):
+        for i in (2 * step, 2 * step + 1):
+            for first in range(0, full, 8):
+                out[i, pl.ds(first, 8), :] = quadratic(weights, load(i, first, 8))
+        low = load(2 * step, full, tail)
+        high = load(2 * step + 1, full, tail)
+        total = quadratic(weights, [jnp.concatenate([a, b], axis=0) for a, b in zip(low, high)])
+        out[2 * step, pl.ds(full, tail), :] = total[:tail]
+        out[2 * step + 1, pl.ds(full, tail), :] = total[tail:]
         return carry
 
-    lax.fori_loop(0, count_x, row, 0)
+    lax.fori_loop(0, count_x // 2, pair, 0)
 
 
 def element_energy(nodes, stiffness):
@@ -387,10 +397,7 @@
     count_y = nodes.shape[2] - 1
     count_z = nodes.shape[3] - 1
     shifted = [nodes[:, :, dy : dy + count_y, dz : dz + count_z] for dy, dz in ((0, 0), (1, 0), (0, 1), (1, 1))]
-    chunks = tuple(range(0, count_y - 7, 8))
-    if count_y % 8:
-        chunks = chunks + (count_y - 8,)
-    kernel = functools.partial(energy_kernel, count_x=count_x, chunks=chunks)
+    kernel = functools.partial(energy_kernel, count_x=count_x, count_y=count_y)
     vmem = pl.BlockSpec(memory_space=pltpu.VMEM)
     energy = pl.pallas_call(
         kernel,

time: 105 us -> 105 us (level)
  no operation moved by 1% of the time
where the time goes in v18:
time: 105 us; the launch traced here: 104 us
  Pallas kernels  68.1 us (65%)
  other arithmetic  18.1 us (17%)
  local copies, waits for them, and re-layouts  16.8 us (16%)
    pallas_call x2, Pallas kernels, with_plane_halo(): pl.pallas_call(kernel, out_shape=shapes, in_specs=[vmem] * len(pieces), o...  27.4 us
    pallas_call x1, Pallas kernels, element_energy(): pl.pallas_call(kernel, out_shape=jax.ShapeDtypeStruct((count_x, count_y,...  14.5 us
    pallas_call x2, Pallas kernels, exchange(): pl.pallas_call(kernel, out_shape=(slab, slab), in_specs=[vmem, vmem], out...  13.9 us
    pallas_call x1, Pallas kernels, gather_peers(): pl.pallas_call(kernel, out_shape=jax.ShapeDtypeStruct(stacked, shard.dtyp...  12.2 us
    add x3, other arithmetic, average_rows(): return own_rows * factor + rim_part * 0.5  4.89 us
    add x3, other arithmetic, smooth(): summed = term_value if summed is None else summed + term_value  3.36 us
    another operation x4, other arithmetic, local(): smoothed = filter_field(jnp.stack([density * sens, density]), sides)  3.18 us
    slice x1, local copies, waits for them, and re-layouts, element_energy(): nodes[:, :, dy:dy + count_y, dz:dz + count_z]  3.05 us

profile of v18, /device:TPU:29, one launch (start us, length us, event | category | flops | bytes accessed | tf_op | source)
XLA Modules:
  0.0 103.8 jit_solution(13180628968752875595)
XLA Ops:
  0.6 12.2 %shard_map.77 = f32[16,3,512]{2,1,0:T(4,128)} custom-call(f32[3,512]{1,0:T(4,128)} %shard.1), custom_call_target="tpu_custom_call" | custom-call | tf_op jit(solution)/shard_map/pallas_call | solution.py:157
  12.8 0.8 iota_compare_fusion
  13.6 1.1 %select_reduce_fusion = f32[3,8]{1,0:T(4,128)S(1)} fusion(f32[3,8192]{1,0:T(4,128)} %bitcast.42, pred[8,8192]{1,0:T(8,128)(4,1)S(1)} %iota_compare_fusion), kind=kLoop, calls=%fused_computation.71 | loop fusion | flops 393192 | bytes 163936 | tf_op jit(solution)/shard_map/reduce_sum | solution.py:455
  15.2 1.3 %copy.59 = f32[3,17,45,1]{3,2,1,0:T(8,128)S(1)} copy(f32[3,17,45,1]{2,3,1,0:T(1,128)} %param.7) | data formatting | bytes 18360 | tf_op args[1]
  16.5 0.9 fusion.1
  18.1 0.9 fusion.58
  19.0 0.7 fusion.59
  19.7 12.3 %shard_map.78 = (f32[3,1,1,129]{3,2,1,0:T(1,128)}, f32[3,1,45,129]{3,2,1,0:T(8,128)}, f32[3,1,1,129]{3,2,1,0:T(1,128)}, f32[3,17,1,129]{3,2,1,0:T(1,128)}, f32[3...) custom-call(f32[3,1,1,129]{3,2,1,0:T(1,128)} %get-tuple-element.71.refs_0, ...), custom_call_target="tpu_custom_call" | custom-call | tf_op jit(solution)/shard_map/pallas_call | solution.py:283
  32.0 0.9 maximum_bitcast_fusion
  33.0 0.9 maximum_bitcast_fusion.1
  34.0 2.8 %fusion.2 = f32[3,17,47,129]{3,2,1,0:T(8,128)S(1)} fusion(f32[3,17,1,129]{3,2,1,0:T(1,128)} %get-tuple-element.23, f32[3,17,45,129]{3,2,1,0:T(8,128)} %copy-done, f32[3,17,1,129]{3,2,1,0:T(1,128)} %get-tuple-element.22, f32[3,47,129]{2,1,0:T(8,128)S(1)} %maximum_bitcast_fusion.1, f32[3,47,129]{2,1,0:T(8,128)S(1)} %maximum_bitcast_fusion, ...), kind=kLoop, calls=%fused_computation.5 | loop fusion | flops 2473704 | bytes 2619318 | tf_op jit(solution)/shard_map/add | solution.py:350
  36.9 0.8 fusion
  37.7 0.7 slice_reduce_fusion
  39.7 6.8 %shard_map.79 = (f32[51,45]{1,0:T(8,128)}, f32[51,45]{1,0:T(8,128)}) custom-call(f32[51,45]{1,0:T(8,128)} %reshape_transpose.6.low, f32[51,45]{1,0:T(8,128)} %reshape_transpose.7.high), custom_call_target="tpu_custom_call" | custom-call | tf_op jit(solution)/shard_map/pallas_call | solution.py:90
  46.5 0.8 broadcast_in_dim.204
  47.2 0.8 broadcast_in_dim.207
  48.0 1.3 %multiply_add_fusion = f32[3,17,45,129]{3,2,1,0:T(8,128)S(1)} fusion(f32[3,17,45]{2,1,0:T(8,128)S(1)} %broadcast_in_dim.207, f32[3,17,45]{2,1,0:T(8,128)S(1)} %broadcast_in_dim.204, f32[129]{0:T(256)S(1)} %and_select_fusion.16, pred[129]{0:T(512)(128)(4,1)S(1)} %get-tuple-element.108, pred[129]{0:T(512)(128)(4,1)S(1)} %get-tuple-element.109, ...), kind=kLoop, calls=%fused_computation.6 | loop fusion | flops 3552660 | bytes 2440476 | tf_op jit(solution)/shard_map/add | solution.py:350
  49.3 3.1 %fusion.55 = (f32[3,17,44,128]{3,2,1,0:T(8,128)}, f32[3,17,44,128]{3,2,1,0:T(8,128)}, f32[3,17,44,128]{3,2,1,0:T(8,128)}, f32[3,17,44,128]{3,2,1,0:T(8,128)}) fusion(f32[3,17,45,129]{3,2,1,0:T(8,128)S(1)} %multiply_add_fusion), kind=kLoop, calls=%fused_computation.167 | loop fusion | bytes 9191424 | tf_op jit(solution)/shard_map/slice | solution.py:399
  52.4 14.5 %shard_map.80 = f32[16,44,128]{2,1,0:T(8,128)} custom-call(f32[24,24]{1,0:T(8,128)} %stiffness.1, f32[3,17,44,128]{3,2,1,0:T(8,128)} %get-tuple-element.65.base, f32[3,17,44,128]{3,2,1,0:T(8,128)} %get-tuple-element.64.up_y, f32[3,17,44,128]{3,2,1,0:T(8,128)} %get-tuple-element.63.up_z, f32[3,17,44,128]{3,2,1,0:T(8,128)} %get-tuple-element.62.up_yz), custom_call_target="tpu_custom_call" | custom-call | tf_op jit(solution)/shard_map/pallas_call | solution.py:402
  66.9 1.1 %fusion.30 = (f32[1,16,44,128]{3,2,1,0:T(8,128)S(1)}, f32[1,16,44,128]{3,2,1,0:T(8,128)S(1)}) fusion(f32[16,44,128]{2,1,0:T(8,128)} %shard_map.80, f32[16,44,128]{2,0,1:T(8,128)S(1)} %copy-done.1), kind=kLoop, calls=%fused_computation.78 | loop fusion | flops 360448 | bytes 1441792 | tf_op jit(solution)/shard_map/stack | solution.py:472
  68.0 0.7 fusion.34
  68.7 0.7 fusion.31
  70.1 15.1 %shard_map.81 = (f32[2,3,3,128]{3,2,1,0:T(4,128)}, f32[2,3,44,128]{3,2,1,0:T(8,128)}, f32[2,3,3,128]{3,2,1,0:T(4,128)}, f32[2,16,3,128]{3,2,1,0:T(4,128)}, f32[2...) custom-call(f32[2,3,3,128]{3,2,1,0:T(4,128)} %get-tuple-element.85.refs_0, ...), custom_call_target="tpu_custom_call" | custom-call | tf_op jit(solution)/shard_map/pallas_call | solution.py:283
  85.3 1.4 %maximum_maximum_fusion = (f32[2,19,50,128]{3,2,1,0:T(8,128)S(1)}, f32[2,19,50,128]{3,2,1,0:T(8,128)S(1)}) fusion(f32[2,16,3,128]{3,2,1,0:T(4,128)} %get-tuple-element.36, f32[1,16,44,128]{3,2,1,0:T(8,128)S(1)} %get-tuple-element.91, f32[1,16,44,128]{3,2,1,0:T(8,128)S(1)} %get-tuple-element.90, f32[2,16,3,128]{3,2,1,0:T(4,128)} %get-tuple-element.35, ...), kind=kLoop, calls=%fused_computation.29 | loop fusion | flops 2918400 | bytes 3072000 | tf_op jit(solution)/shard_map/concatenate | solution.py:297
  88.0 1.0 copy.63
  89.0 1.0 copy.62
  90.0 7.1 %shard_map.82 = (f32[96,44]{1,0:T(8,128)}, f32[96,44]{1,0:T(8,128)}) custom-call(f32[96,44]{1,0:T(8,128)} %bitcast.44, f32[96,44]{1,0:T(8,128)} %bitcast.43), custom_call_target="tpu_custom_call" | custom-call | tf_op jit(solution)/shard_map/pallas_call | solution.py:90
  97.1 1.2 %copy.64 = f32[3,2,16,44]{0,3,2,1:T(8,128)S(1)} copy(f32[3,2,16,44]{3,2,1,0:T(8,128)} %bitcast.46) | data formatting | bytes 33792 | tf_op jit(solution)/shard_map/reshape | solution.py:314
  98.3 1.2 %copy.65 = f32[3,2,16,44]{0,3,2,1:T(8,128)S(1)} copy(f32[3,2,16,44]{3,2,1,0:T(8,128)} %bitcast.45) | data formatting | bytes 33792 | tf_op jit(solution)/shard_map/reshape | solution.py:315
  99.5 2.3 %fusion.11 = f32[2,16,44,128]{3,2,1,0:T(8,128)S(1)} fusion(f32[2,16,44,128]{3,2,1,0:T(8,128)S(1)} %slice_add_fusion.1, f32[2,16,44,3]{3,2,1,0:T(8,128)S(1)} %bitcast.37, f32[2,16,44,3]{3,2,1,0:T(8,128)S(1)} %bitcast.36), kind=kLoop, calls=%fused_computation.45 | loop fusion | flops 3063808 | bytes 1475584 | tf_op jit(solution)/shard_map/add | solution.py:417
  102.1 0.8 copy.67
  103.0 0.8 copy.68
  (37 shorter events, 4.8 us)
Async XLA Ops:
  0.6 15.9 %copy-start.2 = (f32[3,17,45,128]{3,2,1,0:T(8,128)S(1)}, f32[3,17,45,128]{3,2,1,0:T(8,128)}, u32[]{:S(2)}) copy-start(f32[3,17,45,128]{3,2,1,0:T(8,128)} %param.6) | copy-start | bytes 3525124
  17.4 1.6 %copy-start = (f32[3,17,45,129]{3,2,1,0:T(8,128)}, f32[3,17,45,129]{3,2,1,0:T(8,128)S(1)}, u32[]{:S(2)}) copy-start(f32[3,17,45,129]{3,2,1,0:T(8,128)S(1)} %fusion.1) | copy-start | bytes 3552664
  52.4 14.5 %copy-start.1 = (f32[16,44,128]{2,0,1:T(8,128)S(1)}, f32[16,44,128]{2,0,1:T(8,128)}, u32[]{:S(2)}) copy-start(f32[16,44,128]{2,0,1:T(8,128)} %param.10) | copy-start | bytes 1081348
  85.2 1.4 %copy-start.3 = (f32[2,16,3,128]{3,2,1,0:T(4,128)S(1)}, f32[2,16,3,128]{3,2,1,0:T(4,128)}, u32[]{:S(2)}) copy-start(f32[2,16,3,128]{3,2,1,0:T(4,128)} %get-tuple-element.35) | copy-start | bytes 147460
  85.2 1.4 %copy-start.4 = (f32[2,16,3,128]{3,2,1,0:T(4,128)S(1)}, f32[2,16,3,128]{3,2,1,0:T(4,128)}, u32[]{:S(2)}) copy-start(f32[2,16,3,128]{3,2,1,0:T(4,128)} %get-tuple-element.36) | copy-start | bytes 147460

commit v19 on v18

--- a/solution.py
+++ b/solution.py
@@ -361,7 +361,7 @@
     return total
 
 
-def energy_kernel(stiffness, base, up_y, up_z, up_yz, out, weights, *, count_x, count_y):
+def energy_kernel(stiffness, base, up_y, up_z, up_yz, density, out, weights, *, count_x, count_y):
     sources = (base, up_z, up_y, up_yz)
     for a in range(24):
         weights[a * 24 + a] = stiffness[a, a]
@@ -378,21 +378,27 @@
                 vectors.append(source[component, i + corner // 4, pl.ds(first, rows), :])
         return vectors
 
+    def put(i, first, rows, energy):
+        local_density = density[i, pl.ds(first, rows), :]
+        sens = penal_scale * local_density * local_density * energy
+        out[0, i, pl.ds(first, rows), :] = local_density * sens
+        out[1, i, pl.ds(first, rows), :] = local_density
+
     def pair(step, carry):
         for i in (2 * step, 2 * step + 1):
             for first in range(0, full, 8):
-                out[i, pl.ds(first, 8), :] = quadratic(weights, load(i, first, 8))
+                put(i, first, 8, quadratic(weights, load(i, first, 8)))
         low = load(2 * step, full, tail)
         high = load(2 * step + 1, full, tail)
         total = quadratic(weights, [jnp.concatenate([a, b], axis=0) for a, b in zip(low, high)])
-        out[2 * step, pl.ds(full, tail), :] = total[:tail]
-        out[2 * step + 1, pl.ds(full, tail), :] = total[tail:]
+        put(2 * step, full, tail, total[:tail])
+        put(2 * step + 1, full, tail, total[tail:])
         return carry
 
     lax.fori_loop(0, count_x // 2, pair, 0)
 
 
-def element_energy(nodes, stiffness):
+def weighted_sensitivity(nodes, stiffness, density):
     count_x = nodes.shape[1] - 1
     count_y = nodes.shape[2] - 1
     count_z = nodes.shape[3] - 1
@@ -401,11 +407,11 @@
     vmem = pl.BlockSpec(memory_space=pltpu.VMEM)
     energy = pl.pallas_call(
         kernel,
-        out_shape=jax.ShapeDtypeStruct((count_x, count_y, count_z), jnp.float32),
-        in_specs=[pl.BlockSpec(memory_space=pltpu.SMEM)] + [vmem] * 4,
+        out_shape=jax.ShapeDtypeStruct((2, count_x, count_y, count_z), jnp.float32),
+        in_specs=[pl.BlockSpec(memory_space=pltpu.SMEM)] + [vmem] * 5,
         out_specs=vmem,
         scratch_shapes=[pltpu.SMEM((24 * 24,), jnp.float32)],
-    )(stiffness, *shifted)
+    )(stiffness, *shifted, density)
     return energy
 
 
@@ -467,9 +473,7 @@
     averaged = average_rows(extended, 2, lower_y, upper_y)
     extended = with_halo(averaged, (("gz", 3),), 1)
     averaged = average_rows(extended, 3, lower_z, upper_z)
-    energy = element_energy(averaged, element_stiffness)
-    sens = penal_scale * density * density * energy
-    smoothed = filter_field(jnp.stack([density * sens, density]), sides)
+    smoothed = filter_field(weighted_sensitivity(averaged, element_stiffness, density), sides)
     numerator = smoothed[0]
     smooth_density = smoothed[1]
     return (numerator / (density * normalizer), smooth_density / normalizer)

time: 105 us -> 108 us (1.029)
  local copies, waits for them, and re-layouts: 16.8 us -> 22.5 us
  other arithmetic: 18.1 us -> 15.4 us
    slice x3 -> x6, local copies, waits for them, and re-layouts: 2.27 us -> 7.1 us  [with_plane_halo(): piece = lax.slice_in_dim(piece, length - width, length, axis=dim)]
    another operation x4 -> x0, other arithmetic: 3.18 us -> none  [local(): smoothed = filter_field(jnp.stack([density * sens, density]), sides)]
    unnamed x15 -> x18, local copies, waits for them, and re-layouts: 3.03 us -> 3.9 us
where the time goes in v19:
time: 108 us; the launch traced here: 107 us
  Pallas kernels  68.3 us (63%)
  local copies, waits for them, and re-layouts  22.5 us (21%)
  other arithmetic  15.4 us (14%)
    pallas_call x2, Pallas kernels, with_plane_halo(): pl.pallas_call(kernel, out_shape=shapes, in_specs=[vmem] * len(pieces), o...  27.4 us
    pallas_call x1, Pallas kernels, weighted_sensitivity(): pl.pallas_call(kernel, out_shape=jax.ShapeDtypeStruct((2, count_x, count_...  14.8 us
    pallas_call x2, Pallas kernels, exchange(): pl.pallas_call(kernel, out_shape=(slab, slab), in_specs=[vmem, vmem], out...  13.9 us
    pallas_call x1, Pallas kernels, gather_peers(): pl.pallas_call(kernel, out_shape=jax.ShapeDtypeStruct(stacked, shard.dtyp...  12.2 us
    slice x6, local copies, waits for them, and re-layouts, with_plane_halo(): piece = lax.slice_in_dim(piece, length - width, length, axis=dim)  7.1 us
    add x3, other arithmetic, average_rows(): return own_rows * factor + rim_part * 0.5  4.89 us
    unnamed x18, local copies, waits for them, and re-layouts  3.9 us
    add x3, other arithmetic, smooth(): summed = term_value if summed is None else summed + term_value  3.36 us

profile of v19, /device:TPU:29, one launch (start us, length us, event | category | flops | bytes accessed | tf_op | source)
XLA Modules:
  0.0 107.2 jit_solution(18160903403787460324)
XLA Ops:
  0.6 12.2 %shard_map.77 = f32[16,3,512]{2,1,0:T(4,128)} custom-call(f32[3,512]{1,0:T(4,128)} %shard.1), custom_call_target="tpu_custom_call" | custom-call | tf_op jit(solution)/shard_map/pallas_call | solution.py:157
  12.8 0.8 iota_compare_fusion
  13.6 1.1 %select_reduce_fusion = f32[3,8]{1,0:T(4,128)S(1)} fusion(f32[3,8192]{1,0:T(4,128)} %bitcast.38, pred[8,8192]{1,0:T(8,128)(4,1)S(1)} %iota_compare_fusion), kind=kLoop, calls=%fused_computation.59 | loop fusion | flops 393192 | bytes 163936 | tf_op jit(solution)/shard_map/reduce_sum | solution.py:461
  15.2 1.3 %copy.35 = f32[3,17,45,1]{3,2,1,0:T(8,128)S(1)} copy(f32[3,17,45,1]{2,3,1,0:T(1,128)} %param.7) | data formatting | bytes 18360 | tf_op args[1]
  16.5 0.9 fusion.1
  18.1 0.9 fusion.49
  19.0 0.7 fusion.50
  19.7 12.3 %shard_map.78 = (f32[3,1,1,129]{3,2,1,0:T(1,128)}, f32[3,1,45,129]{3,2,1,0:T(8,128)}, f32[3,1,1,129]{3,2,1,0:T(1,128)}, f32[3,17,1,129]{3,2,1,0:T(1,128)}, f32[3...) custom-call(f32[3,1,1,129]{3,2,1,0:T(1,128)} %get-tuple-element.69.refs_0, ...), custom_call_target="tpu_custom_call" | custom-call | tf_op jit(solution)/shard_map/pallas_call | solution.py:283
  32.0 0.9 maximum_bitcast_fusion
  33.0 0.9 maximum_bitcast_fusion.1
  34.0 2.8 %fusion.2 = f32[3,17,47,129]{3,2,1,0:T(8,128)S(1)} fusion(f32[3,17,1,129]{3,2,1,0:T(1,128)} %get-tuple-element.23, f32[3,17,45,129]{3,2,1,0:T(8,128)} %copy-done, f32[3,17,1,129]{3,2,1,0:T(1,128)} %get-tuple-element.22, f32[3,47,129]{2,1,0:T(8,128)S(1)} %maximum_bitcast_fusion.1, f32[3,47,129]{2,1,0:T(8,128)S(1)} %maximum_bitcast_fusion, ...), kind=kLoop, calls=%fused_computation.5 | loop fusion | flops 2473704 | bytes 2619318 | tf_op jit(solution)/shard_map/add | solution.py:350
  36.9 0.8 fusion
  39.7 6.8 %shard_map.79 = (f32[51,45]{1,0:T(8,128)}, f32[51,45]{1,0:T(8,128)}) custom-call(f32[51,45]{1,0:T(8,128)} %reshape_transpose.6.low, f32[51,45]{1,0:T(8,128)} %reshape_transpose.7.high), custom_call_target="tpu_custom_call" | custom-call | tf_op jit(solution)/shard_map/pallas_call | solution.py:90
  46.5 0.8 broadcast_in_dim.204
  47.2 0.8 broadcast_in_dim.207
  48.0 1.3 %multiply_add_fusion = f32[3,17,45,129]{3,2,1,0:T(8,128)S(1)} fusion(f32[3,17,45]{2,1,0:T(8,128)S(1)} %broadcast_in_dim.207, f32[3,17,45]{2,1,0:T(8,128)S(1)} %broadcast_in_dim.204, f32[129]{0:T(256)S(1)} %and_select_fusion.16, pred[129]{0:T(512)(128)(4,1)S(1)} %get-tuple-element.104, pred[129]{0:T(512)(128)(4,1)S(1)} %get-tuple-element.105, ...), kind=kLoop, calls=%fused_computation.6 | loop fusion | flops 3552660 | bytes 2440476 | tf_op jit(solution)/shard_map/add | solution.py:350
  49.3 3.1 %fusion.46 = (f32[3,17,44,128]{3,2,1,0:T(8,128)}, f32[3,17,44,128]{3,2,1,0:T(8,128)}, f32[3,17,44,128]{3,2,1,0:T(8,128)}, f32[3,17,44,128]{3,2,1,0:T(8,128)}) fusion(f32[3,17,45,129]{3,2,1,0:T(8,128)S(1)} %multiply_add_fusion), kind=kLoop, calls=%fused_computation.142 | loop fusion | bytes 9191424 | tf_op jit(solution)/shard_map/slice | solution.py:405
  52.4 0.9 copy.36.density
  53.2 14.8 %shard_map.80 = f32[2,16,44,128]{3,2,1,0:T(8,128)} custom-call(f32[24,24]{1,0:T(8,128)} %stiffness.1, f32[3,17,44,128]{3,2,1,0:T(8,128)} %get-tuple-element.63.base, f32[3,17,44,128]{3,2,1,0:T(8,128)} %get-tuple-element.62.up_y, f32[3,17,44,128]{3,2,1,0:T(8,128)} %get-tuple-element.61.up_z, f32[3,17,44,128]{3,2,1,0:T(8,128)} %get-tuple-element.60.up_yz, ...), custom_call_target="tpu_custom_call" | custom-call | tf_op jit(solution)/shard_map/pallas_call | solution.py:408
  68.1 1.8 %fusion.52 = (f32[2,3,44,128]{3,2,1,0:T(8,128)}, f32[2,3,44,128]{3,2,1,0:T(8,128)}) fusion(f32[2,16,44,128]{3,2,1,0:T(8,128)} %shard_map.80), kind=kLoop, calls=%fused_computation.148 | loop fusion | bytes 540672 | tf_op jit(solution)/shard_map/slice | solution.py:268
  69.8 1.6 %fusion.53 = (f32[2,16,3,128]{3,2,1,0:T(4,128)}, f32[2,16,3,128]{3,2,1,0:T(4,128)}) fusion(f32[2,16,44,128]{3,2,1,0:T(8,128)} %shard_map.80), kind=kLoop, calls=%fused_computation.149 | loop fusion | bytes 196608 | tf_op jit(solution)/shard_map/slice | solution.py:268
  71.5 1.4 %fusion.51 = (f32[2,3,3,128]{3,2,1,0:T(4,128)}, f32[2,3,3,128]{3,2,1,0:T(4,128)}, f32[2,3,3,128]{3,2,1,0:T(4,128)}, f32[2,3,3,128]{3,2,1,0:T(4,128)}) fusion(f32[2,16,44,128]{3,2,1,0:T(8,128)} %shard_map.80), kind=kLoop, calls=%fused_computation.147 | loop fusion | bytes 73728 | tf_op jit(solution)/shard_map/slice | solution.py:268
  72.9 15.1 %shard_map.81 = (f32[2,3,3,128]{3,2,1,0:T(4,128)}, f32[2,3,44,128]{3,2,1,0:T(8,128)}, f32[2,3,3,128]{3,2,1,0:T(4,128)}, f32[2,16,3,128]{3,2,1,0:T(4,128)}, f32[2...) custom-call(f32[2,3,3,128]{3,2,1,0:T(4,128)} %get-tuple-element.83.refs_0, ...), custom_call_target="tpu_custom_call" | custom-call | tf_op jit(solution)/shard_map/pallas_call | solution.py:283
  88.0 2.0 %maximum_maximum_fusion = (f32[2,19,50,128]{3,2,1,0:T(8,128)S(1)}, f32[2,19,50,128]{3,2,1,0:T(8,128)S(1)}) fusion(f32[2,16,3,128]{3,2,1,0:T(4,128)} %get-tuple-element.36, f32[2,16,44,128]{3,2,1,0:T(8,128)} %shard_map.80, f32[2,16,3,128]{3,2,1,0:T(4,128)} %get-tuple-element.35, f32[2,3,3,128]{3,2,1,0:T(4,128)} %get-tuple-element.34, ...), kind=kLoop, calls=%fused_computation.17 | loop fusion | flops 2432000 | bytes 3072000 | tf_op jit(solution)/shard_map/concatenate | solution.py:297
  91.4 1.0 copy.37
  92.3 1.0 copy.38
  93.3 7.1 %shard_map.82 = (f32[96,44]{1,0:T(8,128)}, f32[96,44]{1,0:T(8,128)}) custom-call(f32[96,44]{1,0:T(8,128)} %bitcast.39, f32[96,44]{1,0:T(8,128)} %bitcast.40), custom_call_target="tpu_custom_call" | custom-call | tf_op jit(solution)/shard_map/pallas_call | solution.py:90
  100.4 1.2 %copy.39 = f32[3,2,16,44]{0,3,2,1:T(8,128)S(1)} copy(f32[3,2,16,44]{3,2,1,0:T(8,128)} %bitcast.42) | data formatting | bytes 33792 | tf_op jit(solution)/shard_map/reshape | solution.py:314
  101.6 1.2 %copy.40 = f32[3,2,16,44]{0,3,2,1:T(8,128)S(1)} copy(f32[3,2,16,44]{3,2,1,0:T(8,128)} %bitcast.41) | data formatting | bytes 33792 | tf_op jit(solution)/shard_map/reshape | solution.py:315
  102.8 2.3 %fusion.11 = f32[2,16,44,128]{3,2,1,0:T(8,128)S(1)} fusion(f32[2,16,44,128]{3,2,1,0:T(8,128)S(1)} %slice_add_fusion.1, f32[2,16,44,3]{3,2,1,0:T(8,128)S(1)} %bitcast.33, f32[2,16,44,3]{3,2,1,0:T(8,128)S(1)} %bitcast.32), kind=kLoop, calls=%fused_computation.33 | loop fusion | flops 3063808 | bytes 1475584 | tf_op jit(solution)/shard_map/add | solution.py:423
  105.5 0.8 copy.42
  106.3 0.8 copy.43
  (39 shorter events, 4.9 us)
Async XLA Ops:
  0.6 15.9 %copy-start.3 = (f32[3,17,45,128]{3,2,1,0:T(8,128)S(1)}, f32[3,17,45,128]{3,2,1,0:T(8,128)}, u32[]{:S(2)}) copy-start(f32[3,17,45,128]{3,2,1,0:T(8,128)} %param.6) | copy-start | bytes 3525124
  17.4 1.6 %copy-start = (f32[3,17,45,129]{3,2,1,0:T(8,128)}, f32[3,17,45,129]{3,2,1,0:T(8,128)S(1)}, u32[]{:S(2)}) copy-start(f32[3,17,45,129]{3,2,1,0:T(8,128)S(1)} %fusion.1) | copy-start | bytes 3552664
  49.3 3.1 %copy-start.2 = (f32[16,44,128]{2,0,1:T(8,128)S(1)}, f32[16,44,128]{2,0,1:T(8,128)}, u32[]{:S(2)}) copy-start(f32[16,44,128]{2,0,1:T(8,128)} %param.10) | copy-start | bytes 1081348
  68.1 22.0 %copy-start.1 = (f32[2,16,44,128]{3,2,1,0:T(8,128)S(1)}, f32[2,16,44,128]{3,2,1,0:T(8,128)}, u32[]{:S(2)}) copy-start(f32[2,16,44,128]{3,2,1,0:T(8,128)} %shard_map.80) | copy-start | bytes 2162692
  88.0 2.0 %copy-start.4 = (f32[2,16,3,128]{3,2,1,0:T(4,128)S(1)}, f32[2,16,3,128]{3,2,1,0:T(4,128)}, u32[]{:S(2)}) copy-start(f32[2,16,3,128]{3,2,1,0:T(4,128)} %get-tuple-element.35) | copy-start | bytes 147460
  88.0 2.0 %copy-start.5 = (f32[2,16,3,128]{3,2,1,0:T(4,128)S(1)}, f32[2,16,3,128]{3,2,1,0:T(4,128)}, u32[]{:S(2)}) copy-start(f32[2,16,3,128]{3,2,1,0:T(4,128)} %get-tuple-element.36) | copy-start | bytes 147460
